TPU v7x, 32 devices: a whole 2x2x4 slice. The times are simulated.
32 devices in a mesh: dp: 8 (over z, x), seq: 4 (over y, core).
Axes of the slice: x: 2, y: 2, z: 4, core: 2. Of those that a mesh axis runs over, the one named last changes fastest.
Arguments:
- latents: bfloat16 [8, 32, 32, 1152], P('dp', 'seq'), may hold values from -6 to 6
- text: bfloat16 [8, 300, 1152], P('dp'), may hold values from -6 to 6
- time_embed: float32 [8, 6912], P('dp'), may hold values from -2 to 2
- cotangent: bfloat16 [8, 32, 32, 1152], P('dp', 'seq'), may hold values from -6 to 6
- params: float32 [4, 5160960], P('seq', 'dp'), may hold values from -1.5 to 1.5, as said below
- moment_one: float32 [4, 5160960], P('seq', 'dp'), may hold values from -2 to 2
- moment_two: float32 [4, 5160960], P('seq', 'dp'), may hold values from 0.05 to 2
Outputs:
- output: bfloat16 [8, 32, 32, 1152], P('dp', 'seq')
- grad_input: float32 [8, 32, 32, 1152], P('dp', 'seq')
- gradient: float32 [4, 5160960], P('seq', 'dp')
- moment_one_new: float32 [4, 5160960], P('seq', 'dp')
- moment_two_new: float32 [4, 5160960], P('seq', 'dp')
- update: float32 [4, 5160960], P('seq', 'dp')
- bias_grads: float32 [4, 3744], P('seq')
Inputs may be any that keep to these rules, and one draw needn't show every extreme that they name: `params`: the grid holds the block's parameters in the layout of the first step.
All inputs are finite; a program needn't handle non-finite values.
Results may differ from a plain program's by a relative error of at most 0.02.
Values may be sent and summed in bfloat16 or wider, within the bound.
A program may use at most 256 MiB of HBM per device.

v0:
```python
import math

import jax
import jax.numpy as jnp
from jax import lax
from jax.sharding import PartitionSpec as P

D = 1152
FF = 2880
CROSS_HEADS = 16


precise = lax.Precision.HIGHEST
eps_norm = 1e-06
eps_linear = 1e-06
beta_first = 0.9
beta_second = 0.95
adam_eps = 1e-08
weight_decay = 0.01
adam_steps = 100.0


def with_halo(block, sides, width):
    for axis, dim in sides:
        count = lax.axis_size(axis)
        forward = [(i, i + 1) for i in range(count - 1)]
        backward = [(target, source) for source, target in forward]
        low = lax.ppermute(
            lax.slice_in_dim(block, block.shape[dim] - width, None, axis=dim), axis, forward
        )
        high = lax.ppermute(lax.slice_in_dim(block, 0, width, axis=dim), axis, backward)
        block = jnp.concatenate([low, block, high], axis=dim)
    return block


def piece_specs():
    return [
        (6, D, False),
        (D, 3 * D, False),
        (D, D, False),
        (1, D, True),
        (D, D, False),
        (D, 2 * D, False),
        (D, D, False),
        (1, D, True),
        (D, 2 * FF, False),
        (1, 2 * FF, True),
        (9, 2 * FF, False),
        (1, 2 * FF, True),
        (FF, D, False),
        (1, D, True),
    ]


def unpack(grid, segs):
    pieces = []
    offset = 0
    for rows_of, cols_of, vector in piece_specs():
        length = rows_of * cols_of // segs
        block = grid[:, offset : offset + length].reshape(segs, rows_of, cols_of // segs)
        block = block.transpose(1, 0, 2).reshape(rows_of, cols_of)
        pieces.append(block.reshape(cols_of) if vector else block)
        offset = offset + length
    return pieces


def gather_weights(shard_low, segs, count_dp, which):
    if which == 0:
        whole = lax.all_gather(shard_low, ("dp", "seq"), axis=0, tiled=True)
    else:
        whole = lax.all_gather(shard_low, ("dp", "seq"), axis=0, tiled=True)
    grid = whole.reshape(count_dp, segs, -1).transpose(1, 0, 2).reshape(segs, -1)
    return unpack(grid, segs)


def norm_parts(values):
    centred = values - jnp.mean(values, axis=-1, keepdims=True)
    inverse = lax.rsqrt(jnp.mean(centred * centred, axis=-1, keepdims=True) + eps_norm)
    return (centred * inverse, inverse)


def norm_back(grad_normed, normed, inverse):
    return inverse * (
        grad_normed
        - jnp.mean(grad_normed, axis=-1, keepdims=True)
        - normed * jnp.mean(grad_normed * normed, axis=-1, keepdims=True)
    )


def silu_slope(values):
    sigmoid_v = jax.nn.sigmoid(values)
    return sigmoid_v * (1.0 + values * (1.0 - sigmoid_v))


def to_low(values):
    return values.astype(jnp.bfloat16)


def matmul(left_op, right_op):
    return jnp.dot(left_op, right_op, preferred_element_type=jnp.float32)


def matmul_t(left_op, right_op):
    return lax.dot_general(
        left_op,
        right_op,
        (((left_op.ndim - 1,), (1,)), ((), ())),
        preferred_element_type=jnp.float32,
    )


def outer_sum(left_op, right_op):
    left_flat = left_op.reshape(-1, left_op.shape[-1])
    right_flat = right_op.reshape(-1, right_op.shape[-1])
    return lax.dot_general(
        left_flat, right_flat, (((0,), (0,)), ((), ())), preferred_element_type=jnp.float32
    )


def depth_conv(padded, kernel, row_dev, col_dev, flipped):
    kernel_f = kernel.astype(jnp.float32)
    summed = jnp.zeros(padded.shape[:1] + (row_dev, col_dev) + padded.shape[3:], jnp.float32)
    for tap_row in range(3):
        for tap_col in range(3):
            row_at = 2 - tap_row if flipped else tap_row
            col_at = 2 - tap_col if flipped else tap_col
            summed = (
                summed
                + kernel_f[tap_row * 3 + tap_col]
                * padded[:, row_at : row_at + row_dev, col_at : col_at + col_dev, :]
            )
    return summed


def shards(latents, text, time_embed, cotangent, params, moment_one, moment_two):
    lat_dev, row_dev, col_dev, width = latents.shape
    tokens_dev = row_dev * col_dev
    heads_lin = D // 32
    cross_dim = D // CROSS_HEADS
    score_scale = 1.0 / math.sqrt(cross_dim)
    text_len = text.shape[1]
    segs = lax.axis_size("seq")
    count_dp = lax.axis_size("dp")
    shard_low = params.astype(jnp.bfloat16)
    (
        mod_table,
        w_qkv,
        w_attn_out,
        b_attn_out,
        w_cross_q,
        w_cross_kv,
        w_cross_out,
        b_cross_out,
        w_in,
        b_in,
        w_depth,
        b_depth,
        w_point,
        b_point,
    ) = gather_weights(shard_low, segs, count_dp, 0)
    modulation = mod_table.astype(jnp.float32)[None] + time_embed.reshape(lat_dev, 6, D)
    shift_one = modulation[:, 0][:, None, :]
    scale_one = modulation[:, 1][:, None, :]
    gate_one = modulation[:, 2][:, None, :]
    shift_two = modulation[:, 3][:, None, :]
    scale_two = modulation[:, 4][:, None, :]
    gate_two = modulation[:, 5][:, None, :]
    tokens = latents.reshape(lat_dev, tokens_dev, D).astype(jnp.float32)
    normed_one, inverse_one = norm_parts(tokens)
    hidden_one = to_low(normed_one * (1.0 + scale_one) + shift_one)
    projected = matmul(hidden_one, w_qkv)
    query_pre = projected[..., :D]
    key_pre = projected[..., D : 2 * D]
    queries = to_low(jnp.maximum(query_pre, 0.0)).reshape(lat_dev, tokens_dev, heads_lin, 32)
    keys_lin = to_low(jnp.maximum(key_pre, 0.0)).reshape(lat_dev, tokens_dev, heads_lin, 32)
    values_lin = to_low(projected[..., 2 * D :]).reshape(lat_dev, tokens_dev, heads_lin, 32)
    state_part = jnp.einsum(
        "lrhd,lrhe->lhde", keys_lin, values_lin, preferred_element_type=jnp.float32
    )
    sum_part = jnp.sum(keys_lin, axis=1, dtype=jnp.float32)
    kv_state, key_sum = lax.psum((state_part, sum_part), "seq")
    query_f = queries.astype(jnp.float32)
    numerator = jnp.einsum("lrhd,lhde->lrhe", query_f, kv_state, precision=precise)
    denominator = jnp.einsum("lrhd,lhd->lrh", query_f, key_sum, precision=precise) + eps_linear
    attn_val = numerator / denominator[..., None]
    attended = to_low(attn_val.reshape(lat_dev, tokens_dev, D))
    branch_one = matmul(attended, w_attn_out) + b_attn_out.astype(jnp.float32)
    after_attn = tokens + gate_one * branch_one
    after_low = to_low(after_attn)
    query_c = to_low(matmul(after_low, w_cross_q)).reshape(
        lat_dev, tokens_dev, CROSS_HEADS, cross_dim
    )
    keyval = to_low(matmul(text, w_cross_kv))
    keys_c = keyval[..., :D].reshape(lat_dev, text_len, CROSS_HEADS, cross_dim)
    values_c = keyval[..., D:].reshape(lat_dev, text_len, CROSS_HEADS, cross_dim)
    scores = (
        jnp.einsum("lrhc,lthc->lhrt", query_c, keys_c, preferred_element_type=jnp.float32)
        * score_scale
    )
    row_peak = jnp.max(scores, axis=-1, keepdims=True)
    log_total = row_peak + jnp.log(jnp.sum(jnp.exp(scores - row_peak), axis=-1, keepdims=True))
    probs_low = to_low(jnp.exp(scores - log_total))
    cross_mixed = to_low(
        jnp.einsum(
            "lhrt,lthc->lrhc", probs_low, values_c, preferred_element_type=jnp.float32
        ).reshape(lat_dev, tokens_dev, D)
    )
    after_cross = after_attn + matmul(cross_mixed, w_cross_out) + b_cross_out.astype(jnp.float32)
    normed_two, inverse_two = norm_parts(after_cross)
    hidden_two = to_low(normed_two * (1.0 + scale_two) + shift_two)
    inner_pre = matmul(hidden_two, w_in) + b_in.astype(jnp.float32)
    active = to_low(jax.nn.silu(inner_pre)).reshape(lat_dev, row_dev, col_dev, 2 * FF)
    padded = jnp.pad(with_halo(active, (("seq", 1),), 1), ((0, 0), (0, 0), (1, 1), (0, 0)))
    conv_out = (
        depth_conv(padded, w_depth, row_dev, col_dev, False) + b_depth.astype(jnp.float32)
    ).reshape(lat_dev, tokens_dev, 2 * FF)
    up_part = conv_out[..., :FF]
    gate_part = conv_out[..., FF:]
    gated_mix = to_low(up_part * jax.nn.silu(gate_part))
    branch_two = matmul(gated_mix, w_point) + b_point.astype(jnp.float32)
    output = (after_cross + gate_two * branch_two).astype(jnp.bfloat16).reshape(latents.shape)
    (
        mod_table,
        w_qkv,
        w_attn_out,
        b_attn_out,
        w_cross_q,
        w_cross_kv,
        w_cross_out,
        b_cross_out,
        w_in,
        b_in,
        w_depth,
        b_depth,
        w_point,
        b_point,
    ) = gather_weights(shard_low, segs, count_dp, 1)
    grad_out = cotangent.reshape(lat_dev, tokens_dev, D).astype(jnp.float32)
    grad_gate_two = jnp.sum(grad_out * branch_two, axis=1)
    grad_branch_two = to_low(grad_out * gate_two)
    grad_gated = matmul_t(grad_branch_two, w_point)
    grad_up = grad_gated * jax.nn.silu(gate_part)
    grad_gate = grad_gated * up_part * silu_slope(gate_part)
    grad_conv = to_low(jnp.concatenate([grad_up, grad_gate], axis=-1)).reshape(
        lat_dev, row_dev, col_dev, 2 * FF
    )
    grad_b_depth = jnp.sum(grad_conv, axis=(0, 1, 2), dtype=jnp.float32)
    tap_grads = []
    for tap_row in range(3):
        for tap_col in range(3):
            tap_grads.append(
                jnp.einsum(
                    "lrcf,lrcf->f",
                    padded[:, tap_row : tap_row + row_dev, tap_col : tap_col + col_dev],
                    grad_conv,
                    preferred_element_type=jnp.float32,
                )
            )
    grad_w_depth = jnp.stack(tap_grads)
    grad_padded = jnp.pad(with_halo(grad_conv, (("seq", 1),), 1), ((0, 0), (0, 0), (1, 1), (0, 0)))
    grad_active = depth_conv(grad_padded, w_depth, row_dev, col_dev, True).reshape(
        lat_dev, tokens_dev, 2 * FF
    )
    grad_inner = to_low(grad_active * silu_slope(inner_pre))
    grad_hidden_two = matmul_t(grad_inner, w_in)
    grad_shift_two = jnp.sum(grad_hidden_two, axis=1)
    grad_scale_two = jnp.sum(grad_hidden_two * normed_two, axis=1)
    grad_second = grad_out + norm_back(grad_hidden_two * (1.0 + scale_two), normed_two, inverse_two)
    grad_cross_out = to_low(grad_second)
    grad_mixed = to_low(matmul_t(grad_cross_out, w_cross_out)).reshape(
        lat_dev, tokens_dev, CROSS_HEADS, cross_dim
    )
    scores_again = (
        jnp.einsum("lrhc,lthc->lhrt", query_c, keys_c, preferred_element_type=jnp.float32)
        * score_scale
    )
    probs = jnp.exp(scores_again - log_total)
    grad_probs = jnp.einsum(
        "lrhc,lthc->lhrt", grad_mixed, values_c, preferred_element_type=jnp.float32
    )
    grad_values_c = jnp.einsum(
        "lhrt,lrhc->lthc", to_low(probs), grad_mixed, preferred_element_type=jnp.float32
    )
    grad_scores = to_low(probs * (grad_probs - jnp.sum(probs * grad_probs, axis=-1, keepdims=True)))
    grad_query_c = to_low(
        jnp.einsum("lhrt,lthc->lrhc", grad_scores, keys_c, preferred_element_type=jnp.float32)
        * score_scale
    ).reshape(lat_dev, tokens_dev, D)
    grad_keys_c = (
        jnp.einsum("lhrt,lrhc->lthc", grad_scores, query_c, preferred_element_type=jnp.float32)
        * score_scale
    )
    grad_keyval_part = jnp.concatenate(
        [grad_keys_c.reshape(lat_dev, text_len, D), grad_values_c.reshape(lat_dev, text_len, D)],
        axis=-1,
    )
    grad_keyval_part = grad_keyval_part.reshape(lat_dev, text_len, segs, 2 * D // segs)
    grad_keyval = to_low(
        lax.psum_scatter(
            grad_keyval_part.astype(jnp.bfloat16), "seq", scatter_dimension=2, tiled=True
        ).astype(jnp.float32)
    ).reshape(lat_dev, text_len, 2 * D // segs)
    grad_w_cross_kv = outer_sum(text, grad_keyval)
    grad_first = grad_second + matmul_t(grad_query_c, w_cross_q)
    grad_gate_one = jnp.sum(grad_first * branch_one, axis=1)
    grad_branch_one = to_low(grad_first * gate_one)
    grad_attended = matmul_t(grad_branch_one, w_attn_out).reshape(
        lat_dev, tokens_dev, heads_lin, 32
    )
    grad_numer = grad_attended / denominator[..., None]
    grad_denom = -jnp.sum(grad_attended * attn_val, axis=-1) / denominator
    grad_query = (
        jnp.einsum("lrhe,lhde->lrhd", grad_numer, kv_state, precision=precise)
        + grad_denom[..., None] * key_sum[:, None]
    )
    state_grad_part = jnp.einsum("lrhd,lrhe->lhde", query_f, grad_numer, precision=precise)
    sum_grad_part = jnp.einsum("lrhd,lrh->lhd", query_f, grad_denom, precision=precise)
    state_grad, sum_grad = (
        lax.psum(state_grad_part.astype(jnp.bfloat16), "seq").astype(jnp.float32),
        lax.psum(sum_grad_part.astype(jnp.bfloat16), "seq").astype(jnp.float32),
    )
    keys_f = keys_lin.astype(jnp.float32)
    values_f = values_lin.astype(jnp.float32)
    grad_keys = (
        jnp.einsum("lrhe,lhde->lrhd", values_f, state_grad, precision=precise) + sum_grad[:, None]
    )
    grad_values = jnp.einsum("lrhd,lhde->lrhe", keys_f, state_grad, precision=precise)
    grad_projected = to_low(
        jnp.concatenate(
            [
                grad_query.reshape(lat_dev, tokens_dev, D) * (query_pre > 0.0),
                grad_keys.reshape(lat_dev, tokens_dev, D) * (key_pre > 0.0),
                grad_values.reshape(lat_dev, tokens_dev, D),
            ],
            axis=-1,
        )
    )
    grad_hidden_one = matmul_t(grad_projected, w_qkv)
    grad_input = grad_first + norm_back(
        grad_hidden_one * (1.0 + scale_one), normed_one, inverse_one
    )
    grad_table = jnp.sum(
        jnp.stack(
            [
                jnp.sum(grad_hidden_one, axis=1),
                jnp.sum(grad_hidden_one * normed_one, axis=1),
                grad_gate_one,
                grad_shift_two,
                grad_scale_two,
                grad_gate_two,
            ],
            axis=1,
        ),
        axis=0,
    )
    table_q, depth_q, depth_bias_q = (
        lax.psum_scatter(
            grad_table.reshape(6, segs, D // segs).astype(jnp.bfloat16),
            "seq",
            scatter_dimension=1,
            tiled=True,
        ).astype(jnp.float32),
        lax.psum_scatter(
            grad_w_depth.reshape(9, segs, 2 * FF // segs).astype(jnp.bfloat16),
            "seq",
            scatter_dimension=1,
            tiled=True,
        ).astype(jnp.float32),
        lax.psum_scatter(
            grad_b_depth.reshape(1, segs, 2 * FF // segs).astype(jnp.bfloat16),
            "seq",
            scatter_dimension=1,
            tiled=True,
        ).astype(jnp.float32),
    )
    inputs_cat = jnp.concatenate(
        [hidden_one, attended, after_low, cross_mixed, hidden_two, gated_mix], axis=-1
    )
    inputs_all = lax.all_gather(inputs_cat, "seq", axis=1, tiled=True)

    def quarters(values):
        return values.reshape(lat_dev, tokens_dev, segs, values.shape[-1] // segs)

    outputs_cat = jnp.concatenate(
        [
            quarters(grad_projected),
            quarters(grad_branch_one),
            quarters(grad_query_c),
            quarters(grad_cross_out),
            quarters(grad_inner),
            quarters(grad_branch_two),
        ],
        axis=-1,
    )
    outputs_mine = lax.all_to_all(outputs_cat, "seq", split_axis=2, concat_axis=1, tiled=True)
    outputs_mine = outputs_mine.reshape(lat_dev, outputs_mine.shape[1], outputs_mine.shape[3])
    col_d = D // segs
    col_ff = 2 * FF // segs
    y_qkv = outputs_mine[..., 0 : 3 * col_d]
    y_attn = outputs_mine[..., 3 * col_d : 4 * col_d]
    y_cross_q = outputs_mine[..., 4 * col_d : 5 * col_d]
    y_cross_out = outputs_mine[..., 5 * col_d : 6 * col_d]
    y_inner = outputs_mine[..., 6 * col_d : 6 * col_d + col_ff]
    y_point = outputs_mine[..., 6 * col_d + col_ff : 7 * col_d + col_ff]
    grad_w_qkv = outer_sum(inputs_all[..., 0:D], y_qkv)
    grad_w_attn_out = outer_sum(inputs_all[..., D : 2 * D], y_attn)
    grad_w_cross_q = outer_sum(inputs_all[..., 2 * D : 3 * D], y_cross_q)
    grad_w_cross_out = outer_sum(inputs_all[..., 3 * D : 4 * D], y_cross_out)
    grad_w_in = outer_sum(inputs_all[..., 4 * D : 5 * D], y_inner)
    grad_w_point = outer_sum(inputs_all[..., 5 * D : 5 * D + FF], y_point)
    grad_b_attn_out = jnp.sum(y_attn, axis=(0, 1), dtype=jnp.float32)
    grad_b_cross_out = jnp.sum(y_cross_out, axis=(0, 1), dtype=jnp.float32)
    grad_b_in = jnp.sum(y_inner, axis=(0, 1), dtype=jnp.float32)
    grad_b_point = jnp.sum(y_point, axis=(0, 1), dtype=jnp.float32)
    bias_part = jnp.concatenate(
        [grad_b_attn_out, grad_b_cross_out, grad_b_in, depth_bias_q.ravel(), grad_b_point]
    )
    bias_total = lax.psum(bias_part, "dp")
    quarter_grad = jnp.concatenate(
        [
            table_q.ravel(),
            grad_w_qkv.ravel(),
            grad_w_attn_out.ravel(),
            grad_b_attn_out,
            grad_w_cross_q.ravel(),
            grad_w_cross_kv.ravel(),
            grad_w_cross_out.ravel(),
            grad_b_cross_out,
            grad_w_in.ravel(),
            grad_b_in,
            depth_q.ravel(),
            depth_bias_q.ravel(),
            grad_w_point.ravel(),
            grad_b_point,
        ]
    )
    grad_shard = lax.psum_scatter(
        quarter_grad.reshape(1, -1).astype(jnp.bfloat16), "dp", scatter_dimension=1, tiled=True
    ).astype(jnp.float32)
    square_total = lax.psum(jnp.sum(grad_shard * grad_shard), ("dp", "seq"))
    entries_all = grad_shard.size * lax.axis_size(("dp", "seq"))
    factor = lax.rsqrt(square_total / entries_all + 1e-06)
    gradient = grad_shard * factor
    bias_grads = (bias_total * factor).reshape(1, -1)
    moment_one_new = beta_first * moment_one + (1.0 - beta_first) * gradient
    moment_two_new = beta_second * moment_two + (1.0 - beta_second) * gradient * gradient
    first_hat = moment_one_new / (1.0 - beta_first**adam_steps)
    second_hat = moment_two_new / (1.0 - beta_second**adam_steps)
    update = first_hat / (jnp.sqrt(second_hat) + adam_eps) + weight_decay * params
    return (
        output,
        grad_input.reshape(latents.shape),
        gradient,
        moment_one_new,
        moment_two_new,
        update,
        bias_grads,
    )


def solution(mesh):
    return jax.shard_map(
        shards,
        mesh=mesh,
        in_specs=(
            P("dp", "seq", None, None),
            P("dp", None, None),
            P("dp", None),
            P("dp", "seq", None, None),
            P("seq", "dp"),
            P("seq", "dp"),
            P("seq", "dp"),
        ),
        out_specs=(
            P("dp", "seq", None, None),
            P("dp", "seq", None, None),
            P("seq", "dp"),
            P("seq", "dp"),
            P("seq", "dp"),
            P("seq", "dp"),
            P("seq", None),
        ),
        check_vma=False,
    )
```

profile of v0, /device:TPU:0, one launch (start us, length us, event | category | flops | bytes accessed | tf_op | source)
XLA Modules:
  0.0 2649.9 jit_solution(6872667459148645289)
XLA Ops:
  13.7 431.7 %all-gather.6.cloned.1.call-done = bf16[32,1,645120]{2,1,0:T(2,128)(2,1)} async-done(((bf16[1,1,645120]{2,1,0:T(2,128)(2,1)}), bf16[32,1,645120]{2,1,0:T(2,128)(2,1)}) %all-gather.6.cloned.1.call-update) | async-done | bytes 41287696 | tf_op jit(solution)/shard_map/all_gather | solution.py:69
  445.5 244.6 %reduce.46 = bf16[32,645120]{1,0:T(8,128)(2,1)} reduce(bf16[32,1,645120]{2,1,0:T(2,128)(2,1)} %all-gather.6.cloned.1.call-done, bf16[]{:T(256)} %constant.91), dimensions={1}, to_apply=%all-gather.reduce_sub_computation | reduce | bytes 82575360 | tf_op jit(solution)/shard_map/all_gather | solution.py:69
  690.1 79.0 %reshape.1486 = bf16[8,4,645120]{2,1,0:T(4,128)(2,1)} reshape(bf16[32,645120]{1,0:T(8,128)(2,1)} %reduce.46) | data formatting | bytes 82575360 | tf_op jit(solution)/shard_map/reshape | solution.py:72
  779.1 14.3 reshape.1633
  793.4 16.9 reshape.1489
  810.4 11.9 copy.135
  853.0 11.4 psum.43
  878.3 10.9 reshape.1499
  903.9 10.3 slice.340
  980.6 35.5 %reshape.1645 = bf16[6635520]{0:T(1024)(128)(2,1)} reshape(bf16[4,1658880]{1,0:T(4,128)(2,1)} %slice.340) | data formatting | bytes 26542080
  1016.0 27.3 %reshape.1508 = bf16[4,1152,1440]{2,1,0:T(8,128)(2,1)} reshape(bf16[6635520]{0:T(1024)(128)(2,1)} %reshape.1645) | data formatting | bytes 26542080 | tf_op jit(solution)/shard_map/reshape | solution.py:60
  1043.3 17.4 copy.147
  1074.5 16.6 reshape.1513
  1091.1 11.4 copy.150
  1120.7 11.6 multiply_convert_fusion
  1185.7 18.0 fusion.8
  1274.9 12.4 all-reduce.5
  1360.5 24.4 reduce-scatter.8.cloned.1.call-done
  1394.4 90.9 %all-to-all-done = bf16[1,256,4,3456]{1,3,0,2:T(8,128)(2,1)} async-done(((bf16[1,256,4,3456]{1,3,0,2:T(8,128)(2,1)}), bf16[1,256,4,3456]{1,3,0,2:T(8,128)(2,1)}, u32[]{:S(2)}, u32[]{:S(2)}) %all-to-all-start) | async-done | bytes 7077920 | tf_op jit(solution)/shard_map/all_to_all | solution.py:395
  1501.7 41.5 %all-gather.4.cloned.1.call-done = bf16[1,1024,8640]{1,2,0:T(8,128)(2,1)} async-done(((bf16[1,256,8640]{1,2,0:T(8,128)(2,1)}), bf16[1,1024,8640]{1,2,0:T(8,128)(2,1)}) %all-gather.4.cloned.1.call-update) | async-done | bytes 17694736 | tf_op jit(solution)/shard_map/all_gather | solution.py:379
  1558.9 17.5 concatenate.179
  1646.1 20.4 concatenate.162
  1666.5 68.5 %dynamic-update-slice.1 = bf16[1,5160960]{1,0:T(2,128)(2,1)} dynamic-update-slice(bf16[1,5160960]{1,0:T(2,128)(2,1)} %dynamic-update-slice, bf16[1,995328]{1,0:T(2,128)(2,1)} %concatenate.162, s32[]{} %constant.110, s32[]{} %constant.111) | dynamic-update-slice | bytes 3981316
  1735.0 23.7 dynamic-update-slice.2
  1760.2 23.7 dynamic-update-slice.4
  1783.9 45.8 %dynamic-update-slice.5 = bf16[1,5160960]{1,0:T(2,128)(2,1)} dynamic-update-slice(bf16[1,5160960]{1,0:T(2,128)(2,1)} %dynamic-update-slice.4, bf16[1,663552]{1,0:T(2,128)(2,1)S(1)} %concatenate.169, s32[]{} %constant.110, s32[]{} %constant.115) | dynamic-update-slice | bytes 2654212
  1829.8 23.7 dynamic-update-slice.6
  1865.4 57.4 %dynamic-update-slice.12 = bf16[1,5160960]{1,0:T(2,128)(2,1)} dynamic-update-slice(bf16[1,5160960]{1,0:T(2,128)(2,1)} %dynamic-update-slice.11, bf16[1,829440]{1,0:T(2,128)(2,1)} %concatenate.179, s32[]{} %constant.110, s32[]{} %constant.122) | dynamic-update-slice | bytes 3317764
  1927.0 611.7 %all-reduce.14.cloned.1.call-done = bf16[1,5160960]{1,0:T(2,128)(2,1)} async-done(((bf16[1,5160960]{1,0:T(2,128)(2,1)}), bf16[1,5160960]{1,0:T(2,128)(2,1)}) %all-reduce.14.cloned.1.call-update) | async-done | bytes 10321936
  2545.7 35.1 %psum.47 = f32[3744]{0:T(1024)S(1)} all-reduce(f32[3744]{0:T(1024)S(1)} %concatenate.182), channel_id=1, replica_groups=mesh['dp'=8,'seq'=4] {'dp'}, use_global_device_ids=true, to_apply=%region_35.36 | all-reduce | flops 3744 | bytes 29952 | tf_op jit(solution)/shard_map/psum | solution.py:418
  2580.8 37.2 %psum.46 = f32[]{:T(128)} all-reduce(f32[]{:T(128)} %multiply_reduce_fusion.2), channel_id=1, replica_groups=mesh['dp'=8,'seq'=4] {'dp','seq'}, use_global_device_ids=true, to_apply=%region_34.35 | all-reduce | flops 1 | bytes 8 | tf_op jit(solution)/shard_map/psum | solution.py:440
  2619.3 23.4 multiply_add_fusion.1
  (496 shorter events, 506.1 us)
Async XLA Ops:
  7.2 890.4 %copy-start = (bf16[1,300,1152]{2,1,0:T(8,128)(2,1)S(1)}, bf16[1,300,1152]{2,1,0:T(8,128)(2,1)}, u32[]{:S(2)}) copy-start(bf16[1,300,1152]{2,1,0:T(8,128)(2,1)} %param.8) | copy-start | bytes 2073604
  7.2 438.3 %all-gather.6.cloned.1.call-start = ((), (), s32[]{:S(2)}) async-start(), calls=%async_computation.9 | async-start | bytes 85155840 | tf_op jit(solution)/shard_map/all_gather | solution.py:69
  12.8 1090.4 %all-reduce.10.cloned.1.call-start = ((), (), s32[]{:S(2)}) async-start(), calls=%async_computation.4 | async-start | bytes 1179648 | tf_op jit(solution)/shard_map/psum | solution.py:181
  13.2 837.2 %copy-start.98 = (f32[256]{0:T(256)}, f32[256]{0:T(256)S(1)}, u32[]{:S(2)}) copy-start(f32[256]{0:T(256)S(1)} %div.82) | copy-start | bytes 3076
  13.7 836.8 %copy-start.100 = (f32[256]{0:T(256)}, f32[256]{0:T(256)S(1)}, u32[]{:S(2)}) copy-start(f32[256]{0:T(256)S(1)} %add_rsqrt_fusion.1) | copy-start | bytes 3076
  779.1 43.2 %copy-start.83 = (f32[1152]{0:T(1024)}, f32[1152]{0:T(1024)S(1)}, u32[]{:S(2)}) copy-start(f32[1152]{0:T(1024)S(1)} %get-tuple-element.36) | copy-start | bytes 13828
  779.1 71.4 %copy-start.76 = (f32[1152]{0:T(1024)}, f32[1152]{0:T(1024)S(1)}, u32[]{:S(2)}) copy-start(f32[1152]{0:T(1024)S(1)} %get-tuple-element.40) | copy-start | bytes 13828
  779.1 329.1 %copy-start.81 = (f32[1152]{0:T(1024)}, f32[1152]{0:T(1024)S(1)}, u32[]{:S(2)}) copy-start(f32[1152]{0:T(1024)S(1)} %get-tuple-element.41) | copy-start | bytes 13828
  810.4 11.9 copy-start.29
  853.0 13.8 copy-start.55
  865.4 237.8 %copy-start.88 = (f32[256,36]{0,1:T(8,128)}, f32[256,36]{0,1:T(8,128)S(1)}, u32[]{:S(2)}) copy-start(f32[256,36]{0,1:T(8,128)S(1)} %fusion.66) | copy-start | bytes 110596
  868.2 436.0 %all-reduce.12.cloned.1.call-start = ((), (), s32[]{:S(2)}) async-start(), calls=%async_computation.5 | async-start | bytes 589824 | tf_op jit(solution)/shard_map/psum | solution.py:319
  959.1 155.1 %copy-start.18 = (bf16[1,300,1152]{1,2,0:T(8,128)(2,1)}, bf16[1,300,1152]{1,2,0:T(8,128)(2,1)S(1)}, u32[]{:S(2)}) copy-start(bf16[1,300,1152]{1,2,0:T(8,128)(2,1)S(1)} %copy.145) | copy-start | bytes 2073604
  961.2 154.8 %copy-start.20 = (bf16[1,300,1152]{1,2,0:T(8,128)(2,1)}, bf16[1,300,1152]{1,2,0:T(8,128)(2,1)S(1)}, u32[]{:S(2)}) copy-start(bf16[1,300,1152]{1,2,0:T(8,128)(2,1)S(1)} %copy.142) | copy-start | bytes 2073604
  1120.3 128.4 %copy-start.15 = (f32[256,1152]{1,0:T(8,128)}, f32[256,1152]{1,0:T(8,128)S(1)}, u32[]{:S(2)}) copy-start(f32[256,1152]{1,0:T(8,128)S(1)} %get-tuple-element.98) | copy-start | bytes 3538948
  1134.7 9.7 collective-permute-start
  1136.2 8.3 collective-permute-start.1
  1179.7 49.4 %collective-permute-start.2 = (bf16[1,1,32,5760]{3,2,1,0:T(8,128)(2,1)}, bf16[1,1,32,5760]{3,2,1,0:T(8,128)(2,1)}, u32[]{:S(2)}, u32[]{:S(2)}) collective-permute-start(bf16[1,1,32,5760]{3,2,1,0:T(8,128)(2,1)} %get-tuple-element.80), channel_id=1, source_target_pairs={{0,1},{1,2},{2,3},{4,5},{5,6},{6,7},{8,9},{9,10},{10,11},{12,13},{... | collective-permute-start | bytes 1105928 | tf_op jit(solution)/shard_map/ppermute | solution.py:28
  1184.3 44.8 %collective-permute-start.3 = (bf16[1,1,32,5760]{3,2,1,0:T(8,128)(2,1)}, bf16[1,1,32,5760]{3,2,1,0:T(8,128)(2,1)}, u32[]{:S(2)}, u32[]{:S(2)}) collective-permute-start(bf16[1,1,32,5760]{3,2,1,0:T(8,128)(2,1)} %get-tuple-element.81), channel_id=1, source_target_pairs={{1,0},{2,1},{3,2},{5,4},{6,5},{7,6},{9,8},{10,9},{11,10},{13,12},{... | collective-permute-start | bytes 1105928 | tf_op jit(solution)/shard_map/ppermute | solution.py:31
  1232.2 11.9 slice-start.2
  1232.2 11.9 slice-start.3
  1232.2 11.9 slice-start.4
  1266.2 89.9 %reduce-scatter.10.cloned.1.call-start = ((), (), s32[]{:S(2)}) async-start(), calls=%async_computation.8 | async-start | bytes 245760 | tf_op jit(solution)/shard_map/reduce_scatter | solution.py:363
  1267.1 91.2 %reduce-scatter.12.cloned.1.call-start = ((), (), s32[]{:S(2)}) async-start(), calls=%async_computation.11 | async-start | bytes 30720
  1272.2 15.2 copy-start.80
  1274.0 13.4 copy-start.63
  1287.3 69.7 %copy-start.102 = (bf16[1,4,1440]{2,1,0:T(4,128)(2,1)}, bf16[1,4,1440]{2,1,0:T(4,128)(2,1)S(1)}, u32[]{:S(2)}) copy-start(bf16[1,4,1440]{2,1,0:T(4,128)(2,1)S(1)} %get-tuple-element.43) | copy-start | bytes 34564
  1323.7 61.2 %reduce-scatter.8.cloned.1.call-start = ((), (), s32[]{:S(2)}) async-start(), calls=%async_computation.7 | async-start | bytes 2211840 | tf_op jit(solution)/shard_map/reduce_scatter | solution.py:299
  1326.4 216.7 %all-gather.4.cloned.1.call-start = ((), (), s32[]{:S(2)}) async-start(), calls=%async_computation.6 | async-start | bytes 22118400 | tf_op jit(solution)/shard_map/all_gather | solution.py:379
  1349.7 135.6 %all-to-all-start = ((bf16[1,256,4,3456]{1,3,0,2:T(8,128)(2,1)}), bf16[1,256,4,3456]{1,3,0,2:T(8,128)(2,1)}, u32[]{:S(2)}, u32[]{:S(2)}) async-start(bf16[1,256,4,3456]{1,3,0,2:T(8,128)(2,1)} %bitcast.405), calls=%async_computation | async-start | bytes 14155776 | tf_op jit(solution)/shard_map/all_to_all | solution.py:395
  1355.3 1183.4 %all-reduce.14.cloned.1.call-start = ((), (), s32[]{:S(2)}) async-start(), calls=%async_computation.10 | async-start | bytes 41287680
  1924.8 694.6 %copy-start.17 = (f32[1,645120]{1,0:T(1,128)S(1)}, f32[1,645120]{1,0:T(1,128)}, u32[]{:S(2)}) copy-start(f32[1,645120]{1,0:T(1,128)} %param.11) | copy-start | bytes 7741444
  (97 other events, 356.2 us)
Sparse Core Ops, SparseCore 0:
  12.9 432.4 all-gather.5
  868.3 31.8 all-reduce.9
  1266.3 33.1 all-reduce.11
  1301.8 19.7 reduce-scatter.9
  1323.8 19.0 reduce-scatter.11
  1346.0 38.8 reduce-scatter.7
  1386.4 156.6 all-gather.3
  1924.3 614.4 all-reduce.13
where the time goes:
time: 2690 us; the launch traced here: 2650 us
  waiting for transfers between devices  1200 us (45%)
  local copies, waits for them, and re-layouts  839 us (31%)
  other arithmetic  364 us (14%)
  matrix products  118 us (4%)
  blocking collectives  96.1 us (4%)
    unnamed x10, waiting for transfers between devices  612 us
    all_gather x1, waiting for transfers between devices, gather_weights(): whole = lax.all_gather(shard_low, ('dp', 'seq'), axis=0, tiled=True)  432 us
    unnamed x282, local copies, waits for them, and re-layouts  411 us
    all_gather x1, other arithmetic, gather_weights(): whole = lax.all_gather(shard_low, ('dp', 'seq'), axis=0, tiled=True)  245 us
    reshape x7, local copies, waits for them, and re-layouts, unpack(): grid[:, offset:offset + length].reshape(segs, rows_of, cols_of // segs)  94.3 us
    all_to_all x1, waiting for transfers between devices, shards(): lax.all_to_all(outputs_cat, 'seq', split_axis=2, concat_axis=1, tiled=True)  90.9 us
    reshape x1, local copies, waits for them, and re-layouts, gather_weights(): whole.reshape(count_dp, segs, -1).transpose(1, 0, 2).reshape(segs, -1)  79 us
    transpose x7, local copies, waits for them, and re-layouts, unpack(): block = block.transpose(1, 0, 2).reshape(rows_of, cols_of)  63.5 us
  transfers between devices with their start and end apart: 13, of which 5 were waited for; matrix products, arithmetic and copies ran while one was open for 14% of the time, Pallas kernels for 0%

commit v1 on v0

--- a/solution.py
+++ b/solution.py
@@ -3,6 +3,8 @@
 import jax
 import jax.numpy as jnp
 from jax import lax
+from jax.experimental import pallas as pl
+from jax.experimental.pallas import tpu as pltpu
 from jax.sharding import PartitionSpec as P
 
 D = 1152
@@ -52,25 +54,319 @@
     ]
 
 
-def unpack(grid, segs):
+LANE = 128
+UNIT = 32
+
+
+def merge_units(values, lane_unit):
+    out = values[0]
+    last = values[0]
+    for position in range(1, 4):
+        if values[position] is not last:
+            out = jnp.where(lane_unit >= position, values[position], out)
+            last = values[position]
+    return out
+
+
+def rolled(value, units):
+    units = units % 4
+    return value if units == 0 else pltpu.roll(value, units * UNIT, 1)
+
+
+def matrix_rows(count_rows):
+    return 192 if count_rows % 192 == 0 else 64
+
+
+def read_matrix(flat, offset, rows_of, cols_of, segs):
+    total_rows = flat.shape[1]
+    per_row = cols_of // segs // UNIT
+    unit_at = offset // UNIT
+    block = matrix_rows(rows_of)
+    base = unit_at // 4 // 16 * 16
+    shift = unit_at - 4 * base
+    step = block * per_row // 4
+    need = (shift + block * per_row - 1) // 4 + 1
+    need = -(-need // 16) * 16
+    assert base + (rows_of // block - 1) * step + need <= total_rows
+    tiles = cols_of // LANE
+
+    def kernel(in_ref, out_ref, wide, mixed):
+        def widen(at, _):
+            row = pl.multiple_of(at * 16, 16)
+            for seg in range(segs):
+                wide[pl.ds(pl.multiple_of(seg * need + row, 16), 16), :] = in_ref[
+                    seg, pl.ds(row, 16), :
+                ].astype(jnp.float32)
+            return 0
+
+        lax.fori_loop(0, need // 16, widen, 0)
+        lane_unit = lax.broadcasted_iota(jnp.int32, (8, LANE), 1) // UNIT
+
+        def group(at, _):
+            for phase in range(4):
+                loaded = {}
+                turned = {}
+                for tile in range(tiles):
+                    parts = []
+                    for slot in range(4):
+                        col = 4 * tile + slot
+                        seg, unit = col // per_row, col % per_row
+                        source = shift + phase * per_row + unit
+                        key = (seg, source // 4)
+                        if key not in loaded:
+                            loaded[key] = wide[
+                                pl.ds(seg * need + key[1] + at * (8 * per_row), 8, stride=per_row),
+                                :,
+                            ]
+                        turn = (slot - source) % 4
+                        if (key, turn) not in turned:
+                            turned[key, turn] = rolled(loaded[key], turn)
+                        parts.append(turned[key, turn])
+                    mixed[pl.ds(tile * block + phase + at * 32, 8, stride=4), :] = merge_units(
+                        parts, lane_unit
+                    )
+            return 0
+
+        lax.fori_loop(0, block // 32, group, 0)
+
+        def narrow(at, _):
+            row = pl.multiple_of(at * 16, 16)
+            for tile in range(tiles):
+                out_ref[pl.ds(row, 16), tile * LANE : (tile + 1) * LANE] = mixed[
+                    pl.ds(pl.multiple_of(tile * block + row, 16), 16), :
+                ].astype(jnp.bfloat16)
+            return 0
+
+        lax.fori_loop(0, block // 16, narrow, 0)
+
+    return pl.pallas_call(
+        kernel,
+        grid=(rows_of // block,),
+        in_specs=[
+            pl.BlockSpec(
+                (pl.Element(segs), pl.Element(need), pl.Element(LANE)),
+                lambda at: (0, pl.multiple_of(base + at * step, 16), 0),
+            )
+        ],
+        out_specs=pl.BlockSpec((block, cols_of), lambda at: (at, 0)),
+        out_shape=jax.ShapeDtypeStruct((rows_of, cols_of), jnp.bfloat16),
+        scratch_shapes=[
+            pltpu.VMEM((segs * need, LANE), jnp.float32),
+            pltpu.VMEM((tiles * block, LANE), jnp.float32),
+        ],
+        compiler_params=pltpu.CompilerParams(vmem_limit_bytes=48 << 20),
+        cost_estimate=pl.CostEstimate(
+            flops=0, bytes_accessed=4 * rows_of * cols_of, transcendentals=0
+        ),
+        name="read_matrix",
+    )(flat)
+
+
+def write_flat(segs, parts):
+    specs = piece_specs()
+    block_rows = 192
+    total = sum(rows_of * cols_of // segs for rows_of, cols_of, _ in specs)
+    flat_rows = total // LANE
+    places = []
+    offset = 0
+    big, small = [], []
+    for (rows_of, cols_of, _), value in zip(specs, parts):
+        width = cols_of // segs
+        length = rows_of * width
+        if rows_of > 9:
+            assert rows_of % block_rows == 0
+            places.append((True, offset, rows_of, width, len(big)))
+            big.append(value)
+        else:
+            lead = offset % LANE
+            rest = -(lead + length) % LANE
+            padded = jnp.pad(value.reshape(-1), (lead, rest)).reshape(-1, LANE)
+            places.append((False, offset, length, None, len(small)))
+            small.append(padded)
+        offset += length
+    widths = sorted({place[3] for place in places if place[0]})
+    chunk = 1008
+
+    def kernel(*refs):
+        big_refs = refs[: len(big)]
+        small_refs = refs[len(big) : len(big) + len(small)]
+        out_ref = refs[len(big) + len(small)]
+        flat = refs[len(big) + len(small) + 1]
+        bufs = refs[len(big) + len(small) + 2 : len(big) + len(small) + 2 + len(widths)]
+        out_buf, in_sem, out_sem = refs[-3:]
+        lane_unit = lax.broadcasted_iota(jnp.int32, (8, LANE), 1) // UNIT
+        row_unit = lax.broadcasted_iota(jnp.int32, (1, LANE), 1) // UNIT
+
+        def place_small(ref, offset, length):
+            first = offset // LANE
+            last = (offset + length - 1) // LANE
+            lead = offset % LANE // UNIT
+            tail = (offset + length) % LANE // UNIT
+            count = last - first + 1
+            if count > 2:
+
+                def copy_row(at, _):
+                    flat[pl.ds(first + 1 + at, 1), :] = ref[pl.ds(1 + at, 1), :]
+                    return 0
+
+                lax.fori_loop(0, count - 2, copy_row, 0)
+            keep = row_unit >= lead
+            if count == 1 and tail:
+                keep = keep & (row_unit < tail)
+            flat[first : first + 1, :] = jnp.where(keep, ref[0:1, :], flat[first : first + 1, :])
+            if count > 1:
+                flat[last : last + 1, :] = (
+                    jnp.where(
+                        row_unit < tail, ref[count - 1 : count, :], flat[last : last + 1, :]
+                    )
+                    if tail
+                    else ref[count - 1 : count, :]
+                )
+
+        def place_big(ref, buf, offset, rows_of, width):
+            per_row = width // UNIT
+            first = offset // LANE
+            shift = offset % LANE // UNIT
+            block = block_rows
+            blocks = rows_of // block
+
+            tiles = -(-width // LANE)
+
+            def fetch(at, slot):
+                row = pl.multiple_of(at * block, 64)
+                return [
+                    pltpu.make_async_copy(
+                        ref.at[pl.ds(row, block), tile * LANE : (tile + 1) * LANE],
+                        buf.at[slot, tile],
+                        in_sem.at[slot, tile],
+                    )
+                    for tile in range(tiles)
+                ]
+
+            for copy in fetch(0, 0):
+                copy.start()
+
+            def one_block(at, _):
+                slot = lax.rem(at, 2)
+
+                @pl.when(at + 1 < blocks)
+                def _():
+                    for copy in fetch(at + 1, 1 - slot):
+                        copy.start()
+
+                for copy in fetch(at, slot):
+                    copy.wait()
+
+                def group(sub, _):
+                    loaded = {}
+                    turned = {}
+
+                    def unit_value(phase, unit, lane):
+                        key = (phase, unit // 4)
+                        if key not in loaded:
+                            loaded[key] = buf[
+                                slot, key[1], pl.ds(phase + sub * 32, 8, stride=4), :
+                            ]
+                        turn = (lane - unit) % 4
+                        if (key, turn) not in turned:
+                            turned[key, turn] = rolled(loaded[key], turn)
+                        return turned[key, turn]
+
+                    start = first + (at * (block // 4) + sub * 8) * per_row
+                    for row in range(per_row + (1 if shift else 0)):
+                        where = pl.ds(start + row, 8, stride=per_row)
+                        parts = []
+                        kept = None
+                        for lane in range(4):
+                            unit = 4 * row + lane - shift
+                            if unit < 0 or unit >= 4 * per_row:
+                                if kept is None:
+                                    kept = flat[where, :]
+                                parts.append(kept)
+                            else:
+                                parts.append(unit_value(unit // per_row, unit % per_row, lane))
+                        flat[where, :] = merge_units(parts, lane_unit)
+                    return 0
+
+                lax.fori_loop(0, block // 32, group, 0)
+                return 0
+
+            lax.fori_loop(0, blocks, one_block, 0)
+
+        for is_big, offset, rows_of, width, index in places:
+            if is_big:
+                place_big(big_refs[index], bufs[widths.index(width)], offset, rows_of, width)
+            else:
+                place_small(small_refs[index], offset, rows_of)
+
+        def emit(at, slot):
+            return pltpu.make_async_copy(
+                out_buf.at[slot],
+                out_ref.at[pl.ds(pl.multiple_of(at * chunk, 16), chunk), :],
+                out_sem.at[slot],
+            )
+
+        def one_chunk(at, _):
+            slot = lax.rem(at, 2)
+
+            @pl.when(at >= 2)
+            def _():
+                emit(at - 2, slot).wait()
+
+            def narrow(sub, _):
+                row = pl.multiple_of(sub * 16, 16)
+                out_buf[slot, pl.ds(row, 16), :] = flat[
+                    pl.ds(pl.multiple_of(at * chunk + row, 16), 16), :
+                ].astype(jnp.bfloat16)
+                return 0
+
+            lax.fori_loop(0, chunk // 16, narrow, 0, unroll=3)
+            emit(at, slot).start()
+            return 0
+
+        chunks = flat_rows // chunk
+        lax.fori_loop(0, chunks, one_chunk, 0)
+        emit(chunks - 2, (chunks - 2) % 2).wait()
+        emit(chunks - 1, (chunks - 1) % 2).wait()
+
+    return pl.pallas_call(
+        kernel,
+        in_specs=[pl.BlockSpec(memory_space=pl.ANY)] * len(big)
+        + [pl.BlockSpec(memory_space=pltpu.VMEM)] * len(small),
+        out_specs=pl.BlockSpec(memory_space=pl.ANY),
+        out_shape=jax.ShapeDtypeStruct((flat_rows, LANE), jnp.bfloat16),
+        scratch_shapes=[pltpu.VMEM((flat_rows, LANE), jnp.float32)]
+        + [
+            pltpu.VMEM((2, -(-width // LANE), block_rows, LANE), jnp.float32) for width in widths
+        ]
+        + [
+            pltpu.VMEM((2, chunk, LANE), jnp.bfloat16),
+            pltpu.SemaphoreType.DMA((2, -(-widths[-1] // LANE))),
+            pltpu.SemaphoreType.DMA((2,)),
+        ],
+        compiler_params=pltpu.CompilerParams(vmem_limit_bytes=56 << 20),
+        cost_estimate=pl.CostEstimate(flops=0, bytes_accessed=6 * total, transcendentals=0),
+        name="write_flat",
+    )(*big, *small)
+
+
+def gather_weights(shard_low, segs):
+    whole = lax.all_gather(shard_low.reshape(-1, LANE), ("seq", "dp"), axis=0, tiled=True)
+    flat = whole.reshape(segs, -1, LANE)
     pieces = []
     offset = 0
     for rows_of, cols_of, vector in piece_specs():
         length = rows_of * cols_of // segs
-        block = grid[:, offset : offset + length].reshape(segs, rows_of, cols_of // segs)
-        block = block.transpose(1, 0, 2).reshape(rows_of, cols_of)
-        pieces.append(block.reshape(cols_of) if vector else block)
+        if rows_of > 9:
+            pieces.append(read_matrix(flat, offset, rows_of, cols_of, segs))
+        else:
+            first, last = offset // LANE, -(-(offset + length) // LANE)
+            lead = offset - first * LANE
+            block = flat[:, first:last].reshape(segs, -1)[:, lead : lead + length]
+            block = block.reshape(segs, rows_of, cols_of // segs).transpose(1, 0, 2)
+            pieces.append(block.reshape(cols_of) if vector else block.reshape(rows_of, cols_of))
         offset = offset + length
     return pieces
-
-
-def gather_weights(shard_low, segs, count_dp, which):
-    if which == 0:
-        whole = lax.all_gather(shard_low, ("dp", "seq"), axis=0, tiled=True)
-    else:
-        whole = lax.all_gather(shard_low, ("dp", "seq"), axis=0, tiled=True)
-    grid = whole.reshape(count_dp, segs, -1).transpose(1, 0, 2).reshape(segs, -1)
-    return unpack(grid, segs)
 
 
 def norm_parts(values):
@@ -112,6 +408,7 @@
 def outer_sum(left_op, right_op):
     left_flat = left_op.reshape(-1, left_op.shape[-1])
     right_flat = right_op.reshape(-1, right_op.shape[-1])
+    right_flat = jnp.pad(right_flat, ((0, 0), (0, -right_flat.shape[1] % LANE)))
     return lax.dot_general(
         left_flat, right_flat, (((0,), (0,)), ((), ())), preferred_element_type=jnp.float32
     )
@@ -157,7 +454,7 @@
         b_depth,
         w_point,
         b_point,
-    ) = gather_weights(shard_low, segs, count_dp, 0)
+    ) = gather_weights(shard_low, segs)
     modulation = mod_table.astype(jnp.float32)[None] + time_embed.reshape(lat_dev, 6, D)
     shift_one = modulation[:, 0][:, None, :]
     scale_one = modulation[:, 1][:, None, :]
@@ -219,22 +516,6 @@
     gated_mix = to_low(up_part * jax.nn.silu(gate_part))
     branch_two = matmul(gated_mix, w_point) + b_point.astype(jnp.float32)
     output = (after_cross + gate_two * branch_two).astype(jnp.bfloat16).reshape(latents.shape)
-    (
-        mod_table,
-        w_qkv,
-        w_attn_out,
-        b_attn_out,
-        w_cross_q,
-        w_cross_kv,
-        w_cross_out,
-        b_cross_out,
-        w_in,
-        b_in,
-        w_depth,
-        b_depth,
-        w_point,
-        b_point,
-    ) = gather_weights(shard_low, segs, count_dp, 1)
     grad_out = cotangent.reshape(lat_dev, tokens_dev, D).astype(jnp.float32)
     grad_gate_two = jnp.sum(grad_out * branch_two, axis=1)
     grad_branch_two = to_low(grad_out * gate_two)
@@ -416,27 +697,32 @@
         [grad_b_attn_out, grad_b_cross_out, grad_b_in, depth_bias_q.ravel(), grad_b_point]
     )
     bias_total = lax.psum(bias_part, "dp")
-    quarter_grad = jnp.concatenate(
+    quarter_grad = write_flat(
+        segs,
         [
-            table_q.ravel(),
-            grad_w_qkv.ravel(),
-            grad_w_attn_out.ravel(),
+            table_q,
+            grad_w_qkv,
+            grad_w_attn_out,
             grad_b_attn_out,
-            grad_w_cross_q.ravel(),
-            grad_w_cross_kv.ravel(),
-            grad_w_cross_out.ravel(),
+            grad_w_cross_q,
+            grad_w_cross_kv,
+            grad_w_cross_out,
             grad_b_cross_out,
-            grad_w_in.ravel(),
+            grad_w_in,
             grad_b_in,
-            depth_q.ravel(),
-            depth_bias_q.ravel(),
-            grad_w_point.ravel(),
+            depth_q,
+            depth_bias_q,
+            grad_w_point,
             grad_b_point,
-        ]
-    )
-    grad_shard = lax.psum_scatter(
-        quarter_grad.reshape(1, -1).astype(jnp.bfloat16), "dp", scatter_dimension=1, tiled=True
-    ).astype(jnp.float32)
+        ],
+    )
+    grad_shard = (
+        lax.psum_scatter(
+            quarter_grad.reshape(count_dp, -1, LANE), "dp", scatter_dimension=0, tiled=True
+        )
+        .astype(jnp.float32)
+        .reshape(1, -1)
+    )
     square_total = lax.psum(jnp.sum(grad_shard * grad_shard), ("dp", "seq"))
     entries_all = grad_shard.size * lax.axis_size(("dp", "seq"))
     factor = lax.rsqrt(square_total / entries_all + 1e-06)

time: 2690 us -> 1230 us (0.46)
  local copies, waits for them, and re-layouts: 839 us -> 122 us
  waiting for transfers between devices: 1200 us -> 561 us
  other arithmetic: 364 us -> 129 us
  Pallas kernels: 0 us -> 147 us
    unnamed x10 -> x9, waiting for transfers between devices: 612 us -> 0.41 us
    unnamed x282 -> x268, local copies, waits for them, and re-layouts: 411 us -> 32.4 us
    all_gather x1 -> x0, other arithmetic: 245 us -> none  [gather_weights(): whole = lax.all_gather(shard_low, ('dp', 'seq'), axis=0, tiled=True)]
    all_gather x1, waiting for transfers between devices: 432 us -> 233 us  [gather_weights(): lax.all_gather(shard_low.reshape(-1, LANE), ('seq', 'dp'), axis=0, tiled=...]
    reduce_scatter x0 -> x1, waiting for transfers between devices: none -> 174 us  [shards(): lax.psum_scatter(quarter_grad.reshape(count_dp, -1, LANE), 'dp', scatter_...]
    reshape x8 -> x12, local copies, waits for them, and re-layouts: 173 us -> 12.2 us  [the longest x3 7.34 us: outer_sum(): right_flat = right_op.reshape(-1, right_op.shape[-1])]
    pallas_call x0 -> x8, Pallas kernels: none -> 147 us  [the longest x7 82.1 us: read_matrix(): pl.pallas_call(kernel, grid=(rows_of // block,), in_specs=[pl.BlockSpec((...]
    transpose x7 -> x0, local copies, waits for them, and re-layouts: 63.5 us -> none  [unpack(): block = block.transpose(1, 0, 2).reshape(rows_of, cols_of)]
  transfers between devices with their start and end apart: 13 -> 13, of which waited for: 5 -> 6; matrix products, arithmetic and copies ran while one was open for 14% -> 10% of each run, Pallas kernels for 0% -> 5%
where the time goes in v1:
time: 1230 us; the launch traced here: 1220 us
  waiting for transfers between devices  561 us (46%)
  Pallas kernels  147 us (12%)
  other arithmetic  129 us (10%)
  matrix products  124 us (10%)
  local copies, waits for them, and re-layouts  122 us (10%)
  blocking collectives  98.8 us (8%)
  starting transfers between devices  18.9 us (2%)
  between operations  16.7 us (1%)
    all_gather x1, waiting for transfers between devices, gather_weights(): lax.all_gather(shard_low.reshape(-1, LANE), ('seq', 'dp'), axis=0, tiled=...  233 us
    reduce_scatter x1, waiting for transfers between devices, shards(): lax.psum_scatter(quarter_grad.reshape(count_dp, -1, LANE), 'dp', scatter_...  174 us
    all_to_all x1, waiting for transfers between devices, shards(): lax.all_to_all(outputs_cat, 'seq', split_axis=2, concat_axis=1, tiled=True)  97.6 us
    pallas_call x7, Pallas kernels, read_matrix(): pl.pallas_call(kernel, grid=(rows_of // block,), in_specs=[pl.BlockSpec((...  82.1 us
    pallas_call x1, Pallas kernels, write_flat(): pl.pallas_call(kernel, in_specs=[pl.BlockSpec(memory_space=pl.ANY)] * len...  64.5 us
    psum x1, blocking collectives, shards(): square_total = lax.psum(jnp.sum(grad_shard * grad_shard), ('dp', 'seq'))  37 us
    psum x1, blocking collectives, shards(): bias_total = lax.psum(bias_part, 'dp')  35.2 us
    dot_general x7, matrix products, matmul(): return jnp.dot(left_op, right_op, preferred_element_type=jnp.float32)  33.7 us
  transfers between devices with their start and end apart: 13, of which 6 were waited for; matrix products, arithmetic and copies ran while one was open for 10% of the time, Pallas kernels for 5%

profile of v1, /device:TPU:0, one launch (start us, length us, event | category | flops | bytes accessed | tf_op | source)
XLA Modules:
  0.0 1216.6 jit_solution(13343432538675153151)
XLA Ops:
  7.2 28.9 %convert_reduce_fusion.1 = bf16[645120]{0:T(1024)(128)(2,1)} fusion(f32[1,645120]{1,0:T(1,128)} %param.11), kind=kLoop, calls=%fused_computation.81 | loop fusion | flops 645120 | bytes 3870720 | tf_op jit(solution)/shard_map/convert_element_type | solution.py:441
  37.0 233.3 %all-gather.3.cloned.1.call-done = bf16[161280,128]{1,0:T(8,128)(2,1)} async-done(((bf16[5040,128]{1,0:T(8,128)(2,1)}), bf16[161280,128]{1,0:T(8,128)(2,1)}) %all-gather.3.cloned.1.call-update) | async-done | bytes 41287696 | tf_op jit(solution)/shard_map/all_gather | solution.py:354
  273.6 10.3 read_matrix.9
  283.9 14.2 %read_matrix.7 = bf16[1152,3456]{1,0:T(8,128)(2,1)} custom-call(bf16[4,40320,128]{2,1,0:T(8,128)(2,1)} %bitcast.377), custom_call_target="tpu_custom_call" | custom-call | bytes 15925248 | tf_op jit(solution)/shard_map/read_matrix/pallas_call | solution.py:142
  301.4 5.8 convolution_bitcast_fusion
  317.0 12.0 psum.43
  335.2 6.9 read_matrix.11
  342.1 6.9 read_matrix.10
  350.6 6.9 read_matrix.8
  357.5 18.2 %read_matrix.13 = bf16[2880,1152]{1,0:T(8,128)(2,1)} custom-call(bf16[4,40320,128]{2,1,0:T(8,128)(2,1)} %bitcast.381), custom_call_target="tpu_custom_call" | custom-call | bytes 13271040 | tf_op jit(solution)/shard_map/read_matrix/pallas_call | solution.py:142
  375.7 18.6 %read_matrix.12 = bf16[1152,5760]{1,0:T(8,128)(2,1)} custom-call(bf16[4,40320,128]{2,1,0:T(8,128)(2,1)} %bitcast.382), custom_call_target="tpu_custom_call" | custom-call | bytes 26542080 | tf_op jit(solution)/shard_map/read_matrix/pallas_call | solution.py:142
  428.6 11.3 multiply_convert_fusion
  447.5 6.1 add_add_fusion
  464.0 9.4 multiply_convert_fusion.3
  478.5 16.7 %fusion.8 = (bf16[5760]{0:T(1024)(128)(2,1)}, bf16[5760]{0:T(1024)(128)(2,1)}, bf16[5760]{0:T(1024)(128)(2,1)}, bf16[5760]{0:T(1024)(128)(2,1)}, bf16[5760]{0:T(...) fusion(bf16[1,1,32,5760]{3,2,1,0:T(8,128)(2,1)} %copy-done.49, ...), kind=kLoop, calls=%fused_computation.21 | loop fusion | flops 58930560 | bytes 27383040 | tf_op jit(solution)/shard_map/lrcf,lrcf->f/dot_general | solution.py:533
  510.1 7.7 collective-permute-start.2
  523.8 6.0 multiply_add_fusion
  532.4 10.2 multiply_reduce_fusion.2
  577.0 6.1 fusion.39
  590.4 14.6 %all-reduce.18 = (bf16[36,32]{1,0:T(8,128)(2,1)S(1)}, bf16[1,4,1440]{2,1,0:T(4,128)(2,1)S(1)}) all-reduce(bf16[36,32]{1,0:T(8,128)(2,1)S(1)} %bitcast.454, bf16[1,4,1440]{2,1,0:T(4,128)(2,1)S(1)} %convert_element_type.576), channel_id=1, replica_groups=mesh['dp'=8,'seq'=4] {'seq'}, use_global_device_ids=true, to_apply=%region_14.15 | all-reduce | flops 6912 | bytes 27648 | tf_op jit(solution)/shard_map/psum | solution.py:601
  612.8 7.1 multiply_reduce_fusion.4
  660.2 24.2 %reduce-scatter.8.cloned.1.call-done = bf16[1,300,1,576]{1,3,2,0:T(8,128)(2,1)} async-done(((bf16[1,300,4,576]{1,3,2,0:T(8,128)(2,1)}), bf16[1,300,1,576]{1,3,2,0:T(8,128)(2,1)}) %reduce-scatter.8.cloned.1.call-update) | async-done | bytes 345616 | tf_op jit(solution)/shard_map/reduce_scatter | solution.py:580
  688.0 97.6 %all-to-all-done = bf16[1,256,4,3456]{1,3,0,2:T(8,128)(2,1)} async-done(((bf16[1,256,4,3456]{1,3,0,2:T(8,128)(2,1)}), bf16[1,256,4,3456]{1,3,0,2:T(8,128)(2,1)}, u32[]{:S(2)}, u32[]{:S(2)}) %all-to-all-start) | async-done | bytes 7077920 | tf_op jit(solution)/shard_map/all_to_all | solution.py:676
  785.6 10.2 copy.138
  812.2 30.8 %all-gather.5.cloned.1.call-done = bf16[1,1024,8640]{1,2,0:T(8,128)(2,1)} async-done(((bf16[1,256,8640]{1,2,0:T(8,128)(2,1)}), bf16[1,1024,8640]{1,2,0:T(8,128)(2,1)}) %all-gather.5.cloned.1.call-update) | async-done | bytes 17694736 | tf_op jit(solution)/shard_map/all_gather | solution.py:660
  843.1 6.5 fusion.26.refs_0_
  864.9 5.9 fusion.15.refs_5_
  870.8 64.5 %write_flat.1 = bf16[40320,128]{1,0:T(8,128)(2,1)} custom-call(f32[1152,896]{1,0:T(8,128)} %fusion.26.refs_0_, f32[1152,384]{1,0:T(8,128)} %fusion.25.refs_1_, f32[1152,384]{1,0:T(8,128)} %fusion.24.refs_2_, f32[1152,640]{1,0:T(8,128)} %convolution_bitcast_fusion.2.refs_3_, f32[1152,384]{1,0:T(8,128)} %fusion.23.refs_4_, f32[1152,1536]{1,0:T(8,128)} %fusion.15.refs_5_, ...), custom_call_target="tpu_custom_call" | custom-call | bytes 30965760 | tf_op jit(solution)/shard_map/write_flat/pallas_call | solution.py:332
  935.4 174.2 %reduce-scatter.12.cloned.1.call-done = bf16[1,5040,128]{2,1,0:T(8,128)(2,1)} async-done(((bf16[8,5040,128]{2,1,0:T(8,128)(2,1)}), bf16[1,5040,128]{2,1,0:T(8,128)(2,1)}) %reduce-scatter.12.cloned.1.call-update) | async-done | bytes 1290256 | tf_op jit(solution)/shard_map/reduce_scatter | solution.py:720
  1112.2 35.2 %psum.47 = f32[3744]{0:T(1024)S(1)} all-reduce(f32[3744]{0:T(1024)S(1)} %concatenate.128), channel_id=1, replica_groups=mesh['dp'=8,'seq'=4] {'dp'}, use_global_device_ids=true, to_apply=%region_35.36 | all-reduce | flops 3744 | bytes 29952 | tf_op jit(solution)/shard_map/psum | solution.py:699
  1147.4 37.0 %psum.46 = f32[]{:T(128)} all-reduce(f32[]{:T(128)} %fusion.21), channel_id=1, replica_groups=mesh['dp'=8,'seq'=4] {'dp','seq'}, use_global_device_ids=true, to_apply=%region_34.35 | all-reduce | flops 1 | bytes 8 | tf_op jit(solution)/shard_map/psum | solution.py:726
  1187.2 22.4 %multiply_add_fusion.1 = (f32[1,645120]{1,0:T(1,128)}, f32[1,645120]{1,0:T(1,128)}, f32[1,645120]{1,0:T(1,128)}) fusion(f32[1,645120]{1,0:T(1,128)} %param.11, f32[1,645120]{1,0:T(1,128)S(1)} %bitcast.405, f32[1,645120]{1,0:T(1,128)} %param.13, f32[1,645120]{1,0:T(1,128)} %param.12), kind=kLoop, calls=%fused_computation.79 | loop fusion | flops 8386560 | bytes 18063360 | tf_op jit(solution)/shard_map/add | solution.py:735
  (460 shorter events, 234.3 us)
Async XLA Ops:
  7.2 304.1 %copy-start = (bf16[1,300,1152]{2,1,0:T(8,128)(2,1)S(1)}, bf16[1,300,1152]{2,1,0:T(8,128)(2,1)}, u32[]{:S(2)}) copy-start(bf16[1,300,1152]{2,1,0:T(8,128)(2,1)} %param.8) | copy-start | bytes 2073604
  7.2 29.0 %copy-start.18 = (bf16[1,8,32,1152]{3,2,1,0:T(8,128)(2,1)S(1)}, bf16[1,8,32,1152]{3,2,1,0:T(8,128)(2,1)}, u32[]{:S(2)}) copy-start(bf16[1,8,32,1152]{3,2,1,0:T(8,128)(2,1)} %param.7) | copy-start | bytes 1769476
  7.2 29.3 %copy-start.102 = (f32[1,6912]{1,0:T(1,128)S(1)}, f32[1,6912]{1,0:T(1,128)}, u32[]{:S(2)}) copy-start(f32[1,6912]{1,0:T(1,128)} %param.9) | copy-start | bytes 82948
  7.2 263.2 %all-gather.3.cloned.1.call-start = ((), (), s32[]{:S(2)}) async-start(), calls=%async_computation.5 | async-start | bytes 42577920 | tf_op jit(solution)/shard_map/all_gather | solution.py:354
  36.2 371.6 %all-reduce.22.cloned.1.call-start = ((), (), s32[]{:S(2)}) async-start(), calls=%async_computation.6 | async-start | bytes 1179648 | tf_op jit(solution)/shard_map/psum | solution.py:478
  36.5 263.8 %copy-start.103 = (f32[256]{0:T(256)}, f32[256]{0:T(256)S(1)}, u32[]{:S(2)}) copy-start(f32[256]{0:T(256)S(1)} %div.82) | copy-start | bytes 3076
  37.0 263.2 %copy-start.106 = (f32[256]{0:T(256)}, f32[256]{0:T(256)S(1)}, u32[]{:S(2)}) copy-start(f32[256]{0:T(256)S(1)} %add_rsqrt_fusion.1) | copy-start | bytes 3076
  283.9 14.2 %copy-start.3 = (bf16[1152,2304]{1,0:T(8,128)(2,1)}, bf16[1152,2304]{1,0:T(8,128)(2,1)S(1)}, u32[]{:S(2)}) copy-start(bf16[1152,2304]{1,0:T(8,128)(2,1)S(1)} %read_matrix.9) | copy-start | bytes 15925252
  283.9 16.3 %copy-start.25 = (bf16[1,8,32,1152]{3,2,1,0:T(8,128)(2,1)S(1)}, bf16[1,8,32,1152]{3,2,1,0:T(8,128)(2,1)}, u32[]{:S(2)}) copy-start(bf16[1,8,32,1152]{3,2,1,0:T(8,128)(2,1)} %param.10) | copy-start | bytes 1769476
  332.0 273.1 %all-reduce.24.cloned.1.call-start = ((), (), s32[]{:S(2)}) async-start(), calls=%async_computation.7 | async-start | bytes 589824 | tf_op jit(solution)/shard_map/psum | solution.py:600
  357.5 18.2 %copy-start.4 = (bf16[1152,1152]{1,0:T(8,128)(2,1)}, bf16[1152,1152]{1,0:T(8,128)(2,1)S(1)}, u32[]{:S(2)}) copy-start(bf16[1152,1152]{1,0:T(8,128)(2,1)S(1)} %read_matrix.8) | copy-start | bytes 7962628
  428.6 14.3 %copy-start.69 = (bf16[1,256,36,32]{1,3,2,0:T(8,128)(2,1)S(1)}, bf16[1,256,36,32]{1,3,2,0:T(8,128)(2,1)}, u32[]{:S(2)}) copy-start(bf16[1,256,36,32]{1,3,2,0:T(8,128)(2,1)} %copy-done.68) | copy-start | bytes 1769476
  440.0 5.5 collective-permute-start
  441.4 4.4 collective-permute-start.1
  507.7 11.8 copy-start.94
  507.7 11.8 copy-start.93
  507.7 11.9 copy-start.89
  507.7 11.9 copy-start.91
  507.7 11.9 copy-start.90
  507.7 11.9 copy-start.11
  507.7 11.9 copy-start.12
  510.1 11.4 collective-permute-start.2
  517.8 3.7 collective-permute-start.3
  562.2 93.7 %reduce-scatter.10.cloned.1.call-start = ((), (), s32[]{:S(2)}) async-start(), calls=%async_computation.10 | async-start | bytes 245760 | tf_op jit(solution)/shard_map/reduce_scatter | solution.py:644
  563.1 95.8 %reduce-scatter.14.cloned.1.call-start = ((), (), s32[]{:S(2)}) async-start(), calls=%async_computation.12 | async-start | bytes 30720
  586.9 18.1 %copy-start.38 = (bf16[1,256,1152]{1,2,0:T(8,128)(2,1)S(1)}, bf16[1,256,1152]{1,2,0:T(8,128)(2,1)}, u32[]{:S(2)}) copy-start(bf16[1,256,1152]{1,2,0:T(8,128)(2,1)} %copy-done.37) | copy-start | bytes 1769476
  589.0 18.4 %copy-start.36 = (bf16[1,256,1152]{1,2,0:T(8,128)(2,1)S(1)}, bf16[1,256,1152]{1,2,0:T(8,128)(2,1)}, u32[]{:S(2)}) copy-start(bf16[1,256,1152]{1,2,0:T(8,128)(2,1)} %copy-done.35) | copy-start | bytes 1769476
  624.2 60.2 %reduce-scatter.8.cloned.1.call-start = ((), (), s32[]{:S(2)}) async-start(), calls=%async_computation.9 | async-start | bytes 2211840 | tf_op jit(solution)/shard_map/reduce_scatter | solution.py:580
  627.0 216.1 %all-gather.5.cloned.1.call-start = ((), (), s32[]{:S(2)}) async-start(), calls=%async_computation.8 | async-start | bytes 22118400 | tf_op jit(solution)/shard_map/all_gather | solution.py:660
  649.5 136.1 %all-to-all-start = ((bf16[1,256,4,3456]{1,3,0,2:T(8,128)(2,1)}), bf16[1,256,4,3456]{1,3,0,2:T(8,128)(2,1)}, u32[]{:S(2)}, u32[]{:S(2)}) async-start(bf16[1,256,4,3456]{1,3,0,2:T(8,128)(2,1)} %bitcast.404), calls=%async_computation | async-start | bytes 14155776 | tf_op jit(solution)/shard_map/all_to_all | solution.py:676
  655.2 454.4 %reduce-scatter.12.cloned.1.call-start = ((), (), s32[]{:S(2)}) async-start(), calls=%async_computation.11 | async-start | bytes 11612160 | tf_op jit(solution)/shard_map/reduce_scatter | solution.py:720
  1187.2 22.4 %copy-start.24 = (f32[1,5040,128]{2,1,0:T(8,128)}, f32[1,5040,128]{2,1,0:T(8,128)S(1)}, u32[]{:S(2)}) copy-start(f32[1,5040,128]{2,1,0:T(8,128)S(1)} %convert_multiply_fusion.9) | copy-start | bytes 7741444
  (99 other events, 396.3 us)
Sparse Core Ops, SparseCore 0:
  36.3 234.0 all-gather.2
  332.1 31.8 all-reduce.21
  562.3 34.7 all-reduce.23
  599.3 19.7 reduce-scatter.9
  624.3 18.1 reduce-scatter.13
  645.6 38.7 reduce-scatter.7
  685.9 157.0 all-gather.4
  935.5 174.1 reduce-scatter.11

commit v2 on v1

--- a/solution.py
+++ b/solution.py
@@ -350,8 +350,21 @@
     )(*big, *small)
 
 
+def round_rows(values):
+    def kernel(in_ref, out_ref):
+        out_ref[...] = in_ref[...].astype(jnp.bfloat16)
+
+    return pl.pallas_call(
+        kernel,
+        in_specs=[pl.BlockSpec(memory_space=pltpu.VMEM)],
+        out_specs=pl.BlockSpec(memory_space=pltpu.VMEM),
+        out_shape=jax.ShapeDtypeStruct(values.shape, jnp.bfloat16),
+        name="round_rows",
+    )(values)
+
+
 def gather_weights(shard_low, segs):
-    whole = lax.all_gather(shard_low.reshape(-1, LANE), ("seq", "dp"), axis=0, tiled=True)
+    whole = lax.all_gather(shard_low, ("seq", "dp"), axis=0, tiled=True)
     flat = whole.reshape(segs, -1, LANE)
     pieces = []
     offset = 0
@@ -369,6 +382,195 @@
     return pieces
 
 
+MESH = pl.DeviceIdType.MESH
+
+
+def peer_barrier(groups):
+    barrier = pltpu.get_barrier_semaphore()
+    total = 0
+    for axis, count in groups:
+        me = lax.axis_index(axis)
+        for step in range(1, count):
+            pl.semaphore_signal(
+                barrier, inc=1, device_id={axis: lax.rem(me + step, count)}, device_id_type=MESH
+            )
+        total += count - 1
+    pl.semaphore_wait(barrier, total)
+
+
+def exchange(axis, count, source, slots, send_sem, recv_sem):
+    me = lax.axis_index(axis)
+    for step in range(1, count):
+        pltpu.make_async_remote_copy(
+            src_ref=source,
+            dst_ref=slots.at[me],
+            send_sem=send_sem.at[step - 1],
+            recv_sem=recv_sem.at[me],
+            device_id={axis: lax.rem(me + step, count)},
+            device_id_type=MESH,
+        ).start()
+
+
+def exchange_wait(axis, count, source, slots, send_sem, recv_sem):
+    me = lax.axis_index(axis)
+    for step in range(1, count):
+        peer = lax.rem(me + step, count)
+        copy = pltpu.make_async_remote_copy(
+            src_ref=source,
+            dst_ref=slots.at[peer],
+            send_sem=send_sem.at[step - 1],
+            recv_sem=recv_sem.at[peer],
+            device_id={axis: peer},
+            device_id_type=MESH,
+        )
+        copy.wait_send()
+        copy.wait_recv()
+
+
+def in_order(axis, count, own, slots):
+    me = lax.axis_index(axis)
+    total = None
+    for index in range(count):
+        term = jnp.where(me == index, own, slots[index].astype(jnp.float32))
+        total = term if total is None else total + term
+    return total
+
+
+def seq_sum(block, collective_id):
+    count = lax.axis_size("seq")
+
+    def kernel(in_ref, out_ref, slots, send_sem, recv_sem):
+        peer_barrier([("seq", count)])
+        exchange("seq", count, in_ref, slots, send_sem, recv_sem)
+        exchange_wait("seq", count, in_ref, slots, send_sem, recv_sem)
+        out_ref[...] = in_order("seq", count, in_ref[...].astype(jnp.float32), slots)
+
+    return pl.pallas_call(
+        kernel,
+        in_specs=[pl.BlockSpec(memory_space=pltpu.VMEM)],
+        out_specs=pl.BlockSpec(memory_space=pltpu.VMEM),
+        out_shape=jax.ShapeDtypeStruct(block.shape, jnp.float32),
+        scratch_shapes=[
+            pltpu.VMEM((count,) + block.shape, block.dtype),
+            pltpu.SemaphoreType.DMA((count - 1,)),
+            pltpu.SemaphoreType.DMA((count,)),
+        ],
+        compiler_params=pltpu.CompilerParams(collective_id=collective_id, has_side_effects=True),
+        name="seq_sum",
+    )(block)
+
+
+def state_sum(state, sums, kind, collective_id):
+    heads = state.shape[1]
+    flat = jnp.concatenate(
+        [state.reshape(-1, LANE), jnp.pad(sums.reshape(-1), (0, -sums.size % LANE)).reshape(-1, LANE)]
+    ).astype(kind)
+    rows = flat.shape[0]
+    flat = jnp.pad(flat, ((0, -rows % 16), (0, 0)))
+    total = seq_sum(flat, collective_id)
+    split = state.size // LANE
+    return (
+        total[:split].reshape(state.shape),
+        total[split:].reshape(-1)[: sums.size].reshape(1, heads, -1),
+    )
+
+
+def finish(grad_shard, bias_part, params, moment_one, moment_two):
+    rows = grad_shard.shape[0]
+    count_dp = lax.axis_size("dp")
+    count_seq = lax.axis_size("seq")
+    entries = rows * LANE * count_dp * count_seq
+    chunk = 48 if rows % 48 == 0 else rows
+    bias_rows = bias_part.shape[0]
+
+    def kernel(
+        grad_ref,
+        bias_ref,
+        param_ref,
+        one_ref,
+        two_ref,
+        gradient_ref,
+        one_out,
+        two_out,
+        update_ref,
+        bias_out,
+        square,
+        square_dp,
+        square_seq,
+        partial,
+        bias_slots,
+        send_bias,
+        recv_bias,
+        send_dp,
+        recv_dp,
+        send_seq,
+        recv_seq,
+    ):
+        peer_barrier([("dp", count_dp), ("seq", count_seq)])
+        exchange("dp", count_dp, bias_ref, bias_slots, send_bias, recv_bias)
+
+        def squares(at, total):
+            part = grad_ref[pl.ds(at * chunk, chunk), :].astype(jnp.float32)
+            return total + jnp.sum(part * part, axis=0, keepdims=True)
+
+        total = lax.fori_loop(0, rows // chunk, squares, jnp.zeros((1, LANE), jnp.float32))
+        square[...] = jnp.broadcast_to(total, (8, LANE))
+        exchange("dp", count_dp, square, square_dp, send_dp, recv_dp)
+        exchange_wait("dp", count_dp, square, square_dp, send_dp, recv_dp)
+        partial[...] = in_order("dp", count_dp, square[...], square_dp)
+        exchange("seq", count_seq, partial, square_seq, send_seq, recv_seq)
+        exchange_wait("seq", count_seq, partial, square_seq, send_seq, recv_seq)
+        whole = jnp.sum(
+            in_order("seq", count_seq, partial[...], square_seq)[0:1], axis=1, keepdims=True
+        )
+        factor = lax.rsqrt(whole / entries + 1e-06)
+        exchange_wait("dp", count_dp, bias_ref, bias_slots, send_bias, recv_bias)
+        bias_out[...] = in_order("dp", count_dp, bias_ref[...], bias_slots) * factor
+
+        def step(at, _):
+            where = pl.ds(at * chunk, chunk)
+            gradient = grad_ref[where, :].astype(jnp.float32) * factor
+            first = beta_first * one_ref[where, :] + (1.0 - beta_first) * gradient
+            second = beta_second * two_ref[where, :] + (1.0 - beta_second) * gradient * gradient
+            gradient_ref[where, :] = gradient
+            one_out[where, :] = first
+            two_out[where, :] = second
+            first_hat = first / (1.0 - beta_first**adam_steps)
+            second_hat = second / (1.0 - beta_second**adam_steps)
+            update_ref[where, :] = (
+                first_hat / (jnp.sqrt(second_hat) + adam_eps) + weight_decay * param_ref[where, :]
+            )
+            return 0
+
+        lax.fori_loop(0, rows // chunk, step, 0)
+
+    flat = jax.ShapeDtypeStruct((rows, LANE), jnp.float32)
+    tile = (8, LANE)
+    return pl.pallas_call(
+        kernel,
+        in_specs=[pl.BlockSpec(memory_space=pltpu.VMEM)] * 5,
+        out_specs=[pl.BlockSpec(memory_space=pltpu.VMEM)] * 5,
+        out_shape=[flat] * 4 + [jax.ShapeDtypeStruct((bias_rows, LANE), jnp.float32)],
+        scratch_shapes=[
+            pltpu.VMEM(tile, jnp.float32),
+            pltpu.VMEM((count_dp,) + tile, jnp.float32),
+            pltpu.VMEM((count_seq,) + tile, jnp.float32),
+            pltpu.VMEM(tile, jnp.float32),
+            pltpu.VMEM((count_dp, bias_rows, LANE), jnp.float32),
+            pltpu.SemaphoreType.DMA((count_dp - 1,)),
+            pltpu.SemaphoreType.DMA((count_dp,)),
+            pltpu.SemaphoreType.DMA((count_dp - 1,)),
+            pltpu.SemaphoreType.DMA((count_dp,)),
+            pltpu.SemaphoreType.DMA((count_seq - 1,)),
+            pltpu.SemaphoreType.DMA((count_seq,)),
+        ],
+        compiler_params=pltpu.CompilerParams(
+            collective_id=1, has_side_effects=True, vmem_limit_bytes=48 << 20
+        ),
+        name="finish",
+    )(grad_shard, bias_part, params, moment_one, moment_two)
+
+
 def norm_parts(values):
     centred = values - jnp.mean(values, axis=-1, keepdims=True)
     inverse = lax.rsqrt(jnp.mean(centred * centred, axis=-1, keepdims=True) + eps_norm)
@@ -438,7 +640,43 @@
     text_len = text.shape[1]
     segs = lax.axis_size("seq")
     count_dp = lax.axis_size("dp")
-    shard_low = params.astype(jnp.bfloat16)
+    def spread(values):
+        joined = jnp.concatenate(values, axis=-1).reshape(-1, sum(v.shape[-1] for v in values))
+        whole = lax.all_gather(joined, "seq", axis=0, tiled=True)
+        parts = []
+        at = 0
+        for value in values:
+            parts.append(whole[:, at : at + value.shape[-1]])
+            at += value.shape[-1]
+        return parts
+
+    def collect(values):
+        blocks = jnp.stack(
+            [
+                jnp.concatenate(
+                    [
+                        value.reshape(-1, value.shape[-1])[
+                            :, seg * (value.shape[-1] // segs) : (seg + 1) * (value.shape[-1] // segs)
+                        ]
+                        for value in values
+                    ],
+                    axis=1,
+                )
+                for seg in range(segs)
+            ]
+        )
+        mine = lax.all_to_all(blocks, "seq", split_axis=0, concat_axis=0, tiled=True)
+        mine = mine.reshape(-1, mine.shape[-1])
+        parts = []
+        at = 0
+        for value in values:
+            width = value.shape[-1] // segs
+            parts.append(mine[:, at : at + width])
+            at += width
+        return parts
+
+    params_rows = params.reshape(-1, LANE)
+    shard_low = round_rows(params_rows)
     (
         mod_table,
         w_qkv,
@@ -475,7 +713,7 @@
         "lrhd,lrhe->lhde", keys_lin, values_lin, preferred_element_type=jnp.float32
     )
     sum_part = jnp.sum(keys_lin, axis=1, dtype=jnp.float32)
-    kv_state, key_sum = lax.psum((state_part, sum_part), "seq")
+    kv_state, key_sum = state_sum(state_part, sum_part, jnp.float32, 2)
     query_f = queries.astype(jnp.float32)
     numerator = jnp.einsum("lrhd,lhde->lrhe", query_f, kv_state, precision=precise)
     denominator = jnp.einsum("lrhd,lhd->lrh", query_f, key_sum, precision=precise) + eps_linear
@@ -514,11 +752,20 @@
     up_part = conv_out[..., :FF]
     gate_part = conv_out[..., FF:]
     gated_mix = to_low(up_part * jax.nn.silu(gate_part))
-    branch_two = matmul(gated_mix, w_point) + b_point.astype(jnp.float32)
+    branch_two = lax.optimization_barrier(
+        matmul(gated_mix, w_point) + b_point.astype(jnp.float32)
+    )
     output = (after_cross + gate_two * branch_two).astype(jnp.bfloat16).reshape(latents.shape)
     grad_out = cotangent.reshape(lat_dev, tokens_dev, D).astype(jnp.float32)
     grad_gate_two = jnp.sum(grad_out * branch_two, axis=1)
     grad_branch_two = to_low(grad_out * gate_two)
+    grad_branch_two, x_qkv, x_attn, x_cross_q, x_cross_out, x_inner = lax.optimization_barrier(
+        (
+            grad_branch_two,
+            *spread([hidden_one, attended, after_low]),
+            *spread([cross_mixed, hidden_two]),
+        )
+    )
     grad_gated = matmul_t(grad_branch_two, w_point)
     grad_up = grad_gated * jax.nn.silu(gate_part)
     grad_gate = grad_gated * up_part * silu_slope(gate_part)
@@ -543,6 +790,7 @@
         lat_dev, tokens_dev, 2 * FF
     )
     grad_inner = to_low(grad_active * silu_slope(inner_pre))
+    grad_inner, x_point = lax.optimization_barrier((grad_inner, *spread([gated_mix])))
     grad_hidden_two = matmul_t(grad_inner, w_in)
     grad_shift_two = jnp.sum(grad_hidden_two, axis=1)
     grad_scale_two = jnp.sum(grad_hidden_two * normed_two, axis=1)
@@ -585,6 +833,9 @@
     grad_first = grad_second + matmul_t(grad_query_c, w_cross_q)
     grad_gate_one = jnp.sum(grad_first * branch_one, axis=1)
     grad_branch_one = to_low(grad_first * gate_one)
+    grad_branch_one, y_point, y_inner = lax.optimization_barrier(
+        (grad_branch_one, *collect([grad_branch_two, grad_inner]))
+    )
     grad_attended = matmul_t(grad_branch_one, w_attn_out).reshape(
         lat_dev, tokens_dev, heads_lin, 32
     )
@@ -596,10 +847,7 @@
     )
     state_grad_part = jnp.einsum("lrhd,lrhe->lhde", query_f, grad_numer, precision=precise)
     sum_grad_part = jnp.einsum("lrhd,lrh->lhd", query_f, grad_denom, precision=precise)
-    state_grad, sum_grad = (
-        lax.psum(state_grad_part.astype(jnp.bfloat16), "seq").astype(jnp.float32),
-        lax.psum(sum_grad_part.astype(jnp.bfloat16), "seq").astype(jnp.float32),
-    )
+    state_grad, sum_grad = state_sum(state_grad_part, sum_grad_part, jnp.bfloat16, 3)
     keys_f = keys_lin.astype(jnp.float32)
     values_f = values_lin.astype(jnp.float32)
     grad_keys = (
@@ -615,6 +863,9 @@
             ],
             axis=-1,
         )
+    )
+    grad_projected, y_cross_out, y_cross_q, y_attn = lax.optimization_barrier(
+        (grad_projected, *collect([grad_cross_out, grad_query_c, grad_branch_one]))
     )
     grad_hidden_one = matmul_t(grad_projected, w_qkv)
     grad_input = grad_first + norm_back(
@@ -634,69 +885,44 @@
         ),
         axis=0,
     )
-    table_q, depth_q, depth_bias_q = (
-        lax.psum_scatter(
-            grad_table.reshape(6, segs, D // segs).astype(jnp.bfloat16),
-            "seq",
-            scatter_dimension=1,
-            tiled=True,
-        ).astype(jnp.float32),
-        lax.psum_scatter(
-            grad_w_depth.reshape(9, segs, 2 * FF // segs).astype(jnp.bfloat16),
-            "seq",
-            scatter_dimension=1,
-            tiled=True,
-        ).astype(jnp.float32),
-        lax.psum_scatter(
-            grad_b_depth.reshape(1, segs, 2 * FF // segs).astype(jnp.bfloat16),
-            "seq",
-            scatter_dimension=1,
-            tiled=True,
-        ).astype(jnp.float32),
-    )
-    inputs_cat = jnp.concatenate(
-        [hidden_one, attended, after_low, cross_mixed, hidden_two, gated_mix], axis=-1
-    )
-    inputs_all = lax.all_gather(inputs_cat, "seq", axis=1, tiled=True)
-
-    def quarters(values):
-        return values.reshape(lat_dev, tokens_dev, segs, values.shape[-1] // segs)
-
-    outputs_cat = jnp.concatenate(
-        [
-            quarters(grad_projected),
-            quarters(grad_branch_one),
-            quarters(grad_query_c),
-            quarters(grad_cross_out),
-            quarters(grad_inner),
-            quarters(grad_branch_two),
-        ],
-        axis=-1,
-    )
-    outputs_mine = lax.all_to_all(outputs_cat, "seq", split_axis=2, concat_axis=1, tiled=True)
-    outputs_mine = outputs_mine.reshape(lat_dev, outputs_mine.shape[1], outputs_mine.shape[3])
+    grad_table = lax.optimization_barrier(grad_table)
     col_d = D // segs
     col_ff = 2 * FF // segs
-    y_qkv = outputs_mine[..., 0 : 3 * col_d]
-    y_attn = outputs_mine[..., 3 * col_d : 4 * col_d]
-    y_cross_q = outputs_mine[..., 4 * col_d : 5 * col_d]
-    y_cross_out = outputs_mine[..., 5 * col_d : 6 * col_d]
-    y_inner = outputs_mine[..., 6 * col_d : 6 * col_d + col_ff]
-    y_point = outputs_mine[..., 6 * col_d + col_ff : 7 * col_d + col_ff]
-    grad_w_qkv = outer_sum(inputs_all[..., 0:D], y_qkv)
-    grad_w_attn_out = outer_sum(inputs_all[..., D : 2 * D], y_attn)
-    grad_w_cross_q = outer_sum(inputs_all[..., 2 * D : 3 * D], y_cross_q)
-    grad_w_cross_out = outer_sum(inputs_all[..., 3 * D : 4 * D], y_cross_out)
-    grad_w_in = outer_sum(inputs_all[..., 4 * D : 5 * D], y_inner)
-    grad_w_point = outer_sum(inputs_all[..., 5 * D : 5 * D + FF], y_point)
-    grad_b_attn_out = jnp.sum(y_attn, axis=(0, 1), dtype=jnp.float32)
-    grad_b_cross_out = jnp.sum(y_cross_out, axis=(0, 1), dtype=jnp.float32)
-    grad_b_in = jnp.sum(y_inner, axis=(0, 1), dtype=jnp.float32)
-    grad_b_point = jnp.sum(y_point, axis=(0, 1), dtype=jnp.float32)
+    small_parts = jnp.concatenate(
+        [
+            grad_table.reshape(6, segs, col_d).transpose(1, 0, 2).reshape(segs, -1),
+            grad_w_depth.reshape(9, segs, col_ff).transpose(1, 0, 2).reshape(segs, -1),
+            grad_b_depth.reshape(segs, col_ff),
+        ],
+        axis=1,
+    ).astype(jnp.bfloat16)
+    small_parts = small_parts.reshape(segs, -1, LANE)
+    small_mine = (
+        lax.psum_scatter(small_parts, "seq", scatter_dimension=0, tiled=True)
+        .astype(jnp.float32)
+        .reshape(-1)
+    )
+    table_q = small_mine[: 6 * col_d].reshape(6, col_d)
+    depth_q = small_mine[6 * col_d : 6 * col_d + 9 * col_ff].reshape(9, col_ff)
+    depth_bias_q = small_mine[6 * col_d + 9 * col_ff :].reshape(1, col_ff)
+
+    (y_qkv,) = collect([grad_projected])
+    grad_w_qkv = outer_sum(x_qkv, y_qkv)
+    grad_w_attn_out = outer_sum(x_attn, y_attn)
+    grad_w_cross_q = outer_sum(x_cross_q, y_cross_q)
+    grad_w_cross_out = outer_sum(x_cross_out, y_cross_out)
+    grad_w_in = outer_sum(x_inner, y_inner)
+    grad_w_point = outer_sum(x_point, y_point)
+    grad_b_attn_out = jnp.sum(y_attn, axis=0, dtype=jnp.float32)
+    grad_b_cross_out = jnp.sum(y_cross_out, axis=0, dtype=jnp.float32)
+    grad_b_in = jnp.sum(y_inner, axis=0, dtype=jnp.float32)
+    grad_b_point = jnp.sum(y_point, axis=0, dtype=jnp.float32)
     bias_part = jnp.concatenate(
         [grad_b_attn_out, grad_b_cross_out, grad_b_in, depth_bias_q.ravel(), grad_b_point]
     )
-    bias_total = lax.psum(bias_part, "dp")
+    len_bias = bias_part.size
+    bias_rows = -(-bias_part.size // (8 * LANE)) * 8
+    bias_part = jnp.pad(bias_part, (0, bias_rows * LANE - bias_part.size)).reshape(-1, LANE)
     quarter_grad = write_flat(
         segs,
         [
@@ -716,23 +942,19 @@
             grad_b_point,
         ],
     )
-    grad_shard = (
-        lax.psum_scatter(
-            quarter_grad.reshape(count_dp, -1, LANE), "dp", scatter_dimension=0, tiled=True
-        )
-        .astype(jnp.float32)
-        .reshape(1, -1)
-    )
-    square_total = lax.psum(jnp.sum(grad_shard * grad_shard), ("dp", "seq"))
-    entries_all = grad_shard.size * lax.axis_size(("dp", "seq"))
-    factor = lax.rsqrt(square_total / entries_all + 1e-06)
-    gradient = grad_shard * factor
-    bias_grads = (bias_total * factor).reshape(1, -1)
-    moment_one_new = beta_first * moment_one + (1.0 - beta_first) * gradient
-    moment_two_new = beta_second * moment_two + (1.0 - beta_second) * gradient * gradient
-    first_hat = moment_one_new / (1.0 - beta_first**adam_steps)
-    second_hat = moment_two_new / (1.0 - beta_second**adam_steps)
-    update = first_hat / (jnp.sqrt(second_hat) + adam_eps) + weight_decay * params
+    grad_shard = lax.psum_scatter(
+        quarter_grad.reshape(count_dp, -1, LANE), "dp", scatter_dimension=0, tiled=True
+    ).reshape(-1, LANE)
+    *flat_outs, bias_grads = finish(
+        grad_shard,
+        bias_part,
+        params_rows,
+        moment_one.reshape(-1, LANE),
+        moment_two.reshape(-1, LANE),
+    )
+    gradient, moment_one_new, moment_two_new, update = [
+        value.reshape(params.shape) for value in flat_outs
+    ]
     return (
         output,
         grad_input.reshape(latents.shape),
@@ -740,7 +962,7 @@
         moment_one_new,
         moment_two_new,
         update,
-        bias_grads,
+        bias_grads.reshape(1, -1)[:, :len_bias],
     )
 
 

time: 1230 us -> 1060 us (0.86)
  waiting for transfers between devices: 561 us -> 452 us
  blocking collectives: 98.8 us -> 0 us
  Pallas kernels: 147 us -> 188 us
  other arithmetic: 129 us -> 89.9 us
  local copies, waits for them, and re-layouts: 122 us -> 152 us
  starting transfers between devices: 18.9 us -> 34.4 us
    psum x4 -> x0, blocking collectives: 98.8 us -> none  [the longest x1 37 us: shards(): square_total = lax.psum(jnp.sum(grad_shard * grad_shard), ('dp', 'seq'))]
    all_to_all x1 -> x3, waiting for transfers between devices: 97.6 us -> 31.3 us  [collect(): lax.all_to_all(blocks, 'seq', split_axis=0, concat_axis=0, tiled=True)]
    pallas_call x0 -> x4, Pallas kernels: none -> 41.3 us  [the longest x1 21.1 us: finish(): pl.pallas_call(kernel, in_specs=[pl.BlockSpec(memory_space=pltpu.VMEM)] *...]
    slice x0 -> x20, local copies, waits for them, and re-layouts: none -> 31.2 us  [the longest x2 11.2 us: spread(): parts.append(whole[:, at:at + value.shape[-1]])]
    convert_element_type x2 -> x1, other arithmetic: 29 us -> 0.07 us  [shards(): b_point.astype(jnp.float32)]
    all_gather x2 -> x4, waiting for transfers between devices: 264 us -> 237 us  [the longest x1 235 us: gather_weights(): whole = lax.all_gather(shard_low, ('seq', 'dp'), axis=0, tiled=True)]
    reduce_scatter x1, waiting for transfers between devices: 24.2 us -> 0.01 us  [shards(): lax.psum_scatter(grad_keyval_part.astype(jnp.bfloat16), 'seq', scatter_di...]
    add x2 -> x0, other arithmetic: 22.4 us -> none  [the longest x1 22.4 us: shards(): first_hat / (jnp.sqrt(second_hat) + adam_eps) + weight_decay * params]
  transfers between devices with their start and end apart: 13 -> 14, of which waited for: 6 -> 7; matrix products, arithmetic and copies ran while one was open for 10% -> 20% of each run, Pallas kernels for 5% -> 4%
where the time goes in v2:
time: 1060 us; the launch traced here: 1050 us
  waiting for transfers between devices  452 us (43%)
  Pallas kernels  188 us (18%)
  local copies, waits for them, and re-layouts  152 us (14%)
  matrix products  117 us (11%)
  other arithmetic  89.9 us (8%)
  starting transfers between devices  34.4 us (3%)
  between operations  16.6 us (2%)
    all_gather x1, waiting for transfers between devices, gather_weights(): whole = lax.all_gather(shard_low, ('seq', 'dp'), axis=0, tiled=True)  235 us
    reduce_scatter x1, waiting for transfers between devices, shards(): lax.psum_scatter(quarter_grad.reshape(count_dp, -1, LANE), 'dp', scatter_...  175 us
    pallas_call x7, Pallas kernels, read_matrix(): pl.pallas_call(kernel, grid=(rows_of // block,), in_specs=[pl.BlockSpec((...  81.7 us
    pallas_call x1, Pallas kernels, write_flat(): pl.pallas_call(kernel, in_specs=[pl.BlockSpec(memory_space=pl.ANY)] * len...  64.6 us
    unnamed x293, local copies, waits for them, and re-layouts  38.7 us
    dot_general x7, matrix products, outer_sum(): lax.dot_general(left_flat, right_flat, (((0,), (0,)), ((), ())), preferre...  34.7 us
    dot_general x7, matrix products, matmul(): return jnp.dot(left_op, right_op, preferred_element_type=jnp.float32)  33.3 us
    all_to_all x3, waiting for transfers between devices, collect(): lax.all_to_all(blocks, 'seq', split_axis=0, concat_axis=0, tiled=True)  31.3 us
  transfers between devices with their start and end apart: 14, of which 7 were waited for; matrix products, arithmetic and copies ran while one was open for 20% of the time, Pallas kernels for 4%

profile of v2, /device:TPU:0, one launch (start us, length us, event | category | flops | bytes accessed | tf_op | source)
XLA Modules:
  0.0 1049.7 jit_solution(480880699462122930)
XLA Ops:
  11.0 234.7 %all-gather.8.cloned.1.call-done = bf16[161280,128]{1,0:T(8,128)(2,1)} async-done(((bf16[5040,128]{1,0:T(8,128)(2,1)}), bf16[161280,128]{1,0:T(8,128)(2,1)}) %all-gather.8.cloned.1.call-update) | async-done | bytes 41287696 | tf_op jit(solution)/shard_map/all_gather | solution.py:367
  247.1 6.9 read_matrix.11
  254.0 6.9 read_matrix.10
  262.5 6.9 read_matrix.8
  270.9 10.3 read_matrix.9
  281.2 14.1 %read_matrix.7 = bf16[1152,3456]{1,0:T(8,128)(2,1)} custom-call(bf16[4,40320,128]{2,1,0:T(8,128)(2,1)} %bitcast.422), custom_call_target="tpu_custom_call" | custom-call | bytes 15925248 | tf_op jit(solution)/shard_map/read_matrix/pallas_call | solution.py:142
  297.6 5.8 convolution_bitcast_fusion
  315.0 10.3 seq_sum.2
  371.9 18.0 %read_matrix.13 = bf16[2880,1152]{1,0:T(8,128)(2,1)} custom-call(bf16[4,40320,128]{2,1,0:T(8,128)(2,1)} %bitcast.423), custom_call_target="tpu_custom_call" | custom-call | bytes 13271040 | tf_op jit(solution)/shard_map/read_matrix/pallas_call | solution.py:142
  389.9 18.6 %read_matrix.12 = bf16[1152,5760]{1,0:T(8,128)(2,1)} custom-call(bf16[4,40320,128]{2,1,0:T(8,128)(2,1)} %bitcast.424), custom_call_target="tpu_custom_call" | custom-call | bytes 26542080 | tf_op jit(solution)/shard_map/read_matrix/pallas_call | solution.py:142
  428.5 12.4 %multiply_convert_fusion = (bf16[256,5760]{1,0:T(8,128)(2,1)S(1)}, f32[256,5760]{1,0:T(8,128)}) fusion(f32[5760]{0:T(1024)} %reshape.1349, bf16[1152,5760]{1,0:T(8,128)(2,1)} %read_matrix.12, f32[256,1152]{1,0:T(8,128)} %get-tuple-element.158, f32[1152]{0:T(1024)} %get-tuple-element.74, f32[1152]{0:T(1024)} %copy-done.99, f32[256]{0:T(256)} %copy-done.122, ...), kind=kOutput, calls=%fused_computation.27 | convolution fusion | flops 3407708160 | bytes 23332352 | tf_op jit(solution)/shard_map/dot_general | solution.py:598
  449.1 6.1 add_add_fusion
  472.9 6.3 fusion.96
  479.2 5.2 convolution_bitcast_fusion.1
  488.2 5.7 fusion.20
  500.7 16.0 %fusion.8 = (bf16[5760]{0:T(1024)(128)(2,1)S(1)}, bf16[5760]{0:T(1024)(128)(2,1)S(1)}, bf16[5760]{0:T(1024)(128)(2,1)S(1)}, bf16[5760]{0:T(1024)(128)(2,1)S(1)},...) fusion(bf16[1,1,32,5760]{3,2,1,0:T(8,128)(2,1)} %copy-done.44, ...), kind=kLoop, calls=%fused_computation.21 | loop fusion | flops 58930560 | bytes 27383040 | tf_op jit(solution)/shard_map/lrcf,lrcf->f/dot_general | solution.py:780
  520.9 14.8 %collective-permute-start.2 = (bf16[1,1,32,5760]{3,2,1,0:T(8,128)(2,1)}, bf16[1,1,32,5760]{3,2,1,0:T(8,128)(2,1)}, u32[]{:S(2)}, u32[]{:S(2)}) collective-permute-start(bf16[1,1,32,5760]{3,2,1,0:T(8,128)(2,1)} %get-tuple-element.112), channel_id=1, source_target_pairs={{0,1},{1,2},{2,3},{4,5},{5,6},{6,7},{8,9},{9,10},{10,11},{12,13},{... | collective-permute-start | bytes 1105928 | tf_op jit(solution)/shard_map/ppermute | solution.py:30
  547.4 7.0 multiply_add_fusion
  558.0 10.9 %multiply_reduce_fusion.2 = (bf16[1152]{0:T(1024)(128)(2,1)}, f32[256]{0:T(256)S(1)}, f32[256]{0:T(256)S(1)}, bf16[1152]{0:T(1024)(128)(2,1)}, f32[256,1152]{1,0:T(8,128)S(1)}) fusion(f32[256,1152]{1,0:T(8,128)} %get-tuple-element.158, f32[256]{0:T(256)} %copy-done.122, f32[256]{0:T(256)S(1)} %broadcast_multiply_fusion.5, f32[1152]{0:T(1024)} %copy-done.99, ...), kind=kOutput, calls=%fused_computation.127 | convolution fusion | flops 3400037888 | bytes 18592768 | tf_op jit(solution)/shard_map/dot_general | solution.py:602
  581.4 5.9 copy.121
  619.0 23.9 %all-to-all-done = bf16[4,256,1728]{1,2,0:T(8,128)(2,1)} async-done(((bf16[4,256,1728]{1,2,0:T(8,128)(2,1)}), bf16[4,256,1728]{1,2,0:T(8,128)(2,1)}, u32[]{:S(2)}, u32[]{:S(2)}) %all-to-all-start) | async-done | bytes 3538976 | tf_op jit(solution)/shard_map/all_to_all | solution.py:668
  642.9 6.2 copy.122
  651.2 5.3 slice.509
  660.4 6.9 seq_sum.3
  694.3 8.1 fusion.49.refs_6_
  703.9 6.4 fusion.14.refs_5_
  744.6 7.2 reduce-scatter.6.cloned.1.call-done
  754.7 7.5 all-to-all-done.2
  764.4 6.8 fusion.21.refs_0_
  771.2 64.6 %write_flat.1 = bf16[40320,128]{1,0:T(8,128)(2,1)} custom-call(f32[1152,896]{1,0:T(8,128)} %fusion.21.refs_0_, f32[1152,384]{1,0:T(8,128)} %fusion.55.refs_1_, f32[1152,384]{1,0:T(8,128)} %fusion.53.refs_2_, f32[1152,640]{1,0:T(8,128)} %convolution_bitcast_fusion.2.refs_3_, f32[1152,384]{1,0:T(8,128)} %fusion.51.refs_4_, f32[1152,1536]{1,0:T(8,128)} %fusion.14.refs_5_, ...), custom_call_target="tpu_custom_call" | custom-call | bytes 30965760 | tf_op jit(solution)/shard_map/write_flat/pallas_call | solution.py:332
  835.9 175.4 %reduce-scatter.8.cloned.1.call-done = bf16[1,5040,128]{2,1,0:T(8,128)(2,1)} async-done(((bf16[8,5040,128]{2,1,0:T(8,128)(2,1)}), bf16[1,5040,128]{2,1,0:T(8,128)(2,1)}) %reduce-scatter.8.cloned.1.call-update) | async-done | bytes 1290256 | tf_op jit(solution)/shard_map/reduce_scatter | solution.py:945
  1012.6 21.1 %finish.1 = (f32[5040,128]{1,0:T(8,128)S(1)}, f32[5040,128]{1,0:T(8,128)}, f32[5040,128]{1,0:T(8,128)}, f32[5040,128]{1,0:T(8,128)}, f32[32,128]{1,0:T(8,128)S(1)}) custom-call(bf16[5040,128]{1,0:T(8,128)(2,1)S(1)} %bitcast.414, f32[32,128]{1,0:T(8,128)S(1)} %pad_bitcast_fusion.1.bias_ref, f32[5040,128]{1,0:T(8,128)} %bitcast.445, f32[5040,128]{1,0:T(8,128)} %bitcast.477, ...), custom_call_target="tpu_custom_call" | custom-call | tf_op jit(solution)/shard_map/finish/pallas_call | solution.py:549
  (525 shorter events, 271.2 us)
Async XLA Ops:
  7.2 321.6 %copy-start = (bf16[1,300,1152]{2,1,0:T(8,128)(2,1)S(1)}, bf16[1,300,1152]{2,1,0:T(8,128)(2,1)}, u32[]{:S(2)}) copy-start(bf16[1,300,1152]{2,1,0:T(8,128)(2,1)} %param.8) | copy-start | bytes 2073604
  7.2 238.4 %all-gather.8.cloned.1.call-start = ((), (), s32[]{:S(2)}) async-start(), calls=%async_computation.6 | async-start | bytes 42577920 | tf_op jit(solution)/shard_map/all_gather | solution.py:367
  10.3 455.5 %all-gather.12.cloned.1.call-start = ((), (), s32[]{:S(2)}) async-start(), calls=%async_computation.11 | async-start | bytes 5898240 | tf_op jit(solution)/shard_map/all_gather | solution.py:645
  10.6 285.7 %copy-start.111 = (f32[256]{0:T(256)}, f32[256]{0:T(256)S(1)}, u32[]{:S(2)}) copy-start(f32[256]{0:T(256)S(1)} %div.64) | copy-start | bytes 3076
  11.0 285.3 %copy-start.118 = (f32[256]{0:T(256)}, f32[256]{0:T(256)S(1)}, u32[]{:S(2)}) copy-start(f32[256]{0:T(256)S(1)} %add_rsqrt_fusion.1) | copy-start | bytes 3076
  296.2 54.4 %copy-start.97 = (f32[1152]{0:T(1024)}, f32[1152]{0:T(1024)S(1)}, u32[]{:S(2)}) copy-start(f32[1152]{0:T(1024)S(1)} %get-tuple-element.78) | copy-start | bytes 13828
  296.2 73.0 %copy-start.99 = (f32[1152]{0:T(1024)}, f32[1152]{0:T(1024)S(1)}, u32[]{:S(2)}) copy-start(f32[1152]{0:T(1024)S(1)} %get-tuple-element.75) | copy-start | bytes 13828
  296.2 119.1 %copy-start.94 = (f32[1152]{0:T(1024)}, f32[1152]{0:T(1024)S(1)}, u32[]{:S(2)}) copy-start(f32[1152]{0:T(1024)S(1)} %get-tuple-element.77) | copy-start | bytes 13828
  369.2 20.7 %copy-start.122 = (f32[256]{0:T(256)}, f32[256]{0:T(256)S(1)}, u32[]{:S(2)}) copy-start(f32[256]{0:T(256)S(1)} %add_rsqrt_fusion) | copy-start | bytes 3076
  371.9 101.0 %all-gather.10.cloned.1.call-start = ((), (), s32[]{:S(2)}) async-start(), calls=%async_computation.10 | async-start | bytes 8847360 | tf_op jit(solution)/shard_map/all_gather | solution.py:645
  389.9 19.3 %copy-start.121 = (bf16[4,384]{1,0:T(4,128)(2,1)S(1)}, bf16[4,384]{1,0:T(4,128)(2,1)}, u32[]{:S(2)}) copy-start(bf16[4,384]{1,0:T(4,128)(2,1)} %get-tuple-element.165) | copy-start | bytes 9220
  389.9 25.5 %copy-start.112 = (f32[256]{0:T(256)S(1)}, f32[256]{0:T(256)}, u32[]{:S(2)}) copy-start(f32[256]{0:T(256)} %copy-done.111) | copy-start | bytes 3076
  389.9 25.4 %copy-start.119 = (f32[256]{0:T(256)S(1)}, f32[256]{0:T(256)}, u32[]{:S(2)}) copy-start(f32[256]{0:T(256)} %copy-done.118) | copy-start | bytes 3076
  419.3 138.7 %all-gather.14.cloned.1.call-start = ((), (), s32[]{:S(2)}) async-start(), calls=%async_computation.12 | async-start | bytes 7372800 | tf_op jit(solution)/shard_map/all_gather | solution.py:645
  425.6 23.4 %copy-start.76 = (f32[5760]{0:T(1024)}, f32[5760]{0:T(1024)S(1)}, u32[]{:S(2)}) copy-start(f32[5760]{0:T(1024)S(1)} %mul.465) | copy-start | bytes 69124
  425.7 23.3 %copy-start.78 = (f32[5760]{0:T(1024)}, f32[5760]{0:T(1024)S(1)}, u32[]{:S(2)}) copy-start(f32[5760]{0:T(1024)S(1)} %mul.496) | copy-start | bytes 69124
  425.8 23.2 %copy-start.80 = (f32[5760]{0:T(1024)}, f32[5760]{0:T(1024)S(1)}, u32[]{:S(2)}) copy-start(f32[5760]{0:T(1024)S(1)} %mul.493) | copy-start | bytes 69124
  425.9 23.1 %copy-start.82 = (f32[5760]{0:T(1024)}, f32[5760]{0:T(1024)S(1)}, u32[]{:S(2)}) copy-start(f32[5760]{0:T(1024)S(1)} %mul.490) | copy-start | bytes 69124
  426.0 23.1 %copy-start.84 = (f32[5760]{0:T(1024)}, f32[5760]{0:T(1024)S(1)}, u32[]{:S(2)}) copy-start(f32[5760]{0:T(1024)S(1)} %mul.487) | copy-start | bytes 69124
  426.1 23.0 %copy-start.86 = (f32[5760]{0:T(1024)}, f32[5760]{0:T(1024)S(1)}, u32[]{:S(2)}) copy-start(f32[5760]{0:T(1024)S(1)} %mul.484) | copy-start | bytes 69124
  426.2 22.9 %copy-start.88 = (f32[5760]{0:T(1024)}, f32[5760]{0:T(1024)S(1)}, u32[]{:S(2)}) copy-start(f32[5760]{0:T(1024)S(1)} %mul.481) | copy-start | bytes 69124
  427.0 22.1 %copy-start.90 = (f32[5760]{0:T(1024)}, f32[5760]{0:T(1024)S(1)}, u32[]{:S(2)}) copy-start(f32[5760]{0:T(1024)S(1)} %mul.478) | copy-start | bytes 69124
  440.9 4.9 collective-permute-start
  443.6 3.8 collective-permute-start.1
  520.9 21.8 %collective-permute-start.2 = (bf16[1,1,32,5760]{3,2,1,0:T(8,128)(2,1)}, bf16[1,1,32,5760]{3,2,1,0:T(8,128)(2,1)}, u32[]{:S(2)}, u32[]{:S(2)}) collective-permute-start(bf16[1,1,32,5760]{3,2,1,0:T(8,128)(2,1)} %get-tuple-element.112), channel_id=1, source_target_pairs={{0,1},{1,2},{2,3},{4,5},{5,6},{6,7},{8,9},{9,10},{10,11},{12,13},{... | collective-permute-start | bytes 1105928 | tf_op jit(solution)/shard_map/ppermute | solution.py:30
  535.7 7.0 collective-permute-start.3
  587.3 55.6 %all-to-all-start = ((bf16[4,256,1728]{1,2,0:T(8,128)(2,1)}), bf16[4,256,1728]{1,2,0:T(8,128)(2,1)}, u32[]{:S(2)}, u32[]{:S(2)}) async-start(bf16[4,256,1728]{1,2,0:T(8,128)(2,1)} %copy.121), calls=%async_computation | async-start | bytes 7077888 | tf_op jit(solution)/shard_map/all_to_all | solution.py:668
  592.2 118.1 %reduce-scatter.4.cloned.1.call-start = ((), (), s32[]{:S(2)}) async-start(), calls=%async_computation.7 | async-start | bytes 2211840 | tf_op jit(solution)/shard_map/reduce_scatter | solution.py:828
  679.4 34.6 %all-to-all-start.1 = ((bf16[4,256,864]{1,2,0:T(8,128)(2,1)}), bf16[4,256,864]{1,2,0:T(8,128)(2,1)}, u32[]{:S(2)}, u32[]{:S(2)}) async-start(bf16[4,256,864]{1,2,0:T(8,128)(2,1)} %copy.133), calls=%async_computation.1 | async-start | bytes 3538944 | tf_op jit(solution)/shard_map/all_to_all | solution.py:668
  683.9 67.8 %reduce-scatter.6.cloned.1.call-start = ((), (), s32[]{:S(2)}) async-start(), calls=%async_computation.8 | async-start | bytes 163840 | tf_op jit(solution)/shard_map/reduce_scatter | solution.py:901
  735.7 26.4 %all-to-all-start.2 = ((bf16[4,256,864]{1,2,0:T(8,128)(2,1)}), bf16[4,256,864]{1,2,0:T(8,128)(2,1)S(1)}, u32[]{:S(2)}, u32[]{:S(2)}) async-start(bf16[4,256,864]{1,2,0:T(8,128)(2,1)} %copy.135), calls=%async_computation.2 | async-start | bytes 3538944 | tf_op jit(solution)/shard_map/all_to_all | solution.py:668
  739.3 272.0 %reduce-scatter.8.cloned.1.call-start = ((), (), s32[]{:S(2)}) async-start(), calls=%async_computation.9 | async-start | bytes 11612160 | tf_op jit(solution)/shard_map/reduce_scatter | solution.py:945
  (119 other events, 590.4 us)
Sparse Core Ops, SparseCore 0:
  11.6 234.0 all-gather.7
  372.0 36.0 all-gather.11
  419.5 53.4 all-gather.9
  488.2 55.5 all-gather.13
  602.6 40.5 reduce-scatter.3
  731.0 20.7 reduce-scatter.5
  835.9 175.3 reduce-scatter.7

commit v3 on v2

--- a/solution.py
+++ b/solution.py
@@ -99,7 +99,7 @@
                 ].astype(jnp.float32)
             return 0
 
-        lax.fori_loop(0, need // 16, widen, 0)
+        lax.fori_loop(0, need // 16, widen, 0, unroll=8)
         lane_unit = lax.broadcasted_iota(jnp.int32, (8, LANE), 1) // UNIT
 
         def group(at, _):
@@ -127,7 +127,7 @@
                     )
             return 0
 
-        lax.fori_loop(0, block // 32, group, 0)
+        lax.fori_loop(0, block // 32, group, 0, unroll=2)
 
         def narrow(at, _):
             row = pl.multiple_of(at * 16, 16)
@@ -137,7 +137,7 @@
                 ].astype(jnp.bfloat16)
             return 0
 
-        lax.fori_loop(0, block // 16, narrow, 0)
+        lax.fori_loop(0, block // 16, narrow, 0, unroll=2)
 
     return pl.pallas_call(
         kernel,
@@ -185,7 +185,7 @@
             small.append(padded)
         offset += length
     widths = sorted({place[3] for place in places if place[0]})
-    chunk = 1008
+    chunk = 144
 
     def kernel(*refs):
         big_refs = refs[: len(big)]
@@ -193,7 +193,7 @@
         out_ref = refs[len(big) + len(small)]
         flat = refs[len(big) + len(small) + 1]
         bufs = refs[len(big) + len(small) + 2 : len(big) + len(small) + 2 + len(widths)]
-        out_buf, in_sem, out_sem = refs[-3:]
+        in_sem = refs[-1]
         lane_unit = lax.broadcasted_iota(jnp.int32, (8, LANE), 1) // UNIT
         row_unit = lax.broadcasted_iota(jnp.int32, (1, LANE), 1) // UNIT
 
@@ -223,6 +223,17 @@
                     else ref[count - 1 : count, :]
                 )
 
+        def fetch_block(ref, buf, width, at, slot):
+            row = pl.multiple_of(at * block_rows, 64)
+            return [
+                pltpu.make_async_copy(
+                    ref.at[pl.ds(row, block_rows), tile * LANE : (tile + 1) * LANE],
+                    buf.at[slot, tile],
+                    in_sem.at[widths.index(width), slot, tile],
+                )
+                for tile in range(-(-width // LANE))
+            ]
+
         def place_big(ref, buf, offset, rows_of, width):
             per_row = width // UNIT
             first = offset // LANE
@@ -230,21 +241,8 @@
             block = block_rows
             blocks = rows_of // block
 
-            tiles = -(-width // LANE)
-
             def fetch(at, slot):
-                row = pl.multiple_of(at * block, 64)
-                return [
-                    pltpu.make_async_copy(
-                        ref.at[pl.ds(row, block), tile * LANE : (tile + 1) * LANE],
-                        buf.at[slot, tile],
-                        in_sem.at[slot, tile],
-                    )
-                    for tile in range(tiles)
-                ]
-
-            for copy in fetch(0, 0):
-                copy.start()
+                return fetch_block(ref, buf, width, at, slot)
 
             def one_block(at, _):
                 slot = lax.rem(at, 2)
@@ -288,61 +286,47 @@
                         flat[where, :] = merge_units(parts, lane_unit)
                     return 0
 
-                lax.fori_loop(0, block // 32, group, 0)
+                lax.fori_loop(0, block // 32, group, 0, unroll=3)
                 return 0
 
             lax.fori_loop(0, blocks, one_block, 0)
 
+        def first_fetch(width, after):
+            for is_big, _, _, other, index in places:
+                if is_big and other == width and index > after:
+                    buf = bufs[widths.index(width)]
+                    for copy in fetch_block(big_refs[index], buf, width, 0, 0):
+                        copy.start()
+                    return
+
+        for width in widths:
+            first_fetch(width, -1)
         for is_big, offset, rows_of, width, index in places:
             if is_big:
                 place_big(big_refs[index], bufs[widths.index(width)], offset, rows_of, width)
+                first_fetch(width, index)
             else:
                 place_small(small_refs[index], offset, rows_of)
 
-        def emit(at, slot):
-            return pltpu.make_async_copy(
-                out_buf.at[slot],
-                out_ref.at[pl.ds(pl.multiple_of(at * chunk, 16), chunk), :],
-                out_sem.at[slot],
-            )
-
-        def one_chunk(at, _):
-            slot = lax.rem(at, 2)
-
-            @pl.when(at >= 2)
-            def _():
-                emit(at - 2, slot).wait()
-
-            def narrow(sub, _):
-                row = pl.multiple_of(sub * 16, 16)
-                out_buf[slot, pl.ds(row, 16), :] = flat[
-                    pl.ds(pl.multiple_of(at * chunk + row, 16), 16), :
-                ].astype(jnp.bfloat16)
-                return 0
-
-            lax.fori_loop(0, chunk // 16, narrow, 0, unroll=3)
-            emit(at, slot).start()
+        def narrow(at, _):
+            where = pl.ds(pl.multiple_of(at * chunk, 16), chunk)
+            out_ref[where, :] = flat[where, :].astype(jnp.bfloat16)
             return 0
 
-        chunks = flat_rows // chunk
-        lax.fori_loop(0, chunks, one_chunk, 0)
-        emit(chunks - 2, (chunks - 2) % 2).wait()
-        emit(chunks - 1, (chunks - 1) % 2).wait()
+        lax.fori_loop(0, flat_rows // chunk, narrow, 0)
 
     return pl.pallas_call(
         kernel,
         in_specs=[pl.BlockSpec(memory_space=pl.ANY)] * len(big)
         + [pl.BlockSpec(memory_space=pltpu.VMEM)] * len(small),
-        out_specs=pl.BlockSpec(memory_space=pl.ANY),
+        out_specs=pl.BlockSpec(memory_space=pltpu.VMEM),
         out_shape=jax.ShapeDtypeStruct((flat_rows, LANE), jnp.bfloat16),
         scratch_shapes=[pltpu.VMEM((flat_rows, LANE), jnp.float32)]
         + [
             pltpu.VMEM((2, -(-width // LANE), block_rows, LANE), jnp.float32) for width in widths
         ]
         + [
-            pltpu.VMEM((2, chunk, LANE), jnp.bfloat16),
-            pltpu.SemaphoreType.DMA((2, -(-widths[-1] // LANE))),
-            pltpu.SemaphoreType.DMA((2,)),
+            pltpu.SemaphoreType.DMA((len(widths), 2, -(-widths[-1] // LANE))),
         ],
         compiler_params=pltpu.CompilerParams(vmem_limit_bytes=56 << 20),
         cost_estimate=pl.CostEstimate(flops=0, bytes_accessed=6 * total, transcendentals=0),
@@ -473,6 +457,124 @@
         total[:split].reshape(state.shape),
         total[split:].reshape(-1)[: sums.size].reshape(1, heads, -1),
     )
+
+
+def reduce_shard(flat):
+    rows = flat.shape[0] // 8
+    pieces = 3
+    part = rows // pieces
+    step = 80
+
+    def kernel(in_ref, out_ref, recv_x, send_z, recv_z, x_send, x_recv, z_send, z_recv):
+        me = lax.axis_index("dp")
+        near = lax.rem(me, 2)
+        far = lax.div(me, 2)
+        partner = me + 1 - 2 * near
+
+        def far_of(shift):
+            return lax.rem(far + shift, 4)
+
+        barrier = pltpu.get_barrier_semaphore()
+        pl.semaphore_signal(barrier, inc=1, device_id={"dp": partner}, device_id_type=MESH)
+        for shift in range(1, 4):
+            pl.semaphore_signal(
+                barrier,
+                inc=1,
+                device_id={"dp": 2 * far_of(shift) + near},
+                device_id_type=MESH,
+            )
+        pl.semaphore_wait(barrier, 4)
+
+        def window(shard, piece):
+            return pl.ds(pl.multiple_of(shard * rows + piece * part, 16), part)
+
+        def x_copy(shift, piece):
+            return pltpu.make_async_remote_copy(
+                src_ref=in_ref.at[window(2 * far_of(shift) + 1 - near, piece), :],
+                dst_ref=recv_x.at[shift, pl.ds(piece * part, part), :],
+                send_sem=x_send.at[shift, piece],
+                recv_sem=x_recv.at[shift, piece],
+                device_id={"dp": partner},
+                device_id_type=MESH,
+            )
+
+        def z_copy(shift, piece):
+            return pltpu.make_async_remote_copy(
+                src_ref=send_z.at[shift - 1, pl.ds(piece * part, part), :],
+                dst_ref=recv_z.at[shift - 1, pl.ds(piece * part, part), :],
+                send_sem=z_send.at[shift - 1, piece],
+                recv_sem=z_recv.at[shift - 1, piece],
+                device_id={"dp": 2 * far_of(shift) + near},
+                device_id_type=MESH,
+            )
+
+        order = (1, 2, 3, 0)
+        for shift in order:
+            for piece in range(pieces):
+                x_copy(shift, piece).start()
+
+        def own_sum(shift, row, at):
+            start = (2 * far_of(shift) + near) * rows + row + at * step
+            own = in_ref[pl.ds(pl.multiple_of(start, 16), step), :]
+            other = recv_x[shift, pl.ds(pl.multiple_of(row + at * step, 16), step), :]
+            return own.astype(jnp.float32) + other.astype(jnp.float32)
+
+        for shift in order:
+            for piece in range(pieces):
+                x_copy(shift, piece).wait_recv()
+                row = piece * part
+
+                def add(at, _, shift=shift, row=row):
+                    where = pl.ds(pl.multiple_of(row + at * step, 16), step)
+                    total = own_sum(shift, row, at)
+                    if shift:
+                        send_z[shift - 1, where, :] = total.astype(jnp.bfloat16)
+                    else:
+                        out_ref[where, :] = total
+                    return 0
+
+                lax.fori_loop(0, part // step, add, 0)
+                if shift:
+                    z_copy(shift, piece).start()
+        for shift in range(1, 4):
+            for piece in range(pieces):
+                z_copy(shift, piece).wait_recv()
+                row = piece * part
+
+                def gather(at, _, shift=shift, row=row):
+                    where = pl.ds(pl.multiple_of(row + at * step, 16), step)
+                    out_ref[where, :] = out_ref[where, :] + recv_z[shift - 1, where, :].astype(
+                        jnp.float32
+                    )
+                    return 0
+
+                lax.fori_loop(0, part // step, gather, 0)
+        for shift in range(4):
+            for piece in range(pieces):
+                x_copy(shift, piece).wait_send()
+                if shift:
+                    z_copy(shift, piece).wait_send()
+
+    block = (rows, LANE)
+    return pl.pallas_call(
+        kernel,
+        in_specs=[pl.BlockSpec(memory_space=pltpu.VMEM)],
+        out_specs=pl.BlockSpec(memory_space=pltpu.VMEM),
+        out_shape=jax.ShapeDtypeStruct(block, jnp.float32),
+        scratch_shapes=[
+            pltpu.VMEM((4,) + block, jnp.bfloat16),
+            pltpu.VMEM((3,) + block, jnp.bfloat16),
+            pltpu.VMEM((3,) + block, jnp.bfloat16),
+            pltpu.SemaphoreType.DMA((4, pieces)),
+            pltpu.SemaphoreType.DMA((4, pieces)),
+            pltpu.SemaphoreType.DMA((3, pieces)),
+            pltpu.SemaphoreType.DMA((3, pieces)),
+        ],
+        compiler_params=pltpu.CompilerParams(
+            collective_id=4, has_side_effects=True, vmem_limit_bytes=40 << 20
+        ),
+        name="reduce_shard",
+    )(flat)
 
 
 def finish(grad_shard, bias_part, params, moment_one, moment_two):
@@ -942,9 +1044,12 @@
             grad_b_point,
         ],
     )
-    grad_shard = lax.psum_scatter(
-        quarter_grad.reshape(count_dp, -1, LANE), "dp", scatter_dimension=0, tiled=True
-    ).reshape(-1, LANE)
+    if count_dp == 8 and quarter_grad.shape[0] % (8 * 240) == 0:
+        grad_shard = reduce_shard(quarter_grad)
+    else:
+        grad_shard = lax.psum_scatter(
+            quarter_grad.reshape(count_dp, -1, LANE), "dp", scatter_dimension=0, tiled=True
+        ).reshape(-1, LANE)
     *flat_outs, bias_grads = finish(
         grad_shard,
         bias_part,

time: 1060 us -> 980 us (0.925)
  waiting for transfers between devices: 452 us -> 278 us
  Pallas kernels: 188 us -> 277 us
    reduce_scatter x1 -> x0, waiting for transfers between devices: 175 us -> none  [shards(): lax.psum_scatter(quarter_grad.reshape(count_dp, -1, LANE), 'dp', scatter_...]
    pallas_call x0 -> x1, Pallas kernels: none -> 125 us  [reduce_shard(): pl.pallas_call(kernel, in_specs=[pl.BlockSpec(memory_space=pltpu.VMEM)],...]
    pallas_call x1, Pallas kernels: 64.6 us -> 43.4 us  [write_flat(): pl.pallas_call(kernel, in_specs=[pl.BlockSpec(memory_space=pl.ANY)] * len...]
    pallas_call x7, Pallas kernels: 81.7 us -> 67.8 us  [read_matrix(): pl.pallas_call(kernel, grid=(rows_of // block,), in_specs=[pl.BlockSpec((...]
    unnamed x293 -> x297, local copies, waits for them, and re-layouts: 38.7 us -> 42.7 us
  transfers between devices with their start and end apart: 14 -> 13, of which waited for: 7 -> 6; matrix products, arithmetic and copies ran while one was open for 20% -> 21% of each run, Pallas kernels for 4% -> 4%
where the time goes in v3:
time: 980 us; the launch traced here: 969 us
  waiting for transfers between devices  278 us (28%)
  Pallas kernels  277 us (28%)
  local copies, waits for them, and re-layouts  157 us (16%)
  matrix products  117 us (12%)
  other arithmetic  89.7 us (9%)
  starting transfers between devices  34.4 us (4%)
  between operations  16.6 us (2%)
    all_gather x1, waiting for transfers between devices, gather_weights(): whole = lax.all_gather(shard_low, ('seq', 'dp'), axis=0, tiled=True)  235 us
    pallas_call x1, Pallas kernels, reduce_shard(): pl.pallas_call(kernel, in_specs=[pl.BlockSpec(memory_space=pltpu.VMEM)],...  125 us
    pallas_call x7, Pallas kernels, read_matrix(): pl.pallas_call(kernel, grid=(rows_of // block,), in_specs=[pl.BlockSpec((...  67.8 us
    pallas_call x1, Pallas kernels, write_flat(): pl.pallas_call(kernel, in_specs=[pl.BlockSpec(memory_space=pl.ANY)] * len...  43.4 us
    unnamed x297, local copies, waits for them, and re-layouts  42.7 us
    dot_general x7, matrix products, outer_sum(): lax.dot_general(left_flat, right_flat, (((0,), (0,)), ((), ())), preferre...  34.5 us
    dot_general x7, matrix products, matmul(): return jnp.dot(left_op, right_op, preferred_element_type=jnp.float32)  33.3 us
    all_to_all x3, waiting for transfers between devices, collect(): lax.all_to_all(blocks, 'seq', split_axis=0, concat_axis=0, tiled=True)  31.3 us
  transfers between devices with their start and end apart: 13, of which 6 were waited for; matrix products, arithmetic and copies ran while one was open for 21% of the time, Pallas kernels for 4%

profile of v3, /device:TPU:0, one launch (start us, length us, event | category | flops | bytes accessed | tf_op | source)
XLA Modules:
  0.0 968.8 jit_solution(4794234641371562342)
XLA Ops:
  11.0 234.7 %all-gather.8.cloned.1.call-done = bf16[161280,128]{1,0:T(8,128)(2,1)} async-done(((bf16[5040,128]{1,0:T(8,128)(2,1)}), bf16[161280,128]{1,0:T(8,128)(2,1)}) %all-gather.8.cloned.1.call-update) | async-done | bytes 41287696 | tf_op jit(solution)/shard_map/all_gather | solution.py:351
  247.1 5.6 read_matrix.11
  252.8 5.6 read_matrix.10
  259.9 5.6 read_matrix.8
  267.1 8.0 read_matrix.9
  275.1 12.2 %read_matrix.7 = bf16[1152,3456]{1,0:T(8,128)(2,1)} custom-call(bf16[4,40320,128]{2,1,0:T(8,128)(2,1)} %bitcast.420), custom_call_target="tpu_custom_call" | custom-call | bytes 15925248 | tf_op jit(solution)/shard_map/read_matrix/pallas_call | solution.py:142
  289.5 5.8 convolution_bitcast_fusion
  307.0 10.3 %seq_sum.2 = f32[304,128]{1,0:T(8,128)} custom-call(f32[304,128]{1,0:T(8,128)} %select_maximum_fusion.4.in_ref), custom_call_target="tpu_custom_call" | custom-call | tf_op jit(solution)/shard_map/seq_sum/pallas_call | solution.py:432
  363.8 15.3 %read_matrix.13 = bf16[2880,1152]{1,0:T(8,128)(2,1)} custom-call(bf16[4,40320,128]{2,1,0:T(8,128)(2,1)} %bitcast.421), custom_call_target="tpu_custom_call" | custom-call | bytes 13271040 | tf_op jit(solution)/shard_map/read_matrix/pallas_call | solution.py:142
  379.1 15.5 %read_matrix.12 = bf16[1152,5760]{1,0:T(8,128)(2,1)} custom-call(bf16[4,40320,128]{2,1,0:T(8,128)(2,1)} %bitcast.422), custom_call_target="tpu_custom_call" | custom-call | bytes 26542080 | tf_op jit(solution)/shard_map/read_matrix/pallas_call | solution.py:142
  414.7 12.4 %multiply_convert_fusion = (bf16[256,5760]{1,0:T(8,128)(2,1)S(1)}, f32[256,5760]{1,0:T(8,128)}) fusion(f32[5760]{0:T(1024)} %reshape.1341, bf16[1152,5760]{1,0:T(8,128)(2,1)} %read_matrix.12, f32[256,1152]{1,0:T(8,128)} %get-tuple-element.158, f32[1152]{0:T(1024)} %get-tuple-element.74, f32[1152]{0:T(1024)} %copy-done.99, f32[256]{0:T(256)} %copy-done.124, ...), kind=kOutput, calls=%fused_computation.27 | convolution fusion | flops 3407708160 | bytes 23332352 | tf_op jit(solution)/shard_map/dot_general | solution.py:700
  435.4 6.1 add_add_fusion
  459.1 6.3 fusion.96
  465.4 5.1 convolution_bitcast_fusion.1
  474.4 5.7 fusion.20
  486.9 15.6 %fusion.8 = (bf16[5760]{0:T(1024)(128)(2,1)S(1)}, bf16[5760]{0:T(1024)(128)(2,1)S(1)}, bf16[5760]{0:T(1024)(128)(2,1)S(1)}, bf16[5760]{0:T(1024)(128)(2,1)S(1)},...) fusion(bf16[1,1,32,5760]{3,2,1,0:T(8,128)(2,1)} %copy-done.45, ...), kind=kLoop, calls=%fused_computation.21 | loop fusion | flops 58930560 | bytes 27383040 | tf_op jit(solution)/shard_map/lrcf,lrcf->f/dot_general | solution.py:882
  506.8 14.8 %collective-permute-start.2 = (bf16[1,1,32,5760]{3,2,1,0:T(8,128)(2,1)}, bf16[1,1,32,5760]{3,2,1,0:T(8,128)(2,1)}, u32[]{:S(2)}, u32[]{:S(2)}) collective-permute-start(bf16[1,1,32,5760]{3,2,1,0:T(8,128)(2,1)} %get-tuple-element.112), channel_id=1, source_target_pairs={{0,1},{1,2},{2,3},{4,5},{5,6},{6,7},{8,9},{9,10},{10,11},{12,13},{... | collective-permute-start | bytes 1105928 | tf_op jit(solution)/shard_map/ppermute | solution.py:30
  533.4 7.0 multiply_add_fusion
  544.1 10.9 %multiply_reduce_fusion.2 = (bf16[1152]{0:T(1024)(128)(2,1)}, f32[256]{0:T(256)S(1)}, f32[256]{0:T(256)S(1)}, bf16[1152]{0:T(1024)(128)(2,1)}, f32[256,1152]{1,0:T(8,128)S(1)}) fusion(f32[256,1152]{1,0:T(8,128)} %get-tuple-element.158, f32[256]{0:T(256)} %copy-done.124, f32[256]{0:T(256)S(1)} %broadcast_multiply_fusion.5, f32[1152]{0:T(1024)} %copy-done.99, ...), kind=kOutput, calls=%fused_computation.127 | convolution fusion | flops 3400037888 | bytes 18592768 | tf_op jit(solution)/shard_map/dot_general | solution.py:704
  567.4 5.9 copy.121
  605.1 23.9 %all-to-all-done = bf16[4,256,1728]{1,2,0:T(8,128)(2,1)} async-done(((bf16[4,256,1728]{1,2,0:T(8,128)(2,1)}), bf16[4,256,1728]{1,2,0:T(8,128)(2,1)}, u32[]{:S(2)}, u32[]{:S(2)}) %all-to-all-start) | async-done | bytes 3538976 | tf_op jit(solution)/shard_map/all_to_all | solution.py:770
  628.9 6.2 copy.122
  637.3 5.3 slice.509
  646.5 6.9 seq_sum.3
  680.4 8.2 fusion.49.refs_6_
  690.0 6.2 fusion.14.refs_5_
  730.6 8.0 reduce-scatter.5.cloned.1.call-done
  741.5 7.4 all-to-all-done.2
  751.3 6.9 fusion.21.refs_0_
  758.1 43.4 %write_flat.1.in_ref = bf16[40320,128]{1,0:T(8,128)(2,1)} custom-call(f32[1152,896]{1,0:T(8,128)} %fusion.21.refs_0_, f32[1152,384]{1,0:T(8,128)} %fusion.55.refs_1_, f32[1152,384]{1,0:T(8,128)} %fusion.53.refs_2_, f32[1152,640]{1,0:T(8,128)} %convolution_bitcast_fusion.2.refs_3_, f32[1152,384]{1,0:T(8,128)} %fusion.51.refs_4_, ...), custom_call_target="tpu_custom_call" | custom-call | bytes 30965760 | tf_op jit(solution)/shard_map/write_flat/pallas_call | solution.py:318
  805.4 125.1 %reduce_shard.1.grad_ref = f32[5040,128]{1,0:T(8,128)S(1)} custom-call(bf16[40320,128]{1,0:T(8,128)(2,1)S(1)} %copy-done.1), custom_call_target="tpu_custom_call" | custom-call | tf_op jit(solution)/shard_map/reduce_shard/pallas_call | solution.py:559
  932.0 20.8 %finish.1 = (f32[5040,128]{1,0:T(8,128)S(1)}, f32[5040,128]{1,0:T(8,128)S(1)}, f32[5040,128]{1,0:T(8,128)}, f32[5040,128]{1,0:T(8,128)}, f32[32,128]{1,0:T(8,128)S(1)}) custom-call(f32[5040,128]{1,0:T(8,128)} %copy-done.5, f32[32,128]{1,0:T(8,128)S(1)} %pad_bitcast_fusion.1.bias_ref, f32[5040,128]{1,0:T(8,128)} %bitcast.442, f32[5040,128]{1,0:T(8,128)} %bitcast.471, ...), custom_call_target="tpu_custom_call" | custom-call | tf_op jit(solution)/shard_map/finish/pallas_call | solution.py:651
  (527 shorter events, 275.6 us)
Async XLA Ops:
  7.2 313.6 %copy-start = (bf16[1,300,1152]{2,1,0:T(8,128)(2,1)S(1)}, bf16[1,300,1152]{2,1,0:T(8,128)(2,1)}, u32[]{:S(2)}) copy-start(bf16[1,300,1152]{2,1,0:T(8,128)(2,1)} %param.8) | copy-start | bytes 2073604
  7.2 238.4 %all-gather.8.cloned.1.call-start = ((), (), s32[]{:S(2)}) async-start(), calls=%async_computation.5 | async-start | bytes 42577920 | tf_op jit(solution)/shard_map/all_gather | solution.py:351
  10.3 441.8 %all-gather.12.cloned.1.call-start = ((), (), s32[]{:S(2)}) async-start(), calls=%async_computation.9 | async-start | bytes 5898240 | tf_op jit(solution)/shard_map/all_gather | solution.py:747
  10.6 277.6 %copy-start.113 = (f32[256]{0:T(256)}, f32[256]{0:T(256)S(1)}, u32[]{:S(2)}) copy-start(f32[256]{0:T(256)S(1)} %div.64) | copy-start | bytes 3076
  11.0 277.2 %copy-start.120 = (f32[256]{0:T(256)}, f32[256]{0:T(256)S(1)}, u32[]{:S(2)}) copy-start(f32[256]{0:T(256)S(1)} %add_rsqrt_fusion.1) | copy-start | bytes 3076
  288.2 54.4 %copy-start.97 = (f32[1152]{0:T(1024)}, f32[1152]{0:T(1024)S(1)}, u32[]{:S(2)}) copy-start(f32[1152]{0:T(1024)S(1)} %get-tuple-element.78) | copy-start | bytes 13828
  288.2 72.9 %copy-start.99 = (f32[1152]{0:T(1024)}, f32[1152]{0:T(1024)S(1)}, u32[]{:S(2)}) copy-start(f32[1152]{0:T(1024)S(1)} %get-tuple-element.75) | copy-start | bytes 13828
  288.2 113.3 %copy-start.94 = (f32[1152]{0:T(1024)}, f32[1152]{0:T(1024)S(1)}, u32[]{:S(2)}) copy-start(f32[1152]{0:T(1024)S(1)} %get-tuple-element.77) | copy-start | bytes 13828
  363.8 95.3 %all-gather.10.cloned.1.call-start = ((), (), s32[]{:S(2)}) async-start(), calls=%async_computation.8 | async-start | bytes 8847360 | tf_op jit(solution)/shard_map/all_gather | solution.py:747
  379.1 22.3 %copy-start.114 = (f32[256]{0:T(256)S(1)}, f32[256]{0:T(256)}, u32[]{:S(2)}) copy-start(f32[256]{0:T(256)} %copy-done.113) | copy-start | bytes 3076
  379.1 22.3 %copy-start.121 = (f32[256]{0:T(256)S(1)}, f32[256]{0:T(256)}, u32[]{:S(2)}) copy-start(f32[256]{0:T(256)} %copy-done.120) | copy-start | bytes 3076
  405.4 138.6 %all-gather.14.cloned.1.call-start = ((), (), s32[]{:S(2)}) async-start(), calls=%async_computation.10 | async-start | bytes 7372800 | tf_op jit(solution)/shard_map/all_gather | solution.py:747
  411.8 23.4 %copy-start.76 = (f32[5760]{0:T(1024)}, f32[5760]{0:T(1024)S(1)}, u32[]{:S(2)}) copy-start(f32[5760]{0:T(1024)S(1)} %mul.465) | copy-start | bytes 69124
  411.9 23.4 %copy-start.78 = (f32[5760]{0:T(1024)}, f32[5760]{0:T(1024)S(1)}, u32[]{:S(2)}) copy-start(f32[5760]{0:T(1024)S(1)} %mul.496) | copy-start | bytes 69124
  412.0 23.3 %copy-start.80 = (f32[5760]{0:T(1024)}, f32[5760]{0:T(1024)S(1)}, u32[]{:S(2)}) copy-start(f32[5760]{0:T(1024)S(1)} %mul.493) | copy-start | bytes 69124
  412.1 23.2 %copy-start.82 = (f32[5760]{0:T(1024)}, f32[5760]{0:T(1024)S(1)}, u32[]{:S(2)}) copy-start(f32[5760]{0:T(1024)S(1)} %mul.490) | copy-start | bytes 69124
  412.2 23.1 %copy-start.84 = (f32[5760]{0:T(1024)}, f32[5760]{0:T(1024)S(1)}, u32[]{:S(2)}) copy-start(f32[5760]{0:T(1024)S(1)} %mul.487) | copy-start | bytes 69124
  412.3 23.0 %copy-start.86 = (f32[5760]{0:T(1024)}, f32[5760]{0:T(1024)S(1)}, u32[]{:S(2)}) copy-start(f32[5760]{0:T(1024)S(1)} %mul.484) | copy-start | bytes 69124
  412.4 22.9 %copy-start.88 = (f32[5760]{0:T(1024)}, f32[5760]{0:T(1024)S(1)}, u32[]{:S(2)}) copy-start(f32[5760]{0:T(1024)S(1)} %mul.481) | copy-start | bytes 69124
  413.2 22.1 %copy-start.90 = (f32[5760]{0:T(1024)}, f32[5760]{0:T(1024)S(1)}, u32[]{:S(2)}) copy-start(f32[5760]{0:T(1024)S(1)} %mul.478) | copy-start | bytes 69124
  427.1 4.9 collective-permute-start
  429.8 3.8 collective-permute-start.1
  504.3 18.6 %copy-start.16 = (bf16[1,256,2880]{2,1,0:T(8,128)(2,1)S(1)}, bf16[1,256,2880]{2,1,0:T(8,128)(2,1)}, u32[]{:S(2)}) copy-start(bf16[1,256,2880]{2,1,0:T(8,128)(2,1)} %copy.118) | copy-start | bytes 4423684
  504.3 18.6 %copy-start.17 = (bf16[1,256,2880]{2,1,0:T(8,128)(2,1)S(1)}, bf16[1,256,2880]{2,1,0:T(8,128)(2,1)}, u32[]{:S(2)}) copy-start(bf16[1,256,2880]{2,1,0:T(8,128)(2,1)} %copy.119) | copy-start | bytes 4423684
  506.8 21.9 %collective-permute-start.2 = (bf16[1,1,32,5760]{3,2,1,0:T(8,128)(2,1)}, bf16[1,1,32,5760]{3,2,1,0:T(8,128)(2,1)}, u32[]{:S(2)}, u32[]{:S(2)}) collective-permute-start(bf16[1,1,32,5760]{3,2,1,0:T(8,128)(2,1)} %get-tuple-element.112), channel_id=1, source_target_pairs={{0,1},{1,2},{2,3},{4,5},{5,6},{6,7},{8,9},{9,10},{10,11},{12,13},{... | collective-permute-start | bytes 1105928 | tf_op jit(solution)/shard_map/ppermute | solution.py:30
  521.6 7.0 collective-permute-start.3
  573.4 55.6 %all-to-all-start = ((bf16[4,256,1728]{1,2,0:T(8,128)(2,1)}), bf16[4,256,1728]{1,2,0:T(8,128)(2,1)}, u32[]{:S(2)}, u32[]{:S(2)}) async-start(bf16[4,256,1728]{1,2,0:T(8,128)(2,1)} %copy.121), calls=%async_computation | async-start | bytes 7077888 | tf_op jit(solution)/shard_map/all_to_all | solution.py:770
  578.3 118.0 %reduce-scatter.3.cloned.1.call-start = ((), (), s32[]{:S(2)}) async-start(), calls=%async_computation.6 | async-start | bytes 2211840 | tf_op jit(solution)/shard_map/reduce_scatter | solution.py:930
  658.8 30.7 %copy-start.103 = (f32[1440]{0:T(1024)}, f32[1440]{0:T(1024)S(1)}, u32[]{:S(2)}) copy-start(f32[1440]{0:T(1024)S(1)} %convert_reduce_fusion) | copy-start | bytes 17284
  665.5 34.4 %all-to-all-start.1 = ((bf16[4,256,864]{1,2,0:T(8,128)(2,1)}), bf16[4,256,864]{1,2,0:T(8,128)(2,1)}, u32[]{:S(2)}, u32[]{:S(2)}) async-start(bf16[4,256,864]{1,2,0:T(8,128)(2,1)} %copy.133), calls=%async_computation.1 | async-start | bytes 3538944 | tf_op jit(solution)/shard_map/all_to_all | solution.py:770
  670.1 68.5 %reduce-scatter.5.cloned.1.call-start = ((), (), s32[]{:S(2)}) async-start(), calls=%async_computation.7 | async-start | bytes 163840 | tf_op jit(solution)/shard_map/reduce_scatter | solution.py:1003
  722.3 26.7 %all-to-all-start.2 = ((bf16[4,256,864]{1,2,0:T(8,128)(2,1)}), bf16[4,256,864]{1,2,0:T(8,128)(2,1)S(1)}, u32[]{:S(2)}, u32[]{:S(2)}) async-start(bf16[4,256,864]{1,2,0:T(8,128)(2,1)} %copy.135), calls=%async_computation.2 | async-start | bytes 3538944 | tf_op jit(solution)/shard_map/all_to_all | solution.py:770
  (120 other events, 602.3 us)
Sparse Core Ops, SparseCore 0:
  11.6 234.0 all-gather.7
  363.9 36.0 all-gather.11
  405.5 53.5 all-gather.9
  474.4 55.6 all-gather.13
  588.7 40.5 reduce-scatter.2
  717.6 20.9 reduce-scatter.4

commit v4 on v3

--- a/solution.py
+++ b/solution.py
@@ -56,6 +56,7 @@
 
 LANE = 128
 UNIT = 32
+MESH = pl.DeviceIdType.MESH
 
 
 def merge_units(values, lane_unit):
@@ -334,6 +335,238 @@
     )(*big, *small)
 
 
+def gather_flat(shard):
+    rows = shard.shape[0]
+    first = (rows // 2 + 15) // 16 * 16
+    parts = ((0, first), (first, rows - first))
+
+    def kernel(
+        in_ref,
+        out_ref,
+        own_sem,
+        z_send,
+        z_recv,
+        x_send,
+        x_recv,
+        y_send,
+        y_recv,
+        d_send,
+        d_recv,
+        c_send,
+        c_recv,
+    ):
+        dp = lax.axis_index("dp")
+        seq = lax.axis_index("seq")
+        near, far = lax.rem(dp, 2), lax.div(dp, 2)
+        core, side = lax.rem(seq, 2), lax.div(seq, 2)
+
+        half = lax.div(far, 2)
+        place = far + half * (3 - 2 * far)
+        inner = far + 1 - 2 * half
+        outer = far - 1 + 2 * half
+
+        def dp_of(turn, flip):
+            at = place if turn == 0 else 1 - place if turn == 1 else turn
+            return 2 * (at + half * (3 - 2 * at)) + (1 - near if flip else near)
+
+        def seq_of(flip, other_core):
+            return 2 * (1 - side if flip else side) + (1 - core if other_core else core)
+
+        def region(seq_at, dp_at, part):
+            start, length = parts[part]
+            return out_ref.at[
+                seq_at, pl.ds(pl.multiple_of(dp_at * rows + start, 16), length), :
+            ]
+
+        def own_region(part):
+            start, length = parts[part]
+            return in_ref.at[pl.ds(start, length), :]
+
+        def column(turn, part):
+            return region(seq, dp_of(turn, False), part)
+
+        def source(turn, part):
+            return column(turn, part) if turn else own_region(part)
+
+        def remote(src, dst, send, recv, target):
+            return pltpu.make_async_remote_copy(
+                src_ref=src,
+                dst_ref=dst,
+                send_sem=send,
+                recv_sem=recv,
+                device_id=target,
+                device_id_type=MESH,
+            )
+
+        x_peer = {"dp": dp_of(0, True)}
+        y_peer = {"seq": seq_of(True, False)}
+        c_peer = {"seq": seq_of(False, True)}
+
+        def z_copy(kind, part):
+            turn = (0, 0, 1, 2, 3)[kind]
+            arrives = (place, 0, 2, 1, 2)[kind]
+            return remote(
+                source(turn, part),
+                column(turn, part),
+                z_send.at[kind, part],
+                z_recv.at[arrives, part],
+                {"dp": 2 * (inner if kind in (0, 2) else outer) + near},
+            )
+
+        def z_in(turn, part):
+            here = column(turn, part)
+            return remote(
+                here, here, z_send.at[0, part], z_recv.at[turn - 1, part], {"dp": 2 * inner + near}
+            )
+
+        def x_out(turn, part):
+            return remote(
+                source(turn, part),
+                column(turn, part),
+                x_send.at[turn, part],
+                x_recv.at[turn, part],
+                x_peer,
+            )
+
+        def x_in(turn, part):
+            here = region(seq, dp_of(turn, True), part)
+            return remote(here, here, x_send.at[turn, part], x_recv.at[turn, part], x_peer)
+
+        def y_out(turn, part):
+            return remote(
+                source(turn, part),
+                column(turn, part),
+                y_send.at[turn, part],
+                y_recv.at[turn, part],
+                y_peer,
+            )
+
+        def y_in(turn, part):
+            here = region(seq_of(True, False), dp_of(turn, False), part)
+            return remote(here, here, y_send.at[turn, part], y_recv.at[turn, part], y_peer)
+
+        def d_out(turn, part):
+            if part == 0:
+                here, target = region(seq, dp_of(turn, True), part), y_peer
+            else:
+                here, target = region(seq_of(True, False), dp_of(turn, False), part), x_peer
+            return remote(here, here, d_send.at[turn, part], d_recv.at[turn, part], target)
+
+        def d_in(turn, part):
+            here = region(seq_of(True, False), dp_of(turn, True), part)
+            target = y_peer if part == 0 else x_peer
+            return remote(here, here, d_send.at[turn, part], d_recv.at[turn, part], target)
+
+        def c_copy(kind, turn, part, incoming):
+            where = region(
+                seq_of(kind in (2, 3), incoming), dp_of(turn, kind in (1, 3)), part
+            )
+            src = own_region(part) if kind == 0 and turn == 0 else where
+            return remote(
+                src if not incoming else where,
+                where,
+                c_send.at[kind, turn, part],
+                c_recv.at[kind, turn, part],
+                c_peer,
+            )
+
+        barrier = pltpu.get_barrier_semaphore()
+        for target in (x_peer, y_peer, c_peer, {"dp": 2 * inner + near}):
+            pl.semaphore_signal(barrier, inc=1, device_id=target, device_id_type=MESH)
+
+        @pl.when(place == 1)
+        def _():
+            pl.semaphore_signal(
+                barrier, inc=1, device_id={"dp": 2 * outer + near}, device_id_type=MESH
+            )
+            pl.semaphore_wait(barrier, 5)
+
+        @pl.when(place == 0)
+        def _():
+            pl.semaphore_wait(barrier, 4)
+
+        keep = [
+            pltpu.make_async_copy(own_region(part), region(seq, dp, part), own_sem.at[part])
+            for part in range(2)
+        ]
+        def outwards(kind, part):
+            @pl.when(place == 1)
+            def _():
+                z_copy(kind, part).start()
+
+        for part in range(2):
+            z_copy(0, part).start()
+            outwards(1, part)
+            x_out(0, part).start()
+            y_out(0, part).start()
+        for part in range(2):
+            keep[part].start()
+            c_copy(0, 0, part, False).start()
+
+        def sideways(turn):
+            for part in range(2):
+                x_in(turn, part).wait_recv()
+                if part == 0:
+                    d_out(turn, part).start()
+                c_copy(1, turn, part, False).start()
+                y_in(turn, part).wait_recv()
+                if part == 1:
+                    d_out(turn, part).start()
+                c_copy(2, turn, part, False).start()
+
+        def diagonal(turn):
+            for part in range(2):
+                d_in(turn, part).wait_recv()
+                c_copy(3, turn, part, False).start()
+
+        for turn in range(1, 4):
+            for part in range(2):
+                z_in(turn, part).wait_recv()
+                outwards(turn + 1, part)
+                x_out(turn, part).start()
+                y_out(turn, part).start()
+                c_copy(0, turn, part, False).start()
+            sideways(turn - 1)
+            if turn > 1:
+                diagonal(turn - 2)
+        sideways(3)
+        diagonal(2)
+        diagonal(3)
+
+        @pl.when(place == 1)
+        def _():
+            for kind in range(1, 5):
+                for part in range(2):
+                    z_copy(kind, part).wait_send()
+
+        for part in range(2):
+            keep[part].wait()
+            z_copy(0, part).wait_send()
+            for turn in range(4):
+                x_out(turn, part).wait_send()
+                y_out(turn, part).wait_send()
+                d_out(turn, part).wait_send()
+                for kind in range(4):
+                    c_copy(kind, turn, part, False).wait_send()
+                    c_copy(kind, turn, part, True).wait_recv()
+
+    return pl.pallas_call(
+        kernel,
+        in_specs=[pl.BlockSpec(memory_space=pltpu.VMEM)],
+        out_specs=pl.BlockSpec(memory_space=pl.ANY),
+        out_shape=jax.ShapeDtypeStruct((4, 8 * rows, LANE), jnp.bfloat16),
+        scratch_shapes=[
+            pltpu.SemaphoreType.DMA((2,)),
+            pltpu.SemaphoreType.DMA((5, 2)),
+            pltpu.SemaphoreType.DMA((3, 2)),
+        ]
+        + [pltpu.SemaphoreType.DMA((4, 2))] * 6
+        + [pltpu.SemaphoreType.DMA((4, 4, 2))] * 2,
+        compiler_params=pltpu.CompilerParams(collective_id=5, has_side_effects=True),
+        name="gather_flat",
+    )(shard)
+
+
 def round_rows(values):
     def kernel(in_ref, out_ref):
         out_ref[...] = in_ref[...].astype(jnp.bfloat16)
@@ -348,8 +581,11 @@
 
 
 def gather_weights(shard_low, segs):
-    whole = lax.all_gather(shard_low, ("seq", "dp"), axis=0, tiled=True)
-    flat = whole.reshape(segs, -1, LANE)
+    if segs == 4 and lax.axis_size("dp") == 8 and shard_low.shape[0] % 16 == 0:
+        flat = gather_flat(shard_low)
+    else:
+        whole = lax.all_gather(shard_low, ("seq", "dp"), axis=0, tiled=True)
+        flat = whole.reshape(segs, -1, LANE)
     pieces = []
     offset = 0
     for rows_of, cols_of, vector in piece_specs():
@@ -364,9 +600,6 @@
             pieces.append(block.reshape(cols_of) if vector else block.reshape(rows_of, cols_of))
         offset = offset + length
     return pieces
-
-
-MESH = pl.DeviceIdType.MESH
 
 
 def peer_barrier(groups):
@@ -823,7 +1056,7 @@
     attended = to_low(attn_val.reshape(lat_dev, tokens_dev, D))
     branch_one = matmul(attended, w_attn_out) + b_attn_out.astype(jnp.float32)
     after_attn = tokens + gate_one * branch_one
-    after_low = to_low(after_attn)
+    after_low, x_qkv = lax.optimization_barrier((to_low(after_attn), *spread([hidden_one])))
     query_c = to_low(matmul(after_low, w_cross_q)).reshape(
         lat_dev, tokens_dev, CROSS_HEADS, cross_dim
     )
@@ -844,7 +1077,12 @@
     )
     after_cross = after_attn + matmul(cross_mixed, w_cross_out) + b_cross_out.astype(jnp.float32)
     normed_two, inverse_two = norm_parts(after_cross)
-    hidden_two = to_low(normed_two * (1.0 + scale_two) + shift_two)
+    hidden_two, x_attn, x_cross_q = lax.optimization_barrier(
+        (
+            to_low(normed_two * (1.0 + scale_two) + shift_two),
+            *spread([attended, after_low]),
+        )
+    )
     inner_pre = matmul(hidden_two, w_in) + b_in.astype(jnp.float32)
     active = to_low(jax.nn.silu(inner_pre)).reshape(lat_dev, row_dev, col_dev, 2 * FF)
     padded = jnp.pad(with_halo(active, (("seq", 1),), 1), ((0, 0), (0, 0), (1, 1), (0, 0)))
@@ -861,12 +1099,8 @@
     grad_out = cotangent.reshape(lat_dev, tokens_dev, D).astype(jnp.float32)
     grad_gate_two = jnp.sum(grad_out * branch_two, axis=1)
     grad_branch_two = to_low(grad_out * gate_two)
-    grad_branch_two, x_qkv, x_attn, x_cross_q, x_cross_out, x_inner = lax.optimization_barrier(
-        (
-            grad_branch_two,
-            *spread([hidden_one, attended, after_low]),
-            *spread([cross_mixed, hidden_two]),
-        )
+    grad_branch_two, x_cross_out, x_inner = lax.optimization_barrier(
+        (grad_branch_two, *spread([cross_mixed, hidden_two]))
     )
     grad_gated = matmul_t(grad_branch_two, w_point)
     grad_up = grad_gated * jax.nn.silu(gate_part)

time: 980 us -> 924 us (0.943)
  waiting for transfers between devices: 278 us -> 41.4 us
  Pallas kernels: 277 us -> 454 us
    all_gather x1 -> x0, waiting for transfers between devices: 235 us -> none  [gather_weights(): whole = lax.all_gather(shard_low, ('seq', 'dp'), axis=0, tiled=True)]
    pallas_call x0 -> x1, Pallas kernels: none -> 177 us  [gather_flat(): pl.pallas_call(kernel, in_specs=[pl.BlockSpec(memory_space=pltpu.VMEM)],...]
    unnamed x297 -> x283, local copies, waits for them, and re-layouts: 42.7 us -> 45.3 us
  transfers between devices with their start and end apart: 13 -> 13, of which waited for: 6 -> 4; matrix products, arithmetic and copies ran while one was open for 21% -> 29% of each run, Pallas kernels for 4% -> 9%
where the time goes in v4:
time: 924 us; the launch traced here: 912 us
  Pallas kernels  454 us (49%)
  local copies, waits for them, and re-layouts  159 us (17%)
  matrix products  122 us (13%)
  other arithmetic  89.8 us (10%)
  waiting for transfers between devices  41.4 us (4%)
  starting transfers between devices  28.9 us (3%)
  between operations  16.4 us (2%)
    pallas_call x1, Pallas kernels, gather_flat(): pl.pallas_call(kernel, in_specs=[pl.BlockSpec(memory_space=pltpu.VMEM)],...  177 us
    pallas_call x1, Pallas kernels, reduce_shard(): pl.pallas_call(kernel, in_specs=[pl.BlockSpec(memory_space=pltpu.VMEM)],...  126 us
    pallas_call x7, Pallas kernels, read_matrix(): pl.pallas_call(kernel, grid=(rows_of // block,), in_specs=[pl.BlockSpec((...  68 us
    unnamed x283, local copies, waits for them, and re-layouts  45.3 us
    pallas_call x1, Pallas kernels, write_flat(): pl.pallas_call(kernel, in_specs=[pl.BlockSpec(memory_space=pl.ANY)] * len...  43.4 us
    dot_general x7, matrix products, matmul(): return jnp.dot(left_op, right_op, preferred_element_type=jnp.float32)  36 us
    dot_general x7, matrix products, outer_sum(): lax.dot_general(left_flat, right_flat, (((0,), (0,)), ((), ())), preferre...  34.5 us
    all_to_all x3, waiting for transfers between devices, collect(): lax.all_to_all(blocks, 'seq', split_axis=0, concat_axis=0, tiled=True)  30 us
  transfers between devices with their start and end apart: 13, of which 4 were waited for; matrix products, arithmetic and copies ran while one was open for 29% of the time, Pallas kernels for 9%

profile of v4, /device:TPU:0, one launch (start us, length us, event | category | flops | bytes accessed | tf_op | source)
XLA Modules:
  0.0 911.9 jit_solution(3496211017527859241)
XLA Ops:
  13.7 176.7 %gather_flat.1.in_ref = bf16[4,40320,128]{2,1,0:T(8,128)(2,1)} custom-call(bf16[5040,128]{1,0:T(8,128)(2,1)} %round_rows.1.in_ref), custom_call_target="tpu_custom_call" | custom-call | tf_op jit(solution)/shard_map/gather_flat/pallas_call | solution.py:553
  193.8 5.6 read_matrix.8
  199.4 12.2 %read_matrix.7 = bf16[1152,3456]{1,0:T(8,128)(2,1)} custom-call(bf16[4,40320,128]{2,1,0:T(8,128)(2,1)} %gather_flat.1.in_ref), custom_call_target="tpu_custom_call" | custom-call | bytes 15925248 | tf_op jit(solution)/shard_map/read_matrix/pallas_call | solution.py:143
  211.6 5.8 convolution_bitcast_fusion
  231.6 9.3 %seq_sum.2 = f32[304,128]{1,0:T(8,128)} custom-call(f32[304,128]{1,0:T(8,128)} %select_maximum_fusion.4.in_ref), custom_call_target="tpu_custom_call" | custom-call | tf_op jit(solution)/shard_map/seq_sum/pallas_call | solution.py:665
  263.5 5.6 read_matrix.11
  269.1 5.8 read_matrix.10
  276.5 8.0 read_matrix.9
  319.3 5.0 fusion.95
  328.8 15.3 %read_matrix.13 = bf16[2880,1152]{1,0:T(8,128)(2,1)} custom-call(bf16[4,40320,128]{2,1,0:T(8,128)(2,1)} %gather_flat.1.in_ref), custom_call_target="tpu_custom_call" | custom-call | bytes 13271040 | tf_op jit(solution)/shard_map/read_matrix/pallas_call | solution.py:143
  344.1 15.5 %read_matrix.12 = bf16[1152,5760]{1,0:T(8,128)(2,1)} custom-call(bf16[4,40320,128]{2,1,0:T(8,128)(2,1)} %gather_flat.1.in_ref), custom_call_target="tpu_custom_call" | custom-call | bytes 26542080 | tf_op jit(solution)/shard_map/read_matrix/pallas_call | solution.py:143
  367.3 11.5 %multiply_convert_fusion = (bf16[256,5760]{1,0:T(8,128)(2,1)S(1)}, f32[256,5760]{1,0:T(8,128)}) fusion(f32[5760]{0:T(1024)} %reshape.1276, bf16[1152,5760]{1,0:T(8,128)(2,1)} %read_matrix.12, bf16[1,256,1152]{2,1,0:T(8,128)(2,1)} %fusion.55), kind=kOutput, calls=%fused_computation.27 | convolution fusion | flops 3406233600 | bytes 22731264 | tf_op jit(solution)/shard_map/dot_general | solution.py:933
  388.0 6.1 add_add_fusion
  409.6 5.2 convolution_bitcast_fusion.1
  418.7 5.7 fusion.20
  431.2 16.1 %fusion.8 = (bf16[5760]{0:T(1024)(128)(2,1)S(1)}, bf16[5760]{0:T(1024)(128)(2,1)S(1)}, bf16[5760]{0:T(1024)(128)(2,1)S(1)}, bf16[5760]{0:T(1024)(128)(2,1)S(1)},...) fusion(bf16[1,1,32,5760]{3,2,1,0:T(8,128)(2,1)} %copy-done.41, ...), kind=kLoop, calls=%fused_computation.21 | loop fusion | flops 58930560 | bytes 27383040 | tf_op jit(solution)/shard_map/lrcf,lrcf->f/dot_general | solution.py:1116
  451.6 8.0 collective-permute-start.2
  471.6 7.0 multiply_add_fusion
  482.2 10.9 %multiply_reduce_fusion.2 = (bf16[1152]{0:T(1024)(128)(2,1)}, f32[256]{0:T(256)S(1)}, f32[256]{0:T(256)S(1)}, bf16[1152]{0:T(1024)(128)(2,1)}, f32[256,1152]{1,0:T(8,128)S(1)}) fusion(f32[256,1152]{1,0:T(8,128)} %copy-done.11, f32[256]{0:T(256)} %copy-done.117, f32[256]{0:T(256)S(1)} %copy-done.114, f32[1152]{0:T(1024)} %copy-done.95, ...), kind=kOutput, calls=%fused_computation.123 | convolution fusion | flops 3400037888 | bytes 18592768 | tf_op jit(solution)/shard_map/dot_general | solution.py:937
  505.6 5.9 copy.121
  542.4 24.7 %all-to-all-done = bf16[4,256,1728]{1,2,0:T(8,128)(2,1)} async-done(((bf16[4,256,1728]{1,2,0:T(8,128)(2,1)}), bf16[4,256,1728]{1,2,0:T(8,128)(2,1)}, u32[]{:S(2)}, u32[]{:S(2)}) %all-to-all-start) | async-done | bytes 3538976 | tf_op jit(solution)/shard_map/all_to_all | solution.py:1003
  567.1 6.1 copy.122
  574.4 5.3 slice.497
  586.6 6.9 seq_sum.3
  623.8 8.1 fusion.45.refs_6_
  633.4 6.2 fusion.14.refs_5_
  673.0 10.2 %reduce-scatter.5.cloned.1.call-done = bf16[1,126,128]{2,1,0:T(8,128)(2,1)} async-done(((bf16[4,126,128]{2,1,0:T(8,128)(2,1)}), bf16[1,126,128]{2,1,0:T(8,128)(2,1)}) %reduce-scatter.5.cloned.1.call-update) | async-done | bytes 32272 | tf_op jit(solution)/shard_map/reduce_scatter | solution.py:1237
  686.2 5.3 all-to-all-done.2
  693.7 6.9 fusion.21.refs_0_
  700.6 43.4 %write_flat.1.in_ref = bf16[40320,128]{1,0:T(8,128)(2,1)} custom-call(f32[1152,896]{1,0:T(8,128)} %fusion.21.refs_0_, f32[1152,384]{1,0:T(8,128)} %fusion.51.refs_1_, f32[1152,384]{1,0:T(8,128)} %fusion.49.refs_2_, f32[1152,640]{1,0:T(8,128)} %convolution_bitcast_fusion.2.refs_3_, f32[1152,384]{1,0:T(8,128)} %fusion.47.refs_4_, ...), custom_call_target="tpu_custom_call" | custom-call | bytes 30965760 | tf_op jit(solution)/shard_map/write_flat/pallas_call | solution.py:319
  747.9 125.7 %reduce_shard.1.grad_ref = f32[5040,128]{1,0:T(8,128)S(1)} custom-call(bf16[40320,128]{1,0:T(8,128)(2,1)S(1)} %copy-done.1), custom_call_target="tpu_custom_call" | custom-call | tf_op jit(solution)/shard_map/reduce_shard/pallas_call | solution.py:792
  875.1 20.8 %finish.1 = (f32[5040,128]{1,0:T(8,128)S(1)}, f32[5040,128]{1,0:T(8,128)S(1)}, f32[5040,128]{1,0:T(8,128)}, f32[5040,128]{1,0:T(8,128)}, f32[32,128]{1,0:T(8,128)S(1)}) custom-call(f32[5040,128]{1,0:T(8,128)} %copy-done.4, f32[32,128]{1,0:T(8,128)S(1)} %pad_bitcast_fusion.1.bias_ref, f32[5040,128]{1,0:T(8,128)} %bitcast.430, f32[5040,128]{1,0:T(8,128)} %bitcast.459, ...), custom_call_target="tpu_custom_call" | custom-call | tf_op jit(solution)/shard_map/finish/pallas_call | solution.py:884
  (512 shorter events, 284.9 us)
Async XLA Ops:
  7.2 281.7 %copy-start = (bf16[1,300,1152]{2,1,0:T(8,128)(2,1)S(1)}, bf16[1,300,1152]{2,1,0:T(8,128)(2,1)}, u32[]{:S(2)}) copy-start(bf16[1,300,1152]{2,1,0:T(8,128)(2,1)} %param.8) | copy-start | bytes 2073604
  7.2 254.1 %all-gather.8.cloned.1.call-start = ((), (), s32[]{:S(2)}) async-start(), calls=%async_computation.5 | async-start | bytes 2949120 | tf_op jit(solution)/shard_map/all_gather | solution.py:980
  8.6 183.4 %copy-start.111 = (f32[256]{0:T(256)}, f32[256]{0:T(256)S(1)}, u32[]{:S(2)}) copy-start(f32[256]{0:T(256)S(1)} %div.64) | copy-start | bytes 3076
  10.0 182.0 %copy-start.115 = (f32[256]{0:T(256)}, f32[256]{0:T(256)S(1)}, u32[]{:S(2)}) copy-start(f32[256]{0:T(256)S(1)} %add_rsqrt_fusion.1) | copy-start | bytes 3076
  13.7 178.9 %copy-start.17 = (bf16[1,8,32,1152]{3,2,1,0:T(8,128)(2,1)S(1)}, bf16[1,8,32,1152]{3,2,1,0:T(8,128)(2,1)}, u32[]{:S(2)}) copy-start(bf16[1,8,32,1152]{3,2,1,0:T(8,128)(2,1)} %param.7) | copy-start | bytes 1769476
  192.0 67.1 %copy-start.93 = (f32[1152]{0:T(1024)}, f32[1152]{0:T(1024)S(1)}, u32[]{:S(2)}) copy-start(f32[1152]{0:T(1024)S(1)} %get-tuple-element.82) | copy-start | bytes 13828
  192.0 125.4 %copy-start.95 = (f32[1152]{0:T(1024)}, f32[1152]{0:T(1024)S(1)}, u32[]{:S(2)}) copy-start(f32[1152]{0:T(1024)S(1)} %get-tuple-element.79) | copy-start | bytes 13828
  193.7 125.6 %all-gather.10.cloned.1.call-start = ((), (), s32[]{:S(2)}) async-start(), calls=%async_computation.8 | async-start | bytes 5898240 | tf_op jit(solution)/shard_map/all_gather | solution.py:980
  199.4 57.5 %copy-start.6 = (bf16[1152,1152]{1,0:T(8,128)(2,1)}, bf16[1152,1152]{1,0:T(8,128)(2,1)S(1)}, u32[]{:S(2)}) copy-start(bf16[1152,1152]{1,0:T(8,128)(2,1)S(1)} %read_matrix.8) | copy-start | bytes 7962628
  262.5 142.2 %all-gather.12.cloned.1.call-start = ((), (), s32[]{:S(2)}) async-start(), calls=%async_computation.9 | async-start | bytes 5898240 | tf_op jit(solution)/shard_map/all_gather | solution.py:980
  325.4 156.7 %all-gather.14.cloned.1.call-start = ((), (), s32[]{:S(2)}) async-start(), calls=%async_computation.10 | async-start | bytes 7372800 | tf_op jit(solution)/shard_map/all_gather | solution.py:980
  364.5 23.4 %copy-start.71 = (f32[5760]{0:T(1024)}, f32[5760]{0:T(1024)S(1)}, u32[]{:S(2)}) copy-start(f32[5760]{0:T(1024)S(1)} %mul.447) | copy-start | bytes 69124
  364.6 23.3 %copy-start.73 = (f32[5760]{0:T(1024)}, f32[5760]{0:T(1024)S(1)}, u32[]{:S(2)}) copy-start(f32[5760]{0:T(1024)S(1)} %mul.478) | copy-start | bytes 69124
  364.6 23.2 %copy-start.75 = (f32[5760]{0:T(1024)}, f32[5760]{0:T(1024)S(1)}, u32[]{:S(2)}) copy-start(f32[5760]{0:T(1024)S(1)} %mul.475) | copy-start | bytes 69124
  364.7 23.2 %copy-start.77 = (f32[5760]{0:T(1024)}, f32[5760]{0:T(1024)S(1)}, u32[]{:S(2)}) copy-start(f32[5760]{0:T(1024)S(1)} %mul.472) | copy-start | bytes 69124
  364.8 23.1 %copy-start.79 = (f32[5760]{0:T(1024)}, f32[5760]{0:T(1024)S(1)}, u32[]{:S(2)}) copy-start(f32[5760]{0:T(1024)S(1)} %mul.469) | copy-start | bytes 69124
  364.9 23.0 %copy-start.81 = (f32[5760]{0:T(1024)}, f32[5760]{0:T(1024)S(1)}, u32[]{:S(2)}) copy-start(f32[5760]{0:T(1024)S(1)} %mul.466) | copy-start | bytes 69124
  365.0 22.9 %copy-start.83 = (f32[5760]{0:T(1024)}, f32[5760]{0:T(1024)S(1)}, u32[]{:S(2)}) copy-start(f32[5760]{0:T(1024)S(1)} %mul.463) | copy-start | bytes 69124
  365.9 22.1 %copy-start.85 = (f32[5760]{0:T(1024)}, f32[5760]{0:T(1024)S(1)}, u32[]{:S(2)}) copy-start(f32[5760]{0:T(1024)S(1)} %mul.460) | copy-start | bytes 69124
  367.3 16.8 %copy-start.33 = (bf16[1,8,32,1152]{3,2,1,0:T(8,128)(2,1)S(1)}, bf16[1,8,32,1152]{3,2,1,0:T(8,128)(2,1)}, u32[]{:S(2)}) copy-start(bf16[1,8,32,1152]{3,2,1,0:T(8,128)(2,1)} %param.10) | copy-start | bytes 1769476
  367.3 16.8 %copy-start.97 = (f32[1152]{0:T(1024)S(1)}, f32[1152]{0:T(1024)}, u32[]{:S(2)}) copy-start(f32[1152]{0:T(1024)} %get-tuple-element.77) | copy-start | bytes 13828
  378.9 6.2 collective-permute-start
  382.6 3.6 collective-permute-start.1
  451.6 14.9 %collective-permute-start.2 = (bf16[1,1,32,5760]{3,2,1,0:T(8,128)(2,1)}, bf16[1,1,32,5760]{3,2,1,0:T(8,128)(2,1)}, u32[]{:S(2)}, u32[]{:S(2)}) collective-permute-start(bf16[1,1,32,5760]{3,2,1,0:T(8,128)(2,1)} %get-tuple-element.115), channel_id=1, source_target_pairs={{0,1},{1,2},{2,3},{4,5},{5,6},{6,7},{8,9},{9,10},{10,11},{12,13},{... | collective-permute-start | bytes 1105928 | tf_op jit(solution)/shard_map/ppermute | solution.py:30
  459.6 7.0 collective-permute-start.3
  498.7 18.0 %copy-start.28 = (bf16[256,1152]{0,1:T(8,128)(2,1)}, bf16[256,1152]{0,1:T(8,128)(2,1)S(1)}, u32[]{:S(2)}) copy-start(bf16[256,1152]{0,1:T(8,128)(2,1)S(1)} %copy.120) | copy-start | bytes 1769476
  511.5 55.6 %all-to-all-start = ((bf16[4,256,1728]{1,2,0:T(8,128)(2,1)}), bf16[4,256,1728]{1,2,0:T(8,128)(2,1)}, u32[]{:S(2)}, u32[]{:S(2)}) async-start(bf16[4,256,1728]{1,2,0:T(8,128)(2,1)} %copy.121), calls=%async_computation | async-start | bytes 7077888 | tf_op jit(solution)/shard_map/all_to_all | solution.py:1003
  516.4 123.2 %reduce-scatter.3.cloned.1.call-start = ((), (), s32[]{:S(2)}) async-start(), calls=%async_computation.6 | async-start | bytes 2211840 | tf_op jit(solution)/shard_map/reduce_scatter | solution.py:1164
  609.5 33.8 %all-to-all-start.1 = ((bf16[4,256,864]{1,2,0:T(8,128)(2,1)}), bf16[4,256,864]{1,2,0:T(8,128)(2,1)}, u32[]{:S(2)}, u32[]{:S(2)}) async-start(bf16[4,256,864]{1,2,0:T(8,128)(2,1)} %copy.133), calls=%async_computation.1 | async-start | bytes 3538944 | tf_op jit(solution)/shard_map/all_to_all | solution.py:1003
  614.1 69.1 %reduce-scatter.5.cloned.1.call-start = ((), (), s32[]{:S(2)}) async-start(), calls=%async_computation.7 | async-start | bytes 163840 | tf_op jit(solution)/shard_map/reduce_scatter | solution.py:1237
  664.8 26.6 %all-to-all-start.2 = ((bf16[4,256,864]{1,2,0:T(8,128)(2,1)}), bf16[4,256,864]{1,2,0:T(8,128)(2,1)S(1)}, u32[]{:S(2)}, u32[]{:S(2)}) async-start(bf16[4,256,864]{1,2,0:T(8,128)(2,1)} %copy.135), calls=%async_computation.2 | async-start | bytes 3538944 | tf_op jit(solution)/shard_map/all_to_all | solution.py:1003
  668.6 17.0 %copy-start.122 = (pred[1,14,128]{2,1,0:T(8,128)(4,1)S(1)}, pred[1,14,128]{2,1,0:T(8,128)(4,1)}, u32[]{:S(2)}) copy-start(pred[1,14,128]{2,1,0:T(8,128)(4,1)} %constant.40.clone.1) | copy-start | bytes 5380
  (112 other events, 546.0 us)
Sparse Core Ops, SparseCore 0:
  193.8 24.2 all-gather.7
  262.6 39.0 all-gather.9
  325.6 39.0 all-gather.11
  418.7 50.2 all-gather.13
  526.8 40.5 reduce-scatter.2
  661.6 21.5 reduce-scatter.4

commit v5 on v4

--- a/solution.py
+++ b/solution.py
@@ -810,7 +810,7 @@
     )(flat)
 
 
-def finish(grad_shard, bias_part, params, moment_one, moment_two):
+def scale_of(grad_shard, bias_part):
     rows = grad_shard.shape[0]
     count_dp = lax.axis_size("dp")
     count_seq = lax.axis_size("seq")
@@ -821,13 +821,7 @@
     def kernel(
         grad_ref,
         bias_ref,
-        param_ref,
-        one_ref,
-        two_ref,
-        gradient_ref,
-        one_out,
-        two_out,
-        update_ref,
+        factor_out,
         bias_out,
         square,
         square_dp,
@@ -861,31 +855,17 @@
         factor = lax.rsqrt(whole / entries + 1e-06)
         exchange_wait("dp", count_dp, bias_ref, bias_slots, send_bias, recv_bias)
         bias_out[...] = in_order("dp", count_dp, bias_ref[...], bias_slots) * factor
-
-        def step(at, _):
-            where = pl.ds(at * chunk, chunk)
-            gradient = grad_ref[where, :].astype(jnp.float32) * factor
-            first = beta_first * one_ref[where, :] + (1.0 - beta_first) * gradient
-            second = beta_second * two_ref[where, :] + (1.0 - beta_second) * gradient * gradient
-            gradient_ref[where, :] = gradient
-            one_out[where, :] = first
-            two_out[where, :] = second
-            first_hat = first / (1.0 - beta_first**adam_steps)
-            second_hat = second / (1.0 - beta_second**adam_steps)
-            update_ref[where, :] = (
-                first_hat / (jnp.sqrt(second_hat) + adam_eps) + weight_decay * param_ref[where, :]
-            )
-            return 0
-
-        lax.fori_loop(0, rows // chunk, step, 0)
-
-    flat = jax.ShapeDtypeStruct((rows, LANE), jnp.float32)
+        factor_out[...] = jnp.broadcast_to(factor, (8, LANE))
+
     tile = (8, LANE)
     return pl.pallas_call(
         kernel,
-        in_specs=[pl.BlockSpec(memory_space=pltpu.VMEM)] * 5,
-        out_specs=[pl.BlockSpec(memory_space=pltpu.VMEM)] * 5,
-        out_shape=[flat] * 4 + [jax.ShapeDtypeStruct((bias_rows, LANE), jnp.float32)],
+        in_specs=[pl.BlockSpec(memory_space=pltpu.VMEM)] * 2,
+        out_specs=[pl.BlockSpec(memory_space=pltpu.VMEM)] * 2,
+        out_shape=[
+            jax.ShapeDtypeStruct(tile, jnp.float32),
+            jax.ShapeDtypeStruct((bias_rows, LANE), jnp.float32),
+        ],
         scratch_shapes=[
             pltpu.VMEM(tile, jnp.float32),
             pltpu.VMEM((count_dp,) + tile, jnp.float32),
@@ -900,10 +880,40 @@
             pltpu.SemaphoreType.DMA((count_seq,)),
         ],
         compiler_params=pltpu.CompilerParams(
-            collective_id=1, has_side_effects=True, vmem_limit_bytes=48 << 20
+            collective_id=1, has_side_effects=True, vmem_limit_bytes=16 << 20
         ),
-        name="finish",
-    )(grad_shard, bias_part, params, moment_one, moment_two)
+        name="scale_of",
+    )(grad_shard, bias_part)
+
+
+def adam(factor, grad_shard, params, moment_one, moment_two):
+    rows = grad_shard.shape[0]
+    block = 504 if rows % 504 == 0 else rows
+
+    def kernel(
+        factor_ref, grad_ref, param_ref, one_ref, two_ref, gradient_ref, one_out, two_out, update_ref
+    ):
+        gradient = grad_ref[...] * factor_ref[0:1, :]
+        first = beta_first * one_ref[...] + (1.0 - beta_first) * gradient
+        second = beta_second * two_ref[...] + (1.0 - beta_second) * gradient * gradient
+        gradient_ref[...] = gradient
+        one_out[...] = first
+        two_out[...] = second
+        first_hat = first / (1.0 - beta_first**adam_steps)
+        second_hat = second / (1.0 - beta_second**adam_steps)
+        update_ref[...] = (
+            first_hat / (jnp.sqrt(second_hat) + adam_eps) + weight_decay * param_ref[...]
+        )
+
+    spec = pl.BlockSpec((block, LANE), lambda at: (at, 0))
+    return pl.pallas_call(
+        kernel,
+        grid=(rows // block,),
+        in_specs=[pl.BlockSpec((8, LANE), lambda at: (0, 0))] + [spec] * 4,
+        out_specs=[spec] * 4,
+        out_shape=[jax.ShapeDtypeStruct((rows, LANE), jnp.float32)] * 4,
+        name="adam",
+    )(factor, grad_shard, params, moment_one, moment_two)
 
 
 def norm_parts(values):
@@ -1169,8 +1179,8 @@
     grad_first = grad_second + matmul_t(grad_query_c, w_cross_q)
     grad_gate_one = jnp.sum(grad_first * branch_one, axis=1)
     grad_branch_one = to_low(grad_first * gate_one)
-    grad_branch_one, y_point, y_inner = lax.optimization_barrier(
-        (grad_branch_one, *collect([grad_branch_two, grad_inner]))
+    grad_branch_one, y_inner, y_point = lax.optimization_barrier(
+        (grad_branch_one, *collect([grad_inner, grad_branch_two]))
     )
     grad_attended = matmul_t(grad_branch_one, w_attn_out).reshape(
         lat_dev, tokens_dev, heads_lin, 32
@@ -1283,10 +1293,12 @@
     else:
         grad_shard = lax.psum_scatter(
             quarter_grad.reshape(count_dp, -1, LANE), "dp", scatter_dimension=0, tiled=True
-        ).reshape(-1, LANE)
-    *flat_outs, bias_grads = finish(
+        )
+        grad_shard = grad_shard.reshape(-1, LANE).astype(jnp.float32)
+    factor, bias_grads = scale_of(grad_shard, bias_part)
+    flat_outs = adam(
+        factor,
         grad_shard,
-        bias_part,
         params_rows,
         moment_one.reshape(-1, LANE),
         moment_two.reshape(-1, LANE),

time: 924 us -> 915 us (level)
  local copies, waits for them, and re-layouts: 159 us -> 149 us
    unnamed x283 -> x277, local copies, waits for them, and re-layouts: 45.3 us -> 36 us
    pallas_call x1 -> x2, Pallas kernels: 20.8 us -> 22.8 us  [the longest x1 11.6 us: scale_of(): pl.pallas_call(kernel, in_specs=[pl.BlockSpec(memory_space=pltpu.VMEM)] *...]
where the time goes in v5:
time: 915 us; the launch traced here: 903 us
  Pallas kernels  456 us (50%)
  local copies, waits for them, and re-layouts  149 us (16%)
  matrix products  122 us (13%)
  other arithmetic  89 us (10%)
  waiting for transfers between devices  41.4 us (5%)
  starting transfers between devices  28.9 us (3%)
  between operations  16.3 us (2%)
    pallas_call x1, Pallas kernels, gather_flat(): pl.pallas_call(kernel, in_specs=[pl.BlockSpec(memory_space=pltpu.VMEM)],...  177 us
    pallas_call x1, Pallas kernels, reduce_shard(): pl.pallas_call(kernel, in_specs=[pl.BlockSpec(memory_space=pltpu.VMEM)],...  126 us
    pallas_call x7, Pallas kernels, read_matrix(): pl.pallas_call(kernel, grid=(rows_of // block,), in_specs=[pl.BlockSpec((...  68 us
    pallas_call x1, Pallas kernels, write_flat(): pl.pallas_call(kernel, in_specs=[pl.BlockSpec(memory_space=pl.ANY)] * len...  43.4 us
    dot_general x7, matrix products, matmul(): return jnp.dot(left_op, right_op, preferred_element_type=jnp.float32)  36 us
    unnamed x277, local copies, waits for them, and re-layouts  36 us
    dot_general x7, matrix products, outer_sum(): lax.dot_general(left_flat, right_flat, (((0,), (0,)), ((), ())), preferre...  34.5 us
    all_to_all x3, waiting for transfers between devices, collect(): lax.all_to_all(blocks, 'seq', split_axis=0, concat_axis=0, tiled=True)  30 us
  transfers between devices with their start and end apart: 13, of which 4 were waited for; matrix products, arithmetic and copies ran while one was open for 29% of the time, Pallas kernels for 9%

profile of v5, /device:TPU:0, one launch (start us, length us, event | category | flops | bytes accessed | tf_op | source)
XLA Modules:
  0.0 902.7 jit_solution(14821163003208737582)
XLA Ops:
  13.7 176.7 %gather_flat.1.in_ref = bf16[4,40320,128]{2,1,0:T(8,128)(2,1)} custom-call(bf16[5040,128]{1,0:T(8,128)(2,1)} %round_rows.1.in_ref), custom_call_target="tpu_custom_call" | custom-call | tf_op jit(solution)/shard_map/gather_flat/pallas_call | solution.py:553
  193.8 5.6 read_matrix.8
  199.4 12.2 %read_matrix.7 = bf16[1152,3456]{1,0:T(8,128)(2,1)} custom-call(bf16[4,40320,128]{2,1,0:T(8,128)(2,1)} %gather_flat.1.in_ref), custom_call_target="tpu_custom_call" | custom-call | bytes 15925248 | tf_op jit(solution)/shard_map/read_matrix/pallas_call | solution.py:143
  211.6 5.8 convolution_bitcast_fusion
  231.6 9.3 %seq_sum.2 = f32[304,128]{1,0:T(8,128)} custom-call(f32[304,128]{1,0:T(8,128)} %select_maximum_fusion.4.in_ref), custom_call_target="tpu_custom_call" | custom-call | tf_op jit(solution)/shard_map/seq_sum/pallas_call | solution.py:665
  263.5 5.6 read_matrix.11
  269.1 5.8 read_matrix.10
  276.5 8.0 read_matrix.9
  319.3 5.0 fusion.95
  328.8 15.3 %read_matrix.13 = bf16[2880,1152]{1,0:T(8,128)(2,1)} custom-call(bf16[4,40320,128]{2,1,0:T(8,128)(2,1)} %gather_flat.1.in_ref), custom_call_target="tpu_custom_call" | custom-call | bytes 13271040 | tf_op jit(solution)/shard_map/read_matrix/pallas_call | solution.py:143
  344.1 15.5 %read_matrix.12 = bf16[1152,5760]{1,0:T(8,128)(2,1)} custom-call(bf16[4,40320,128]{2,1,0:T(8,128)(2,1)} %gather_flat.1.in_ref), custom_call_target="tpu_custom_call" | custom-call | bytes 26542080 | tf_op jit(solution)/shard_map/read_matrix/pallas_call | solution.py:143
  367.3 11.5 %multiply_convert_fusion = (bf16[256,5760]{1,0:T(8,128)(2,1)S(1)}, f32[256,5760]{1,0:T(8,128)}) fusion(f32[5760]{0:T(1024)} %reshape.1276, bf16[1152,5760]{1,0:T(8,128)(2,1)} %read_matrix.12, bf16[1,256,1152]{2,1,0:T(8,128)(2,1)} %fusion.55), kind=kOutput, calls=%fused_computation.27 | convolution fusion | flops 3406233600 | bytes 22731264 | tf_op jit(solution)/shard_map/dot_general | solution.py:943
  388.0 6.1 add_add_fusion
  409.6 5.2 convolution_bitcast_fusion.1
  418.7 5.7 fusion.20
  431.2 16.1 %fusion.8 = (bf16[5760]{0:T(1024)(128)(2,1)S(1)}, bf16[5760]{0:T(1024)(128)(2,1)S(1)}, bf16[5760]{0:T(1024)(128)(2,1)S(1)}, bf16[5760]{0:T(1024)(128)(2,1)S(1)},...) fusion(bf16[1,1,32,5760]{3,2,1,0:T(8,128)(2,1)} %copy-done.42, ...), kind=kLoop, calls=%fused_computation.21 | loop fusion | flops 58930560 | bytes 27383040 | tf_op jit(solution)/shard_map/lrcf,lrcf->f/dot_general | solution.py:1126
  451.6 8.0 collective-permute-start.2
  471.6 7.0 multiply_add_fusion
  482.2 10.9 %multiply_reduce_fusion.2 = (bf16[1152]{0:T(1024)(128)(2,1)}, f32[256]{0:T(256)S(1)}, f32[256]{0:T(256)S(1)}, bf16[1152]{0:T(1024)(128)(2,1)}, f32[256,1152]{1,0:T(8,128)S(1)}) fusion(f32[256,1152]{1,0:T(8,128)} %copy-done.12, f32[256]{0:T(256)} %copy-done.116, f32[256]{0:T(256)S(1)} %copy-done.113, f32[1152]{0:T(1024)} %copy-done.94, ...), kind=kOutput, calls=%fused_computation.123 | convolution fusion | flops 3400037888 | bytes 18592768 | tf_op jit(solution)/shard_map/dot_general | solution.py:947
  505.2 5.9 copy.121
  542.0 24.7 %all-to-all-done = bf16[4,256,1728]{1,2,0:T(8,128)(2,1)} async-done(((bf16[4,256,1728]{1,2,0:T(8,128)(2,1)}), bf16[4,256,1728]{1,2,0:T(8,128)(2,1)}, u32[]{:S(2)}, u32[]{:S(2)}) %all-to-all-start) | async-done | bytes 3538976 | tf_op jit(solution)/shard_map/all_to_all | solution.py:1013
  566.7 6.1 copy.122
  585.2 6.9 seq_sum.3
  622.4 8.1 fusion.45.refs_6_
  632.0 6.2 fusion.14.refs_5_
  671.5 10.2 %reduce-scatter.5.cloned.1.call-done = bf16[1,126,128]{2,1,0:T(8,128)(2,1)} async-done(((bf16[4,126,128]{2,1,0:T(8,128)(2,1)}), bf16[1,126,128]{2,1,0:T(8,128)(2,1)}) %reduce-scatter.5.cloned.1.call-update) | async-done | bytes 32272 | tf_op jit(solution)/shard_map/reduce_scatter | solution.py:1247
  684.7 5.3 all-to-all-done.2
  692.3 6.9 fusion.21.refs_0_
  699.1 43.4 %write_flat.1.in_ref = bf16[40320,128]{1,0:T(8,128)(2,1)} custom-call(f32[1152,896]{1,0:T(8,128)} %fusion.21.refs_0_, f32[1152,384]{1,0:T(8,128)} %fusion.51.refs_1_, f32[1152,384]{1,0:T(8,128)} %fusion.49.refs_2_, f32[1152,640]{1,0:T(8,128)} %convolution_bitcast_fusion.2.refs_3_, f32[1152,384]{1,0:T(8,128)} %fusion.47.refs_4_, ...), custom_call_target="tpu_custom_call" | custom-call | bytes 30965760 | tf_op jit(solution)/shard_map/write_flat/pallas_call | solution.py:319
  746.5 125.7 %reduce_shard.1.grad_ref = f32[5040,128]{1,0:T(8,128)S(1)} custom-call(bf16[40320,128]{1,0:T(8,128)(2,1)S(1)} %copy-done.1), custom_call_target="tpu_custom_call" | custom-call | tf_op jit(solution)/shard_map/reduce_shard/pallas_call | solution.py:792
  872.2 11.6 %scale_of.1 = (f32[8,128]{1,0:T(8,128)S(1)}, f32[32,128]{1,0:T(8,128)S(1)}) custom-call(f32[5040,128]{1,0:T(8,128)S(1)} %reduce_shard.1.grad_ref, f32[32,128]{1,0:T(8,128)S(1)} %pad_bitcast_fusion.1.bias_ref), custom_call_target="tpu_custom_call" | custom-call | tf_op jit(solution)/shard_map/scale_of/pallas_call | solution.py:861
  884.4 11.2 %adam.1 = (f32[5040,128]{1,0:T(8,128)}, f32[5040,128]{1,0:T(8,128)}, f32[5040,128]{1,0:T(8,128)}, f32[5040,128]{1,0:T(8,128)}) custom-call(f32[8,128]{1,0:T(8,128)} %copy-done.8, f32[5040,128]{1,0:T(8,128)} %copy-done.2, f32[5040,128]{1,0:T(8,128)} %bitcast.428, f32[5040,128]{1,0:T(8,128)} %bitcast.457, f32[5040,128]{1,0:T(8,128)} %bitcast.458), custom_call_target="tpu_custom_call" | custom-call | tf_op jit(solution)/shard_map/adam/pallas_call | solution.py:909
  (507 shorter events, 279.0 us)
Async XLA Ops:
  7.2 281.7 %copy-start = (bf16[1,300,1152]{2,1,0:T(8,128)(2,1)S(1)}, bf16[1,300,1152]{2,1,0:T(8,128)(2,1)}, u32[]{:S(2)}) copy-start(bf16[1,300,1152]{2,1,0:T(8,128)(2,1)} %param.8) | copy-start | bytes 2073604
  7.2 254.1 %all-gather.8.cloned.1.call-start = ((), (), s32[]{:S(2)}) async-start(), calls=%async_computation.5 | async-start | bytes 2949120 | tf_op jit(solution)/shard_map/all_gather | solution.py:990
  8.6 183.4 %copy-start.110 = (f32[256]{0:T(256)}, f32[256]{0:T(256)S(1)}, u32[]{:S(2)}) copy-start(f32[256]{0:T(256)S(1)} %div.64) | copy-start | bytes 3076
  10.0 182.0 %copy-start.114 = (f32[256]{0:T(256)}, f32[256]{0:T(256)S(1)}, u32[]{:S(2)}) copy-start(f32[256]{0:T(256)S(1)} %add_rsqrt_fusion.1) | copy-start | bytes 3076
  13.7 178.9 %copy-start.18 = (bf16[1,8,32,1152]{3,2,1,0:T(8,128)(2,1)S(1)}, bf16[1,8,32,1152]{3,2,1,0:T(8,128)(2,1)}, u32[]{:S(2)}) copy-start(bf16[1,8,32,1152]{3,2,1,0:T(8,128)(2,1)} %param.7) | copy-start | bytes 1769476
  192.0 67.1 %copy-start.92 = (f32[1152]{0:T(1024)}, f32[1152]{0:T(1024)S(1)}, u32[]{:S(2)}) copy-start(f32[1152]{0:T(1024)S(1)} %get-tuple-element.84) | copy-start | bytes 13828
  192.0 125.4 %copy-start.94 = (f32[1152]{0:T(1024)}, f32[1152]{0:T(1024)S(1)}, u32[]{:S(2)}) copy-start(f32[1152]{0:T(1024)S(1)} %get-tuple-element.81) | copy-start | bytes 13828
  193.7 125.6 %all-gather.10.cloned.1.call-start = ((), (), s32[]{:S(2)}) async-start(), calls=%async_computation.8 | async-start | bytes 5898240 | tf_op jit(solution)/shard_map/all_gather | solution.py:990
  199.4 57.5 %copy-start.6 = (bf16[1152,1152]{1,0:T(8,128)(2,1)}, bf16[1152,1152]{1,0:T(8,128)(2,1)S(1)}, u32[]{:S(2)}) copy-start(bf16[1152,1152]{1,0:T(8,128)(2,1)S(1)} %read_matrix.8) | copy-start | bytes 7962628
  262.5 142.2 %all-gather.12.cloned.1.call-start = ((), (), s32[]{:S(2)}) async-start(), calls=%async_computation.9 | async-start | bytes 5898240 | tf_op jit(solution)/shard_map/all_gather | solution.py:990
  325.4 156.7 %all-gather.14.cloned.1.call-start = ((), (), s32[]{:S(2)}) async-start(), calls=%async_computation.10 | async-start | bytes 7372800 | tf_op jit(solution)/shard_map/all_gather | solution.py:990
  364.5 23.4 %copy-start.70 = (f32[5760]{0:T(1024)}, f32[5760]{0:T(1024)S(1)}, u32[]{:S(2)}) copy-start(f32[5760]{0:T(1024)S(1)} %mul.447) | copy-start | bytes 69124
  364.6 23.3 %copy-start.72 = (f32[5760]{0:T(1024)}, f32[5760]{0:T(1024)S(1)}, u32[]{:S(2)}) copy-start(f32[5760]{0:T(1024)S(1)} %mul.478) | copy-start | bytes 69124
  364.6 23.2 %copy-start.74 = (f32[5760]{0:T(1024)}, f32[5760]{0:T(1024)S(1)}, u32[]{:S(2)}) copy-start(f32[5760]{0:T(1024)S(1)} %mul.475) | copy-start | bytes 69124
  364.7 23.2 %copy-start.76 = (f32[5760]{0:T(1024)}, f32[5760]{0:T(1024)S(1)}, u32[]{:S(2)}) copy-start(f32[5760]{0:T(1024)S(1)} %mul.472) | copy-start | bytes 69124
  364.8 23.1 %copy-start.78 = (f32[5760]{0:T(1024)}, f32[5760]{0:T(1024)S(1)}, u32[]{:S(2)}) copy-start(f32[5760]{0:T(1024)S(1)} %mul.469) | copy-start | bytes 69124
  364.9 23.0 %copy-start.80 = (f32[5760]{0:T(1024)}, f32[5760]{0:T(1024)S(1)}, u32[]{:S(2)}) copy-start(f32[5760]{0:T(1024)S(1)} %mul.466) | copy-start | bytes 69124
  365.0 22.9 %copy-start.82 = (f32[5760]{0:T(1024)}, f32[5760]{0:T(1024)S(1)}, u32[]{:S(2)}) copy-start(f32[5760]{0:T(1024)S(1)} %mul.463) | copy-start | bytes 69124
  365.9 22.1 %copy-start.84 = (f32[5760]{0:T(1024)}, f32[5760]{0:T(1024)S(1)}, u32[]{:S(2)}) copy-start(f32[5760]{0:T(1024)S(1)} %mul.460) | copy-start | bytes 69124
  367.3 16.8 %copy-start.34 = (bf16[1,8,32,1152]{3,2,1,0:T(8,128)(2,1)S(1)}, bf16[1,8,32,1152]{3,2,1,0:T(8,128)(2,1)}, u32[]{:S(2)}) copy-start(bf16[1,8,32,1152]{3,2,1,0:T(8,128)(2,1)} %param.10) | copy-start | bytes 1769476
  367.3 16.8 %copy-start.96 = (f32[1152]{0:T(1024)S(1)}, f32[1152]{0:T(1024)}, u32[]{:S(2)}) copy-start(f32[1152]{0:T(1024)} %get-tuple-element.79) | copy-start | bytes 13828
  378.9 6.2 collective-permute-start
  382.6 3.6 collective-permute-start.1
  451.6 14.9 %collective-permute-start.2 = (bf16[1,1,32,5760]{3,2,1,0:T(8,128)(2,1)}, bf16[1,1,32,5760]{3,2,1,0:T(8,128)(2,1)}, u32[]{:S(2)}, u32[]{:S(2)}) collective-permute-start(bf16[1,1,32,5760]{3,2,1,0:T(8,128)(2,1)} %get-tuple-element.117), channel_id=1, source_target_pairs={{0,1},{1,2},{2,3},{4,5},{5,6},{6,7},{8,9},{9,10},{10,11},{12,13},{... | collective-permute-start | bytes 1105928 | tf_op jit(solution)/shard_map/ppermute | solution.py:30
  459.6 7.0 collective-permute-start.3
  498.7 17.6 %copy-start.29 = (bf16[256,1152]{0,1:T(8,128)(2,1)}, bf16[256,1152]{0,1:T(8,128)(2,1)S(1)}, u32[]{:S(2)}) copy-start(bf16[256,1152]{0,1:T(8,128)(2,1)S(1)} %copy.120) | copy-start | bytes 1769476
  511.1 55.6 %all-to-all-start = ((bf16[4,256,1728]{1,2,0:T(8,128)(2,1)}), bf16[4,256,1728]{1,2,0:T(8,128)(2,1)}, u32[]{:S(2)}, u32[]{:S(2)}) async-start(bf16[4,256,1728]{1,2,0:T(8,128)(2,1)} %copy.121), calls=%async_computation | async-start | bytes 7077888 | tf_op jit(solution)/shard_map/all_to_all | solution.py:1013
  516.0 122.2 %reduce-scatter.3.cloned.1.call-start = ((), (), s32[]{:S(2)}) async-start(), calls=%async_computation.6 | async-start | bytes 2211840 | tf_op jit(solution)/shard_map/reduce_scatter | solution.py:1174
  608.1 33.8 %all-to-all-start.1 = ((bf16[4,256,864]{1,2,0:T(8,128)(2,1)}), bf16[4,256,864]{1,2,0:T(8,128)(2,1)}, u32[]{:S(2)}, u32[]{:S(2)}) async-start(bf16[4,256,864]{1,2,0:T(8,128)(2,1)} %copy.133), calls=%async_computation.1 | async-start | bytes 3538944 | tf_op jit(solution)/shard_map/all_to_all | solution.py:1013
  612.6 69.1 %reduce-scatter.5.cloned.1.call-start = ((), (), s32[]{:S(2)}) async-start(), calls=%async_computation.7 | async-start | bytes 163840 | tf_op jit(solution)/shard_map/reduce_scatter | solution.py:1247
  663.4 26.6 %all-to-all-start.2 = ((bf16[4,256,864]{1,2,0:T(8,128)(2,1)}), bf16[4,256,864]{1,2,0:T(8,128)(2,1)S(1)}, u32[]{:S(2)}, u32[]{:S(2)}) async-start(bf16[4,256,864]{1,2,0:T(8,128)(2,1)} %copy.135), calls=%async_computation.2 | async-start | bytes 3538944 | tf_op jit(solution)/shard_map/all_to_all | solution.py:1013
  667.2 16.9 %copy-start.121 = (pred[1,14,128]{2,1,0:T(8,128)(4,1)S(1)}, pred[1,14,128]{2,1,0:T(8,128)(4,1)}, u32[]{:S(2)}) copy-start(pred[1,14,128]{2,1,0:T(8,128)(4,1)} %constant.40.clone.1) | copy-start | bytes 5380
  (111 other events, 550.5 us)
Sparse Core Ops, SparseCore 0:
  193.8 24.2 all-gather.7
  262.6 39.0 all-gather.9
  325.6 39.0 all-gather.11
  418.7 50.2 all-gather.13
  526.4 40.5 reduce-scatter.2
  660.2 21.5 reduce-scatter.4

commit v6 on v5

--- a/solution.py
+++ b/solution.py
@@ -75,7 +75,7 @@
 
 
 def matrix_rows(count_rows):
-    return 192 if count_rows % 192 == 0 else 64
+    return 384 if count_rows % 384 == 0 else 576 if count_rows % 576 == 0 else 64
 
 
 def read_matrix(flat, offset, rows_of, cols_of, segs):
@@ -165,7 +165,7 @@
 
 def write_flat(segs, parts):
     specs = piece_specs()
-    block_rows = 192
+    block_rows = 576
     total = sum(rows_of * cols_of // segs for rows_of, cols_of, _ in specs)
     flat_rows = total // LANE
     places = []
@@ -287,7 +287,7 @@
                         flat[where, :] = merge_units(parts, lane_unit)
                     return 0
 
-                lax.fori_loop(0, block // 32, group, 0, unroll=3)
+                lax.fori_loop(0, block // 32, group, 0, unroll=6)
                 return 0
 
             lax.fori_loop(0, blocks, one_block, 0)

time: 915 us -> 892 us (0.975)
  Pallas kernels: 456 us -> 434 us
    pallas_call x1, Pallas kernels: 43.4 us -> 27.8 us  [write_flat(): pl.pallas_call(kernel, in_specs=[pl.BlockSpec(memory_space=pl.ANY)] * len...]
  transfers between devices with their start and end apart: 13 -> 13, of which waited for: 4 -> 4; matrix products, arithmetic and copies ran while one was open for 29% -> 30% of each run, Pallas kernels for 9% -> 9%
where the time goes in v6:
time: 892 us; the launch traced here: 881 us
  Pallas kernels  434 us (49%)
  local copies, waits for them, and re-layouts  149 us (17%)
  matrix products  122 us (14%)
  other arithmetic  89.1 us (10%)
  waiting for transfers between devices  41.4 us (5%)
  starting transfers between devices  29 us (3%)
  between operations  16.3 us (2%)
    pallas_call x1, Pallas kernels, gather_flat(): pl.pallas_call(kernel, in_specs=[pl.BlockSpec(memory_space=pltpu.VMEM)],...  177 us
    pallas_call x1, Pallas kernels, reduce_shard(): pl.pallas_call(kernel, in_specs=[pl.BlockSpec(memory_space=pltpu.VMEM)],...  125 us
    pallas_call x7, Pallas kernels, read_matrix(): pl.pallas_call(kernel, grid=(rows_of // block,), in_specs=[pl.BlockSpec((...  62 us
    dot_general x7, matrix products, matmul(): return jnp.dot(left_op, right_op, preferred_element_type=jnp.float32)  36.1 us
    unnamed x277, local copies, waits for them, and re-layouts  36 us
    dot_general x7, matrix products, outer_sum(): lax.dot_general(left_flat, right_flat, (((0,), (0,)), ((), ())), preferre...  34.5 us
    all_to_all x3, waiting for transfers between devices, collect(): lax.all_to_all(blocks, 'seq', split_axis=0, concat_axis=0, tiled=True)  30.3 us
    pallas_call x1, Pallas kernels, write_flat(): pl.pallas_call(kernel, in_specs=[pl.BlockSpec(memory_space=pl.ANY)] * len...  27.8 us
  transfers between devices with their start and end apart: 13, of which 4 were waited for; matrix products, arithmetic and copies ran while one was open for 30% of the time, Pallas kernels for 9%

profile of v6, /device:TPU:0, one launch (start us, length us, event | category | flops | bytes accessed | tf_op | source)
XLA Modules:
  0.0 881.0 jit_solution(12865873471341482931)
XLA Ops:
  13.7 176.7 %gather_flat.1.in_ref = bf16[4,40320,128]{2,1,0:T(8,128)(2,1)} custom-call(bf16[5040,128]{1,0:T(8,128)(2,1)} %round_rows.1.in_ref), custom_call_target="tpu_custom_call" | custom-call | tf_op jit(solution)/shard_map/gather_flat/pallas_call | solution.py:553
  198.7 12.0 %read_matrix.7 = bf16[1152,3456]{1,0:T(8,128)(2,1)} custom-call(bf16[4,40320,128]{2,1,0:T(8,128)(2,1)} %gather_flat.1.in_ref), custom_call_target="tpu_custom_call" | custom-call | bytes 15925248 | tf_op jit(solution)/shard_map/read_matrix/pallas_call | solution.py:143
  210.7 5.9 convolution_bitcast_fusion
  230.6 9.3 %seq_sum.2 = f32[304,128]{1,0:T(8,128)} custom-call(f32[304,128]{1,0:T(8,128)} %select_maximum_fusion.4.in_ref), custom_call_target="tpu_custom_call" | custom-call | tf_op jit(solution)/shard_map/seq_sum/pallas_call | solution.py:665
  267.4 4.9 read_matrix.10
  273.8 8.0 read_matrix.9
  316.6 5.0 fusion.95
  326.1 11.7 %read_matrix.13 = bf16[2880,1152]{1,0:T(8,128)(2,1)} custom-call(bf16[4,40320,128]{2,1,0:T(8,128)(2,1)} %gather_flat.1.in_ref), custom_call_target="tpu_custom_call" | custom-call | bytes 13271040 | tf_op jit(solution)/shard_map/read_matrix/pallas_call | solution.py:143
  337.9 15.7 %read_matrix.12 = bf16[1152,5760]{1,0:T(8,128)(2,1)} custom-call(bf16[4,40320,128]{2,1,0:T(8,128)(2,1)} %gather_flat.1.in_ref), custom_call_target="tpu_custom_call" | custom-call | bytes 26542080 | tf_op jit(solution)/shard_map/read_matrix/pallas_call | solution.py:143
  361.3 11.5 %multiply_convert_fusion = (bf16[256,5760]{1,0:T(8,128)(2,1)S(1)}, f32[256,5760]{1,0:T(8,128)}) fusion(f32[5760]{0:T(1024)} %reshape.1276, bf16[1152,5760]{1,0:T(8,128)(2,1)} %read_matrix.12, bf16[1,256,1152]{2,1,0:T(8,128)(2,1)} %fusion.55), kind=kOutput, calls=%fused_computation.27 | convolution fusion | flops 3406233600 | bytes 22731264 | tf_op jit(solution)/shard_map/dot_general | solution.py:943
  382.1 6.1 add_add_fusion
  398.7 5.0 fusion.94
  403.7 5.2 convolution_bitcast_fusion.1
  412.7 5.7 fusion.20
  425.3 16.1 %fusion.8 = (bf16[5760]{0:T(1024)(128)(2,1)S(1)}, bf16[5760]{0:T(1024)(128)(2,1)S(1)}, bf16[5760]{0:T(1024)(128)(2,1)S(1)}, bf16[5760]{0:T(1024)(128)(2,1)S(1)},...) fusion(bf16[1,1,32,5760]{3,2,1,0:T(8,128)(2,1)} %copy-done.42, ...), kind=kLoop, calls=%fused_computation.21 | loop fusion | flops 58930560 | bytes 27383040 | tf_op jit(solution)/shard_map/lrcf,lrcf->f/dot_general | solution.py:1126
  445.6 8.1 collective-permute-start.2
  460.8 4.9 select_maximum_fusion
  465.8 7.0 multiply_add_fusion
  476.4 10.9 %multiply_reduce_fusion.2 = (bf16[1152]{0:T(1024)(128)(2,1)}, f32[256]{0:T(256)S(1)}, f32[256]{0:T(256)S(1)}, bf16[1152]{0:T(1024)(128)(2,1)}, f32[256,1152]{1,0:T(8,128)S(1)}) fusion(f32[256,1152]{1,0:T(8,128)} %copy-done.12, f32[256]{0:T(256)} %copy-done.116, f32[256]{0:T(256)S(1)} %copy-done.113, f32[1152]{0:T(1024)} %copy-done.94, ...), kind=kOutput, calls=%fused_computation.123 | convolution fusion | flops 3400037888 | bytes 18592768 | tf_op jit(solution)/shard_map/dot_general | solution.py:947
  499.4 5.9 copy.121
  536.2 24.7 %all-to-all-done = bf16[4,256,1728]{1,2,0:T(8,128)(2,1)} async-done(((bf16[4,256,1728]{1,2,0:T(8,128)(2,1)}), bf16[4,256,1728]{1,2,0:T(8,128)(2,1)}, u32[]{:S(2)}, u32[]{:S(2)}) %all-to-all-start) | async-done | bytes 3538976 | tf_op jit(solution)/shard_map/all_to_all | solution.py:1013
  560.9 6.1 copy.122
  579.4 6.9 seq_sum.3
  616.6 8.1 fusion.45.refs_6_
  626.2 6.2 fusion.14.refs_5_
  665.8 9.9 %reduce-scatter.5.cloned.1.call-done = bf16[1,126,128]{2,1,0:T(8,128)(2,1)} async-done(((bf16[4,126,128]{2,1,0:T(8,128)(2,1)}), bf16[1,126,128]{2,1,0:T(8,128)(2,1)}) %reduce-scatter.5.cloned.1.call-update) | async-done | bytes 32272 | tf_op jit(solution)/shard_map/reduce_scatter | solution.py:1247
  678.6 5.6 all-to-all-done.2
  686.5 6.9 fusion.21.refs_0_
  693.4 27.8 %write_flat.1.in_ref = bf16[40320,128]{1,0:T(8,128)(2,1)} custom-call(f32[1152,896]{1,0:T(8,128)} %fusion.21.refs_0_, f32[1152,384]{1,0:T(8,128)} %fusion.51.refs_1_, f32[1152,384]{1,0:T(8,128)} %fusion.49.refs_2_, f32[1152,640]{1,0:T(8,128)} %convolution_bitcast_fusion.2.refs_3_, f32[1152,384]{1,0:T(8,128)} %fusion.47.refs_4_, ...), custom_call_target="tpu_custom_call" | custom-call | bytes 30965760 | tf_op jit(solution)/shard_map/write_flat/pallas_call | solution.py:319
  725.1 125.3 %reduce_shard.1.grad_ref = f32[5040,128]{1,0:T(8,128)S(1)} custom-call(bf16[40320,128]{1,0:T(8,128)(2,1)S(1)} %copy-done.1), custom_call_target="tpu_custom_call" | custom-call | tf_op jit(solution)/shard_map/reduce_shard/pallas_call | solution.py:792
  850.4 11.6 %scale_of.1 = (f32[8,128]{1,0:T(8,128)S(1)}, f32[32,128]{1,0:T(8,128)S(1)}) custom-call(f32[5040,128]{1,0:T(8,128)S(1)} %reduce_shard.1.grad_ref, f32[32,128]{1,0:T(8,128)S(1)} %pad_bitcast_fusion.1.bias_ref), custom_call_target="tpu_custom_call" | custom-call | tf_op jit(solution)/shard_map/scale_of/pallas_call | solution.py:861
  862.6 11.2 %adam.1 = (f32[5040,128]{1,0:T(8,128)}, f32[5040,128]{1,0:T(8,128)}, f32[5040,128]{1,0:T(8,128)}, f32[5040,128]{1,0:T(8,128)}) custom-call(f32[8,128]{1,0:T(8,128)} %copy-done.8, f32[5040,128]{1,0:T(8,128)} %copy-done.2, f32[5040,128]{1,0:T(8,128)} %bitcast.428, f32[5040,128]{1,0:T(8,128)} %bitcast.457, f32[5040,128]{1,0:T(8,128)} %bitcast.458), custom_call_target="tpu_custom_call" | custom-call | tf_op jit(solution)/shard_map/adam/pallas_call | solution.py:909
  (507 shorter events, 279.1 us)
Async XLA Ops:
  7.2 279.1 %copy-start = (bf16[1,300,1152]{2,1,0:T(8,128)(2,1)S(1)}, bf16[1,300,1152]{2,1,0:T(8,128)(2,1)}, u32[]{:S(2)}) copy-start(bf16[1,300,1152]{2,1,0:T(8,128)(2,1)} %param.8) | copy-start | bytes 2073604
  7.2 253.0 %all-gather.8.cloned.1.call-start = ((), (), s32[]{:S(2)}) async-start(), calls=%async_computation.5 | async-start | bytes 2949120 | tf_op jit(solution)/shard_map/all_gather | solution.py:990
  8.6 183.4 %copy-start.110 = (f32[256]{0:T(256)}, f32[256]{0:T(256)S(1)}, u32[]{:S(2)}) copy-start(f32[256]{0:T(256)S(1)} %div.64) | copy-start | bytes 3076
  10.0 182.0 %copy-start.114 = (f32[256]{0:T(256)}, f32[256]{0:T(256)S(1)}, u32[]{:S(2)}) copy-start(f32[256]{0:T(256)S(1)} %add_rsqrt_fusion.1) | copy-start | bytes 3076
  13.7 178.9 %copy-start.18 = (bf16[1,8,32,1152]{3,2,1,0:T(8,128)(2,1)S(1)}, bf16[1,8,32,1152]{3,2,1,0:T(8,128)(2,1)}, u32[]{:S(2)}) copy-start(bf16[1,8,32,1152]{3,2,1,0:T(8,128)(2,1)} %param.7) | copy-start | bytes 1769476
  192.0 66.1 %copy-start.92 = (f32[1152]{0:T(1024)}, f32[1152]{0:T(1024)S(1)}, u32[]{:S(2)}) copy-start(f32[1152]{0:T(1024)S(1)} %get-tuple-element.84) | copy-start | bytes 13828
  192.0 122.7 %copy-start.94 = (f32[1152]{0:T(1024)}, f32[1152]{0:T(1024)S(1)}, u32[]{:S(2)}) copy-start(f32[1152]{0:T(1024)S(1)} %get-tuple-element.81) | copy-start | bytes 13828
  193.7 122.9 %all-gather.10.cloned.1.call-start = ((), (), s32[]{:S(2)}) async-start(), calls=%async_computation.8 | async-start | bytes 5898240 | tf_op jit(solution)/shard_map/all_gather | solution.py:990
  198.7 57.2 %copy-start.6 = (bf16[1152,1152]{1,0:T(8,128)(2,1)}, bf16[1152,1152]{1,0:T(8,128)(2,1)S(1)}, u32[]{:S(2)}) copy-start(bf16[1152,1152]{1,0:T(8,128)(2,1)S(1)} %read_matrix.8) | copy-start | bytes 7962628
  261.4 137.3 %all-gather.12.cloned.1.call-start = ((), (), s32[]{:S(2)}) async-start(), calls=%async_computation.9 | async-start | bytes 5898240 | tf_op jit(solution)/shard_map/all_gather | solution.py:990
  322.8 153.6 %all-gather.14.cloned.1.call-start = ((), (), s32[]{:S(2)}) async-start(), calls=%async_computation.10 | async-start | bytes 7372800 | tf_op jit(solution)/shard_map/all_gather | solution.py:990
  358.5 23.5 %copy-start.70 = (f32[5760]{0:T(1024)}, f32[5760]{0:T(1024)S(1)}, u32[]{:S(2)}) copy-start(f32[5760]{0:T(1024)S(1)} %mul.447) | copy-start | bytes 69124
  358.5 23.4 %copy-start.72 = (f32[5760]{0:T(1024)}, f32[5760]{0:T(1024)S(1)}, u32[]{:S(2)}) copy-start(f32[5760]{0:T(1024)S(1)} %mul.478) | copy-start | bytes 69124
  358.6 23.3 %copy-start.74 = (f32[5760]{0:T(1024)}, f32[5760]{0:T(1024)S(1)}, u32[]{:S(2)}) copy-start(f32[5760]{0:T(1024)S(1)} %mul.475) | copy-start | bytes 69124
  358.7 23.2 %copy-start.76 = (f32[5760]{0:T(1024)}, f32[5760]{0:T(1024)S(1)}, u32[]{:S(2)}) copy-start(f32[5760]{0:T(1024)S(1)} %mul.472) | copy-start | bytes 69124
  358.8 23.1 %copy-start.78 = (f32[5760]{0:T(1024)}, f32[5760]{0:T(1024)S(1)}, u32[]{:S(2)}) copy-start(f32[5760]{0:T(1024)S(1)} %mul.469) | copy-start | bytes 69124
  358.9 23.1 %copy-start.80 = (f32[5760]{0:T(1024)}, f32[5760]{0:T(1024)S(1)}, u32[]{:S(2)}) copy-start(f32[5760]{0:T(1024)S(1)} %mul.466) | copy-start | bytes 69124
  359.0 23.0 %copy-start.82 = (f32[5760]{0:T(1024)}, f32[5760]{0:T(1024)S(1)}, u32[]{:S(2)}) copy-start(f32[5760]{0:T(1024)S(1)} %mul.463) | copy-start | bytes 69124
  359.9 22.1 %copy-start.84 = (f32[5760]{0:T(1024)}, f32[5760]{0:T(1024)S(1)}, u32[]{:S(2)}) copy-start(f32[5760]{0:T(1024)S(1)} %mul.460) | copy-start | bytes 69124
  361.3 16.9 %copy-start.34 = (bf16[1,8,32,1152]{3,2,1,0:T(8,128)(2,1)S(1)}, bf16[1,8,32,1152]{3,2,1,0:T(8,128)(2,1)}, u32[]{:S(2)}) copy-start(bf16[1,8,32,1152]{3,2,1,0:T(8,128)(2,1)} %param.10) | copy-start | bytes 1769476
  361.3 16.9 %copy-start.96 = (f32[1152]{0:T(1024)S(1)}, f32[1152]{0:T(1024)}, u32[]{:S(2)}) copy-start(f32[1152]{0:T(1024)} %get-tuple-element.79) | copy-start | bytes 13828
  372.9 6.3 collective-permute-start
  376.7 3.6 collective-permute-start.1
  445.6 15.0 %collective-permute-start.2 = (bf16[1,1,32,5760]{3,2,1,0:T(8,128)(2,1)}, bf16[1,1,32,5760]{3,2,1,0:T(8,128)(2,1)}, u32[]{:S(2)}, u32[]{:S(2)}) collective-permute-start(bf16[1,1,32,5760]{3,2,1,0:T(8,128)(2,1)} %get-tuple-element.117), channel_id=1, source_target_pairs={{0,1},{1,2},{2,3},{4,5},{5,6},{6,7},{8,9},{9,10},{10,11},{12,13},{... | collective-permute-start | bytes 1105928 | tf_op jit(solution)/shard_map/ppermute | solution.py:30
  453.7 7.0 collective-permute-start.3
  492.9 17.6 %copy-start.29 = (bf16[256,1152]{0,1:T(8,128)(2,1)}, bf16[256,1152]{0,1:T(8,128)(2,1)S(1)}, u32[]{:S(2)}) copy-start(bf16[256,1152]{0,1:T(8,128)(2,1)S(1)} %copy.120) | copy-start | bytes 1769476
  505.3 55.6 %all-to-all-start = ((bf16[4,256,1728]{1,2,0:T(8,128)(2,1)}), bf16[4,256,1728]{1,2,0:T(8,128)(2,1)}, u32[]{:S(2)}, u32[]{:S(2)}) async-start(bf16[4,256,1728]{1,2,0:T(8,128)(2,1)} %copy.121), calls=%async_computation | async-start | bytes 7077888 | tf_op jit(solution)/shard_map/all_to_all | solution.py:1013
  510.2 122.2 %reduce-scatter.3.cloned.1.call-start = ((), (), s32[]{:S(2)}) async-start(), calls=%async_computation.6 | async-start | bytes 2211840 | tf_op jit(solution)/shard_map/reduce_scatter | solution.py:1174
  602.3 33.8 %all-to-all-start.1 = ((bf16[4,256,864]{1,2,0:T(8,128)(2,1)}), bf16[4,256,864]{1,2,0:T(8,128)(2,1)}, u32[]{:S(2)}, u32[]{:S(2)}) async-start(bf16[4,256,864]{1,2,0:T(8,128)(2,1)} %copy.133), calls=%async_computation.1 | async-start | bytes 3538944 | tf_op jit(solution)/shard_map/all_to_all | solution.py:1013
  606.9 68.8 %reduce-scatter.5.cloned.1.call-start = ((), (), s32[]{:S(2)}) async-start(), calls=%async_computation.7 | async-start | bytes 163840 | tf_op jit(solution)/shard_map/reduce_scatter | solution.py:1247
  657.6 26.6 %all-to-all-start.2 = ((bf16[4,256,864]{1,2,0:T(8,128)(2,1)}), bf16[4,256,864]{1,2,0:T(8,128)(2,1)S(1)}, u32[]{:S(2)}, u32[]{:S(2)}) async-start(bf16[4,256,864]{1,2,0:T(8,128)(2,1)} %copy.135), calls=%async_computation.2 | async-start | bytes 3538944 | tf_op jit(solution)/shard_map/all_to_all | solution.py:1013
  661.4 16.6 %copy-start.121 = (pred[1,14,128]{2,1,0:T(8,128)(4,1)S(1)}, pred[1,14,128]{2,1,0:T(8,128)(4,1)}, u32[]{:S(2)}) copy-start(pred[1,14,128]{2,1,0:T(8,128)(4,1)} %constant.40.clone.1) | copy-start | bytes 5380
  (111 other events, 551.5 us)
Sparse Core Ops, SparseCore 0:
  193.8 24.2 all-gather.7
  261.6 39.0 all-gather.9
  322.9 39.1 all-gather.11
  412.8 49.9 all-gather.13
  520.6 40.5 reduce-scatter.2
  654.4 21.2 reduce-scatter.4

commit v7 on v6

--- a/solution.py
+++ b/solution.py
@@ -694,9 +694,9 @@
 
 def reduce_shard(flat):
     rows = flat.shape[0] // 8
-    pieces = 3
+    pieces = 5
     part = rows // pieces
-    step = 80
+    step = 112
 
     def kernel(in_ref, out_ref, recv_x, send_z, recv_z, x_send, x_recv, z_send, z_recv):
         me = lax.axis_index("dp")
@@ -888,7 +888,7 @@
 
 def adam(factor, grad_shard, params, moment_one, moment_two):
     rows = grad_shard.shape[0]
-    block = 504 if rows % 504 == 0 else rows
+    block = 1680 if rows % 1680 == 0 else rows
 
     def kernel(
         factor_ref, grad_ref, param_ref, one_ref, two_ref, gradient_ref, one_out, two_out, update_ref
@@ -1288,7 +1288,7 @@
             grad_b_point,
         ],
     )
-    if count_dp == 8 and quarter_grad.shape[0] % (8 * 240) == 0:
+    if count_dp == 8 and quarter_grad.shape[0] % (8 * 560) == 0:
         grad_shard = reduce_shard(quarter_grad)
     else:
         grad_shard = lax.psum_scatter(

time: 892 us -> 886 us (level)
  no operation moved by 1% of the time
where the time goes in v7:
time: 886 us; the launch traced here: 875 us
  Pallas kernels  428 us (48%)
  local copies, waits for them, and re-layouts  149 us (17%)
  matrix products  122 us (14%)
  other arithmetic  89.1 us (10%)
  waiting for transfers between devices  41.4 us (5%)
  starting transfers between devices  29 us (3%)
  between operations  16.3 us (2%)
    pallas_call x1, Pallas kernels, gather_flat(): pl.pallas_call(kernel, in_specs=[pl.BlockSpec(memory_space=pltpu.VMEM)],...  177 us
    pallas_call x1, Pallas kernels, reduce_shard(): pl.pallas_call(kernel, in_specs=[pl.BlockSpec(memory_space=pltpu.VMEM)],...  122 us
    pallas_call x7, Pallas kernels, read_matrix(): pl.pallas_call(kernel, grid=(rows_of // block,), in_specs=[pl.BlockSpec((...  62 us
    dot_general x7, matrix products, matmul(): return jnp.dot(left_op, right_op, preferred_element_type=jnp.float32)  36.1 us
    unnamed x277, local copies, waits for them, and re-layouts  36 us
    dot_general x7, matrix products, outer_sum(): lax.dot_general(left_flat, right_flat, (((0,), (0,)), ((), ())), preferre...  34.5 us
    all_to_all x3, waiting for transfers between devices, collect(): lax.all_to_all(blocks, 'seq', split_axis=0, concat_axis=0, tiled=True)  30.3 us
    pallas_call x1, Pallas kernels, write_flat(): pl.pallas_call(kernel, in_specs=[pl.BlockSpec(memory_space=pl.ANY)] * len...  27.8 us
  transfers between devices with their start and end apart: 13, of which 4 were waited for; matrix products, arithmetic and copies ran while one was open for 30% of the time, Pallas kernels for 9%

profile of v7, /device:TPU:0, one launch (start us, length us, event | category | flops | bytes accessed | tf_op | source)
XLA Modules:
  0.0 874.9 jit_solution(17453161184758464194)
XLA Ops:
  13.7 176.7 %gather_flat.1.in_ref = bf16[4,40320,128]{2,1,0:T(8,128)(2,1)} custom-call(bf16[5040,128]{1,0:T(8,128)(2,1)} %round_rows.1.in_ref), custom_call_target="tpu_custom_call" | custom-call | tf_op jit(solution)/shard_map/gather_flat/pallas_call | solution.py:553
  198.7 12.0 %read_matrix.7 = bf16[1152,3456]{1,0:T(8,128)(2,1)} custom-call(bf16[4,40320,128]{2,1,0:T(8,128)(2,1)} %gather_flat.1.in_ref), custom_call_target="tpu_custom_call" | custom-call | bytes 15925248 | tf_op jit(solution)/shard_map/read_matrix/pallas_call | solution.py:143
  210.7 5.9 convolution_bitcast_fusion
  230.6 9.3 %seq_sum.2 = f32[304,128]{1,0:T(8,128)} custom-call(f32[304,128]{1,0:T(8,128)} %select_maximum_fusion.4.in_ref), custom_call_target="tpu_custom_call" | custom-call | tf_op jit(solution)/shard_map/seq_sum/pallas_call | solution.py:665
  267.4 4.9 read_matrix.10
  273.8 8.0 read_matrix.9
  316.6 5.0 fusion.95
  326.1 11.7 %read_matrix.13 = bf16[2880,1152]{1,0:T(8,128)(2,1)} custom-call(bf16[4,40320,128]{2,1,0:T(8,128)(2,1)} %gather_flat.1.in_ref), custom_call_target="tpu_custom_call" | custom-call | bytes 13271040 | tf_op jit(solution)/shard_map/read_matrix/pallas_call | solution.py:143
  337.9 15.7 %read_matrix.12 = bf16[1152,5760]{1,0:T(8,128)(2,1)} custom-call(bf16[4,40320,128]{2,1,0:T(8,128)(2,1)} %gather_flat.1.in_ref), custom_call_target="tpu_custom_call" | custom-call | bytes 26542080 | tf_op jit(solution)/shard_map/read_matrix/pallas_call | solution.py:143
  361.3 11.5 %multiply_convert_fusion = (bf16[256,5760]{1,0:T(8,128)(2,1)S(1)}, f32[256,5760]{1,0:T(8,128)}) fusion(f32[5760]{0:T(1024)} %reshape.1276, bf16[1152,5760]{1,0:T(8,128)(2,1)} %read_matrix.12, bf16[1,256,1152]{2,1,0:T(8,128)(2,1)} %fusion.55), kind=kOutput, calls=%fused_computation.27 | convolution fusion | flops 3406233600 | bytes 22731264 | tf_op jit(solution)/shard_map/dot_general | solution.py:943
  382.1 6.1 add_add_fusion
  398.7 5.0 fusion.94
  403.7 5.2 convolution_bitcast_fusion.1
  412.7 5.7 fusion.20
  425.3 16.1 %fusion.8 = (bf16[5760]{0:T(1024)(128)(2,1)S(1)}, bf16[5760]{0:T(1024)(128)(2,1)S(1)}, bf16[5760]{0:T(1024)(128)(2,1)S(1)}, bf16[5760]{0:T(1024)(128)(2,1)S(1)},...) fusion(bf16[1,1,32,5760]{3,2,1,0:T(8,128)(2,1)} %copy-done.42, ...), kind=kLoop, calls=%fused_computation.21 | loop fusion | flops 58930560 | bytes 27383040 | tf_op jit(solution)/shard_map/lrcf,lrcf->f/dot_general | solution.py:1126
  445.6 8.1 collective-permute-start.2
  460.8 4.9 select_maximum_fusion
  465.8 7.0 multiply_add_fusion
  476.4 10.9 %multiply_reduce_fusion.2 = (bf16[1152]{0:T(1024)(128)(2,1)}, f32[256]{0:T(256)S(1)}, f32[256]{0:T(256)S(1)}, bf16[1152]{0:T(1024)(128)(2,1)}, f32[256,1152]{1,0:T(8,128)S(1)}) fusion(f32[256,1152]{1,0:T(8,128)} %copy-done.12, f32[256]{0:T(256)} %copy-done.116, f32[256]{0:T(256)S(1)} %copy-done.113, f32[1152]{0:T(1024)} %copy-done.94, ...), kind=kOutput, calls=%fused_computation.123 | convolution fusion | flops 3400037888 | bytes 18592768 | tf_op jit(solution)/shard_map/dot_general | solution.py:947
  499.4 5.9 copy.121
  536.2 24.7 %all-to-all-done = bf16[4,256,1728]{1,2,0:T(8,128)(2,1)} async-done(((bf16[4,256,1728]{1,2,0:T(8,128)(2,1)}), bf16[4,256,1728]{1,2,0:T(8,128)(2,1)}, u32[]{:S(2)}, u32[]{:S(2)}) %all-to-all-start) | async-done | bytes 3538976 | tf_op jit(solution)/shard_map/all_to_all | solution.py:1013
  560.9 6.1 copy.122
  579.4 6.9 seq_sum.3
  616.6 8.1 fusion.45.refs_6_
  626.2 6.2 fusion.14.refs_5_
  665.8 9.9 %reduce-scatter.5.cloned.1.call-done = bf16[1,126,128]{2,1,0:T(8,128)(2,1)} async-done(((bf16[4,126,128]{2,1,0:T(8,128)(2,1)}), bf16[1,126,128]{2,1,0:T(8,128)(2,1)}) %reduce-scatter.5.cloned.1.call-update) | async-done | bytes 32272 | tf_op jit(solution)/shard_map/reduce_scatter | solution.py:1247
  678.6 5.6 all-to-all-done.2
  686.5 6.9 fusion.21.refs_0_
  693.4 27.8 %write_flat.1.in_ref = bf16[40320,128]{1,0:T(8,128)(2,1)} custom-call(f32[1152,896]{1,0:T(8,128)} %fusion.21.refs_0_, f32[1152,384]{1,0:T(8,128)} %fusion.51.refs_1_, f32[1152,384]{1,0:T(8,128)} %fusion.49.refs_2_, f32[1152,640]{1,0:T(8,128)} %convolution_bitcast_fusion.2.refs_3_, f32[1152,384]{1,0:T(8,128)} %fusion.47.refs_4_, ...), custom_call_target="tpu_custom_call" | custom-call | bytes 30965760 | tf_op jit(solution)/shard_map/write_flat/pallas_call | solution.py:319
  725.1 121.7 %reduce_shard.1.grad_ref = f32[5040,128]{1,0:T(8,128)S(1)} custom-call(bf16[40320,128]{1,0:T(8,128)(2,1)S(1)} %copy-done.1), custom_call_target="tpu_custom_call" | custom-call | tf_op jit(solution)/shard_map/reduce_shard/pallas_call | solution.py:792
  846.8 11.7 %scale_of.1 = (f32[8,128]{1,0:T(8,128)S(1)}, f32[32,128]{1,0:T(8,128)S(1)}) custom-call(f32[5040,128]{1,0:T(8,128)S(1)} %reduce_shard.1.grad_ref, f32[32,128]{1,0:T(8,128)S(1)} %pad_bitcast_fusion.1.bias_ref), custom_call_target="tpu_custom_call" | custom-call | tf_op jit(solution)/shard_map/scale_of/pallas_call | solution.py:861
  859.1 8.7 adam.1
  (507 shorter events, 279.1 us)
Async XLA Ops:
  7.2 279.1 %copy-start = (bf16[1,300,1152]{2,1,0:T(8,128)(2,1)S(1)}, bf16[1,300,1152]{2,1,0:T(8,128)(2,1)}, u32[]{:S(2)}) copy-start(bf16[1,300,1152]{2,1,0:T(8,128)(2,1)} %param.8) | copy-start | bytes 2073604
  7.2 253.0 %all-gather.8.cloned.1.call-start = ((), (), s32[]{:S(2)}) async-start(), calls=%async_computation.5 | async-start | bytes 2949120 | tf_op jit(solution)/shard_map/all_gather | solution.py:990
  8.6 183.4 %copy-start.110 = (f32[256]{0:T(256)}, f32[256]{0:T(256)S(1)}, u32[]{:S(2)}) copy-start(f32[256]{0:T(256)S(1)} %div.64) | copy-start | bytes 3076
  10.0 182.0 %copy-start.114 = (f32[256]{0:T(256)}, f32[256]{0:T(256)S(1)}, u32[]{:S(2)}) copy-start(f32[256]{0:T(256)S(1)} %add_rsqrt_fusion.1) | copy-start | bytes 3076
  13.7 178.9 %copy-start.18 = (bf16[1,8,32,1152]{3,2,1,0:T(8,128)(2,1)S(1)}, bf16[1,8,32,1152]{3,2,1,0:T(8,128)(2,1)}, u32[]{:S(2)}) copy-start(bf16[1,8,32,1152]{3,2,1,0:T(8,128)(2,1)} %param.7) | copy-start | bytes 1769476
  192.0 66.1 %copy-start.92 = (f32[1152]{0:T(1024)}, f32[1152]{0:T(1024)S(1)}, u32[]{:S(2)}) copy-start(f32[1152]{0:T(1024)S(1)} %get-tuple-element.84) | copy-start | bytes 13828
  192.0 122.7 %copy-start.94 = (f32[1152]{0:T(1024)}, f32[1152]{0:T(1024)S(1)}, u32[]{:S(2)}) copy-start(f32[1152]{0:T(1024)S(1)} %get-tuple-element.81) | copy-start | bytes 13828
  193.7 122.9 %all-gather.10.cloned.1.call-start = ((), (), s32[]{:S(2)}) async-start(), calls=%async_computation.8 | async-start | bytes 5898240 | tf_op jit(solution)/shard_map/all_gather | solution.py:990
  198.7 57.2 %copy-start.6 = (bf16[1152,1152]{1,0:T(8,128)(2,1)}, bf16[1152,1152]{1,0:T(8,128)(2,1)S(1)}, u32[]{:S(2)}) copy-start(bf16[1152,1152]{1,0:T(8,128)(2,1)S(1)} %read_matrix.8) | copy-start | bytes 7962628
  261.4 137.3 %all-gather.12.cloned.1.call-start = ((), (), s32[]{:S(2)}) async-start(), calls=%async_computation.9 | async-start | bytes 5898240 | tf_op jit(solution)/shard_map/all_gather | solution.py:990
  322.8 153.6 %all-gather.14.cloned.1.call-start = ((), (), s32[]{:S(2)}) async-start(), calls=%async_computation.10 | async-start | bytes 7372800 | tf_op jit(solution)/shard_map/all_gather | solution.py:990
  358.5 23.5 %copy-start.70 = (f32[5760]{0:T(1024)}, f32[5760]{0:T(1024)S(1)}, u32[]{:S(2)}) copy-start(f32[5760]{0:T(1024)S(1)} %mul.447) | copy-start | bytes 69124
  358.5 23.4 %copy-start.72 = (f32[5760]{0:T(1024)}, f32[5760]{0:T(1024)S(1)}, u32[]{:S(2)}) copy-start(f32[5760]{0:T(1024)S(1)} %mul.478) | copy-start | bytes 69124
  358.6 23.3 %copy-start.74 = (f32[5760]{0:T(1024)}, f32[5760]{0:T(1024)S(1)}, u32[]{:S(2)}) copy-start(f32[5760]{0:T(1024)S(1)} %mul.475) | copy-start | bytes 69124
  358.7 23.2 %copy-start.76 = (f32[5760]{0:T(1024)}, f32[5760]{0:T(1024)S(1)}, u32[]{:S(2)}) copy-start(f32[5760]{0:T(1024)S(1)} %mul.472) | copy-start | bytes 69124
  358.8 23.1 %copy-start.78 = (f32[5760]{0:T(1024)}, f32[5760]{0:T(1024)S(1)}, u32[]{:S(2)}) copy-start(f32[5760]{0:T(1024)S(1)} %mul.469) | copy-start | bytes 69124
  358.9 23.1 %copy-start.80 = (f32[5760]{0:T(1024)}, f32[5760]{0:T(1024)S(1)}, u32[]{:S(2)}) copy-start(f32[5760]{0:T(1024)S(1)} %mul.466) | copy-start | bytes 69124
  359.0 23.0 %copy-start.82 = (f32[5760]{0:T(1024)}, f32[5760]{0:T(1024)S(1)}, u32[]{:S(2)}) copy-start(f32[5760]{0:T(1024)S(1)} %mul.463) | copy-start | bytes 69124
  359.9 22.1 %copy-start.84 = (f32[5760]{0:T(1024)}, f32[5760]{0:T(1024)S(1)}, u32[]{:S(2)}) copy-start(f32[5760]{0:T(1024)S(1)} %mul.460) | copy-start | bytes 69124
  361.3 16.9 %copy-start.34 = (bf16[1,8,32,1152]{3,2,1,0:T(8,128)(2,1)S(1)}, bf16[1,8,32,1152]{3,2,1,0:T(8,128)(2,1)}, u32[]{:S(2)}) copy-start(bf16[1,8,32,1152]{3,2,1,0:T(8,128)(2,1)} %param.10) | copy-start | bytes 1769476
  361.3 16.9 %copy-start.96 = (f32[1152]{0:T(1024)S(1)}, f32[1152]{0:T(1024)}, u32[]{:S(2)}) copy-start(f32[1152]{0:T(1024)} %get-tuple-element.79) | copy-start | bytes 13828
  372.9 6.3 collective-permute-start
  376.7 3.6 collective-permute-start.1
  445.6 15.0 %collective-permute-start.2 = (bf16[1,1,32,5760]{3,2,1,0:T(8,128)(2,1)}, bf16[1,1,32,5760]{3,2,1,0:T(8,128)(2,1)}, u32[]{:S(2)}, u32[]{:S(2)}) collective-permute-start(bf16[1,1,32,5760]{3,2,1,0:T(8,128)(2,1)} %get-tuple-element.117), channel_id=1, source_target_pairs={{0,1},{1,2},{2,3},{4,5},{5,6},{6,7},{8,9},{9,10},{10,11},{12,13},{... | collective-permute-start | bytes 1105928 | tf_op jit(solution)/shard_map/ppermute | solution.py:30
  453.7 7.0 collective-permute-start.3
  492.9 17.6 %copy-start.29 = (bf16[256,1152]{0,1:T(8,128)(2,1)}, bf16[256,1152]{0,1:T(8,128)(2,1)S(1)}, u32[]{:S(2)}) copy-start(bf16[256,1152]{0,1:T(8,128)(2,1)S(1)} %copy.120) | copy-start | bytes 1769476
  505.3 55.6 %all-to-all-start = ((bf16[4,256,1728]{1,2,0:T(8,128)(2,1)}), bf16[4,256,1728]{1,2,0:T(8,128)(2,1)}, u32[]{:S(2)}, u32[]{:S(2)}) async-start(bf16[4,256,1728]{1,2,0:T(8,128)(2,1)} %copy.121), calls=%async_computation | async-start | bytes 7077888 | tf_op jit(solution)/shard_map/all_to_all | solution.py:1013
  510.2 122.2 %reduce-scatter.3.cloned.1.call-start = ((), (), s32[]{:S(2)}) async-start(), calls=%async_computation.6 | async-start | bytes 2211840 | tf_op jit(solution)/shard_map/reduce_scatter | solution.py:1174
  602.3 33.8 %all-to-all-start.1 = ((bf16[4,256,864]{1,2,0:T(8,128)(2,1)}), bf16[4,256,864]{1,2,0:T(8,128)(2,1)}, u32[]{:S(2)}, u32[]{:S(2)}) async-start(bf16[4,256,864]{1,2,0:T(8,128)(2,1)} %copy.133), calls=%async_computation.1 | async-start | bytes 3538944 | tf_op jit(solution)/shard_map/all_to_all | solution.py:1013
  606.9 68.8 %reduce-scatter.5.cloned.1.call-start = ((), (), s32[]{:S(2)}) async-start(), calls=%async_computation.7 | async-start | bytes 163840 | tf_op jit(solution)/shard_map/reduce_scatter | solution.py:1247
  657.6 26.6 %all-to-all-start.2 = ((bf16[4,256,864]{1,2,0:T(8,128)(2,1)}), bf16[4,256,864]{1,2,0:T(8,128)(2,1)S(1)}, u32[]{:S(2)}, u32[]{:S(2)}) async-start(bf16[4,256,864]{1,2,0:T(8,128)(2,1)} %copy.135), calls=%async_computation.2 | async-start | bytes 3538944 | tf_op jit(solution)/shard_map/all_to_all | solution.py:1013
  661.4 16.6 %copy-start.121 = (pred[1,14,128]{2,1,0:T(8,128)(4,1)S(1)}, pred[1,14,128]{2,1,0:T(8,128)(4,1)}, u32[]{:S(2)}) copy-start(pred[1,14,128]{2,1,0:T(8,128)(4,1)} %constant.40.clone.1) | copy-start | bytes 5380
  (111 other events, 551.6 us)
Sparse Core Ops, SparseCore 0:
  193.8 24.2 all-gather.7
  261.6 39.0 all-gather.9
  322.9 39.1 all-gather.11
  412.8 49.9 all-gather.13
  520.6 40.5 reduce-scatter.2
  654.4 21.2 reduce-scatter.4
